TPU v7x, 256 devices: a whole 4x4x8 slice. The times are simulated.
256 devices in a mesh: rows: 32 (over x_lo, z, core), cols: 8 (over y, x_hi).
Axes of the slice: x: 4 (x_hi: 2, x_lo: 2; x = x_hi * 2 + x_lo), y: 4, z: 8, core: 2. Of those that a mesh axis runs over, the one named last changes fastest.
Arguments:
- current_frame: bfloat16 [128, 512, 1024], P(None, 'rows', 'cols'), may hold values from -6 to 6
- history_frames: bfloat16 [3, 128, 512, 1024], P(None, None, 'rows', 'cols'), may hold values from -6 to 6
- offsets: int32 [3, 2], replicated, may hold values from -16 to 16, as said below
- compress_weight: bfloat16 [32, 128], replicated, may hold values from -0.5 to 0.5
- mixer_weight: bfloat16 [3, 3, 128, 224], replicated, may hold values from -0.125 to 0.125
- mixer_bias: float32 [128], replicated, may hold values from -3 to 3
Outputs:
- joined_grid: bfloat16 [128, 512, 1024], P(None, 'rows', 'cols')
Inputs may be any that keep to these rules, and one draw needn't show every extreme that they name: offsets[k, 0] lies in -8..8 and offsets[k, 1] in -16..16; no offset is 0; in each of the two columns one frame's offset equals the bound and another equals its negative.
All inputs are finite; a program needn't handle non-finite values.
Results may differ from a plain program's by a relative error of at most 0.0034.
Values may be sent and summed in bfloat16 or wider, within the bound.
No kernel may reach another device: no remote copies, remote signals or barrier semaphores. Data moves between devices by JAX's collectives and lax.ppermute only.
A program may use at most 64 MiB of HBM per device.

v0:
```python
import jax
import jax.numpy as jnp
from jax import lax
from jax.sharding import PartitionSpec as P

CP = 32
SHIFT_X = 16


def with_halo(shard, sides, width):
    for axis, dim in sides:
        size, length = (lax.axis_size(axis), shard.shape[dim])
        up = [(i, (i + 1) % size) for i in range(size - 1)]
        down = [(j, i) for i, j in up]
        last = lax.slice_in_dim(shard, length - width, length, axis=dim)
        first = lax.slice_in_dim(shard, 0, width, axis=dim)
        before = lax.ppermute(last, axis, up)
        after = lax.ppermute(first, axis, down)
        shard = jnp.concatenate([before, shard, after], axis=dim)
    return shard


def conv_taps(present_rows, older_rows, mixer_weight, mixer_bias):
    height = present_rows.shape[1] - 2
    width = present_rows.shape[2] - 2
    channels = present_rows.shape[0]
    total = jnp.zeros((mixer_weight.shape[2], height * width), jnp.float32)
    for tap_row in range(3):
        for tap_col in range(3):
            present = present_rows[
                :, tap_row : tap_row + height, tap_col : tap_col + width
            ].reshape(channels, -1)
            older = older_rows[:, tap_row : tap_row + height, tap_col : tap_col + width].reshape(
                older_rows.shape[0], -1
            )
            total = total + jnp.dot(
                mixer_weight[tap_row, tap_col, :, :channels],
                present,
                preferred_element_type=jnp.float32,
            )
            total = total + jnp.dot(
                mixer_weight[tap_row, tap_col, :, channels:],
                older,
                preferred_element_type=jnp.float32,
            )
    result = jnp.maximum(total + mixer_bias[:, None], 0.0)
    return result.astype(jnp.bfloat16).reshape(-1, height, width)


def pack_block(values, depth, extent, breadth):
    flat_values = values.reshape(-1)
    padding = depth * extent * breadth - flat_values.shape[0]
    flat_values = jnp.concatenate([flat_values, jnp.zeros((padding,), flat_values.dtype)])
    return flat_values.reshape(depth, extent, breadth)


def body(current_frame, history_frames, offsets, compress_weight, mixer_weight, mixer_bias):
    frames, channels, local_rows, local_cols = history_frames.shape
    reach_rows = local_rows // 2 + 1
    reach_cols = SHIFT_X + 1
    row_half = min(reach_rows, local_rows // 2)
    row_depth = -(-channels // row_half)
    reduced = jnp.einsum(
        "oc,fcrx->forx", compress_weight, history_frames, preferred_element_type=jnp.float32
    ).astype(jnp.bfloat16)
    source = reduced.reshape(frames * CP, local_rows, local_cols)
    channel_depth = CP
    first_piece = pack_block(current_frame[:, 0, :], row_depth, row_half, local_cols)
    last_piece = pack_block(current_frame[:, local_rows - 1, :], row_depth, row_half, local_cols)
    middle = jnp.zeros((row_depth, local_rows - 2 * row_half, local_cols), jnp.bfloat16)
    edge_slab = jnp.concatenate([first_piece, middle, last_piece], axis=1)
    source = jnp.concatenate([source, edge_slab], axis=0)
    source = with_halo(source, (("rows", 1),), reach_rows)
    carried = source[source.shape[0] - row_depth :]
    source = source[: source.shape[0] - row_depth]
    above_row = carried[:, reach_rows - row_half : reach_rows, :].reshape(-1, local_cols)
    below_row = carried[:, reach_rows + local_rows : reach_rows + local_rows + row_half, :].reshape(
        -1, local_cols
    )
    present_middle = jnp.concatenate(
        [above_row[:, None, :], current_frame, below_row[:, None, :]], axis=1
    )
    row_span = source.shape[1]
    col_half = min(reach_cols, local_cols // 2)
    edge_count = channels * (local_rows + 2)
    col_depth = -(-edge_count // (row_span * col_half))
    first_piece = pack_block(present_middle[:, :, 0], col_depth, row_span, col_half)
    last_piece = pack_block(present_middle[:, :, local_cols - 1], col_depth, row_span, col_half)
    middle = jnp.zeros((col_depth, row_span, local_cols - 2 * col_half), jnp.bfloat16)
    edge_slab = jnp.concatenate([first_piece, middle, last_piece], axis=2)
    source = jnp.concatenate([source, edge_slab], axis=0)
    source = with_halo(source, (("cols", 2),), reach_cols)
    carried = source[source.shape[0] - col_depth :]
    source = source[: source.shape[0] - col_depth]
    left_col = (
        carried[:, :, reach_cols - col_half : reach_cols]
        .reshape(-1)[:edge_count]
        .reshape(channels, local_rows + 2)
    )
    right_col = (
        carried[:, :, reach_cols + local_cols : reach_cols + local_cols + col_half]
        .reshape(-1)[:edge_count]
        .reshape(channels, local_rows + 2)
    )
    present_rows = jnp.concatenate(
        [left_col[:, :, None], present_middle, right_col[:, :, None]], axis=2
    )
    pieces = []
    for frame_index in range(frames):
        start_row = reach_rows - 1 - offsets[frame_index, 0]
        start_col = reach_cols - 1 - offsets[frame_index, 1]
        window = lax.dynamic_slice(
            source,
            (jnp.int32(frame_index * channel_depth), start_row, start_col),
            (channel_depth, local_rows + 2, local_cols + 2),
        )
        pieces.append(window)
    shifted = jnp.concatenate(pieces, axis=0)
    row_places = (
        lax.axis_index("rows") * local_rows - 1 + jnp.arange(local_rows + 2, dtype=jnp.int32)
    )
    col_places = (
        lax.axis_index("cols") * local_cols - 1 + jnp.arange(local_cols + 2, dtype=jnp.int32)
    )
    row_inside = (row_places >= 0) & (row_places < local_rows * lax.axis_size("rows"))
    col_inside = (col_places >= 0) & (col_places < local_cols * lax.axis_size("cols"))
    inside = row_inside[:, None] & col_inside[None, :]
    shifted = jnp.where(inside[None, :, :], shifted, jnp.zeros_like(shifted))
    return conv_taps(present_rows, shifted, mixer_weight, mixer_bias)


def solution(mesh):
    in_specs = (P(None, "rows", "cols"), P(None, None, "rows", "cols"), P(), P(), P(), P())
    out_specs = P(None, "rows", "cols")
    return jax.shard_map(body, mesh=mesh, in_specs=in_specs, out_specs=out_specs, check_vma=False)
```

profile of v0, /device:TPU:14, one launch (start us, length us, event | category | flops | bytes accessed | tf_op | source)
XLA Modules:
  0.0 81.0 jit_solution(16023673802687517256)
XLA Ops:
  0.0 1.3 %fusion.87 = (bf16[128,1,128]{2,1,0:T(2,128)(2,1)S(1)}, bf16[128,1,128]{2,1,0:T(2,128)(2,1)S(1)}) fusion(bf16[128,16,128]{2,1,0:T(8,128)(2,1)} %param.6), kind=kLoop, calls=%fused_computation.129 | loop fusion | bytes 131072 | tf_op jit(solution)/shard_map/slice | solution.py:68
  1.3 0.3 copy-done
  1.6 1.1 %fusion.18 = bf16[3,32,16,128]{3,1,2,0:T(8,128)(2,1)S(1)} fusion(bf16[3,128,16,128]{3,2,1,0:T(8,128)(2,1)S(1)} %copy-done, bf16[32,128]{1,0:T(8,128)(2,1)} %param.9), kind=kOutput, calls=%fused_computation.38 | convolution fusion | flops 50528256 | bytes 1974272 | tf_op jit(solution)/shard_map/oc,fcrx->forx/dot_general | solution.py:63
  2.9 1.1 %fusion.88 = (bf16[112,9,128]{2,1,0:T(8,128)(2,1)}, bf16[112,9,128]{2,1,0:T(8,128)(2,1)}) fusion(bf16[112,16,128]{2,1,0:T(8,128)(2,1)S(1)} %maximum_maximum_fusion.2), kind=kLoop, calls=%fused_computation.130 | loop fusion | bytes 1032192 | tf_op jit(solution)/shard_map/slice | solution.py:15
  4.0 1.9 %collective-permute-start = (bf16[112,9,128]{2,1,0:T(8,128)(2,1)}, bf16[112,9,128]{2,1,0:T(8,128)(2,1)S(1)}, u32[]{:S(2)}, u32[]{:S(2)}) collective-permute-start(bf16[112,9,128]{2,1,0:T(8,128)(2,1)} %get-tuple-element.33), channel_id=1, source_target_pairs={{0,8},{8,16},{16,24},{24,32},{32,40},{40,48},{48,56},{56,64},{64,7... | collective-permute-start | bytes 774152 | tf_op jit(solution)/shard_map/ppermute | solution.py:17
  6.0 7.5 %collective-permute-start.1 = (bf16[112,9,128]{2,1,0:T(8,128)(2,1)}, bf16[112,9,128]{2,1,0:T(8,128)(2,1)}, u32[]{:S(2)}, u32[]{:S(2)}) collective-permute-start(bf16[112,9,128]{2,1,0:T(8,128)(2,1)} %get-tuple-element.34), channel_id=1, source_target_pairs={{8,0},{16,8},{24,16},{32,24},{40,32},{48,40},{56,48},{64,56},{72,6... | collective-permute-start | bytes 774152 | tf_op jit(solution)/shard_map/ppermute | solution.py:18
  13.5 0.7 broadcast_and_fusion
  14.1 0.7 fusion.89
  14.8 0.5 copy.27
  23.0 0.7 copy.37
  23.7 1.4 %slice_bitcast_fusion = bf16[128,1,128]{2,0,1:T(8,128)(2,1)} fusion(bf16[112,9,128]{2,1,0:T(8,128)(2,1)} %collective-permute-done.1), kind=kLoop, calls=%fused_computation.74 | loop fusion | bytes 65536 | tf_op jit(solution)/shard_map/broadcast_in_dim;reshape | solution.py:81
  25.1 0.9 %copy.28 = bf16[128,1,128]{0,2,1:T(8,128)(2,1)S(1)} copy(bf16[128,1,128]{2,0,1:T(8,128)(2,1)} %slice_bitcast_fusion) | data formatting | bytes 65536 | tf_op jit(solution)/shard_map/broadcast_in_dim;reshape | solution.py:81
  26.0 1.4 %copy.41 = bf16[128,1,128]{2,1,0:T(2,128)(2,1)} copy(bf16[128,1,128]{2,0,1:T(8,128)(2,1)} %slice_bitcast_fusion) | data formatting | bytes 65536 | tf_op jit(solution)/shard_map/broadcast_in_dim;reshape | solution.py:81
  27.4 0.6 pad_maximum_fusion.14
  28.0 0.7 copy.29
  28.8 0.9 %reshape_squeeze.6 = bf16[2304]{0:T(1024)(128)(2,1)S(1)} reshape(bf16[128,18,1]{1,0,2:T(8,128)(2,1)} %copy.29) | data formatting | bytes 9216 | tf_op jit(solution)/shard_map/reshape;squeeze | solution.py:51
  29.9 0.8 %copy.30 = bf16[128,18,1]{1,0,2:T(8,128)(2,1)S(1)} copy(bf16[128,18,1]{0,2,1:T(2,128)(2,1)} %get-tuple-element.28) | data formatting | bytes 9216 | tf_op jit(solution)/shard_map/slice | solution.py:88
  30.9 0.6 concatenate.52
  31.5 0.9 %reshape.140 = bf16[4,34,17]{2,1,0:T(8,128)(2,1)S(1)} reshape(bf16[2312]{0:T(1024)(128)(2,1)} %concatenate.52) | data formatting | bytes 9248 | tf_op jit(solution)/shard_map/reshape | solution.py:54
  32.4 1.5 %pad_maximum_fusion.5 = bf16[96,34,128]{2,1,0:T(8,128)(2,1)S(1)} fusion(bf16[112,9,128]{2,1,0:T(8,128)(2,1)} %collective-permute-done.1, bf16[112,9,128]{2,1,0:T(8,128)(2,1)} %copy-done.16, bf16[96,16,128]{2,1,0:T(8,128)(2,1)S(1)} %bitcast.195, bf16[16,8,128]{2,1,0:T(8,128)(2,1)} %copy-done.22, bf16[16,8,128]{2,1,0:T(8,128)(2,1)} %copy-done.23), kind=kLoop, calls=%fused_computation.41 | loop fusion | flops 4177920 | bytes 1810432 | tf_op jit(solution)/shard_map/concatenate | solution.py:19
  34.1 1.7 %fusion.84 = (bf16[100,34,17]{2,1,0:T(8,128)(2,1)}, bf16[100,34,17]{2,1,0:T(8,128)(2,1)}) fusion(bf16[100,34,128]{2,1,0:T(8,128)(2,1)S(1)} %maximum_maximum_fusion), kind=kLoop, calls=%fused_computation.126 | loop fusion | bytes 462400 | tf_op jit(solution)/shard_map/slice | solution.py:16
  35.8 2.5 %copy.31 = bf16[100,34,17]{0,1,2:T(8,128)(2,1)} copy(bf16[100,34,17]{2,1,0:T(8,128)(2,1)} %get-tuple-element.18) | data formatting | bytes 231200 | tf_op jit(solution)/shard_map/slice | solution.py:15
  38.3 4.0 %collective-permute-start.2 = (bf16[100,34,17]{0,1,2:T(8,128)(2,1)}, bf16[100,34,17]{0,1,2:T(8,128)(2,1)S(1)}, u32[]{:S(2)}, u32[]{:S(2)}) collective-permute-start(bf16[100,34,17]{0,1,2:T(8,128)(2,1)} %copy.31), channel_id=1, source_target_pairs={{0,1},{1,2},{2,3},{3,4},{4,5},{5,6},{6,7},{8,9},{9,10},{10,11},{11... | collective-permute-start | bytes 346808 | tf_op jit(solution)/shard_map/ppermute | solution.py:17
  42.3 2.5 %copy.34 = bf16[100,34,17]{0,1,2:T(8,128)(2,1)} copy(bf16[100,34,17]{2,1,0:T(8,128)(2,1)} %get-tuple-element.17) | data formatting | bytes 231200 | tf_op jit(solution)/shard_map/slice | solution.py:16
  44.8 3.3 %collective-permute-start.3 = (bf16[100,34,17]{0,1,2:T(8,128)(2,1)}, bf16[100,34,17]{0,1,2:T(8,128)(2,1)S(1)}, u32[]{:S(2)}, u32[]{:S(2)}) collective-permute-start(bf16[100,34,17]{0,1,2:T(8,128)(2,1)} %copy.34), channel_id=1, source_target_pairs={{1,0},{2,1},{3,2},{4,3},{5,4},{6,5},{7,6},{9,8},{10,9},{11,10},{12... | collective-permute-start | bytes 346808 | tf_op jit(solution)/shard_map/ppermute | solution.py:18
  48.1 2.4 %pad_maximum_fusion.10 = (bf16[128,16,128]{2,1,0:T(8,128)(2,1)}, bf16[128,16,128]{2,1,0:T(8,128)(2,1)}) fusion(bf16[128,1,128]{2,1,0:T(2,128)(2,1)} %copy.41, bf16[128,16,128]{2,1,0:T(8,128)(2,1)S(1)} %copy-done.1, bf16[128,1,128]{2,1,0:T(2,128)(2,1)} %copy.37), kind=kLoop, calls=%fused_computation.53 | loop fusion | flops 2097152 | bytes 1638400 | tf_op jit(solution)/shard_map/concatenate | solution.py:80
  50.5 1.6 %copy.35 = bf16[100,34,17]{2,1,0:T(8,128)(2,1)} copy(bf16[100,34,17]{0,1,2:T(8,128)(2,1)S(1)} %collective-permute-done.2) | data formatting | bytes 231200 | tf_op jit(solution)/shard_map/ppermute | solution.py:17
  52.1 2.6 %collective-permute-done.3 = bf16[100,34,17]{0,1,2:T(8,128)(2,1)S(1)} collective-permute-done((bf16[100,34,17]{0,1,2:T(8,128)(2,1)}, bf16[100,34,17]{0,1,2:T(8,128)(2,1)S(1)}, u32[]{:S(2)}, u32[]{:S(2)}) %collective-permute-start.3) | collective-permute-done | bytes 115632 | tf_op jit(solution)/shard_map/ppermute | solution.py:18
  54.7 1.6 %copy.36 = bf16[100,34,17]{2,1,0:T(8,128)(2,1)} copy(bf16[100,34,17]{0,1,2:T(8,128)(2,1)S(1)} %collective-permute-done.3) | data formatting | bytes 231200 | tf_op jit(solution)/shard_map/ppermute | solution.py:18
  56.3 3.6 %pad_maximum_fusion = bf16[96,34,162]{2,1,0:T(8,128)(2,1)S(1)} fusion(bf16[100,34,17]{2,1,0:T(8,128)(2,1)} %copy.36, bf16[100,34,17]{2,1,0:T(8,128)(2,1)} %copy.35, bf16[96,34,128]{2,1,0:T(8,128)(2,1)S(1)} %pad_maximum_fusion.5, bf16[4,34,17]{2,1,0:T(8,128)(2,1)S(1)} %reshape.140, bf16[4,34,94]{2,1,0:T(8,128)(2,1)S(1)} %broadcast_in_dim.18, ...), kind=kLoop, calls=%fused_computation.30 | loop fusion | flops 6345216 | bytes 2159136 | tf_op jit(solution)/shard_map/concatenate | solution.py:19
  60.0 0.8 %constant_dynamic-slice_fusion.2 = (bf16[32,18,130]{2,1,0:T(8,128)(2,1)S(1)}, bf16[32,18,130]{2,1,0:T(8,128)(2,1)S(1)}, bf16[32,18,130]{2,1,0:T(8,128)(2,1)S(1)}) fusion(bf16[96,34,162]{2,1,0:T(8,128)(2,1)S(1)} %pad_maximum_fusion, s32[]{:T(128)S(6)} %select_n.22, s32[]{:T(128)S(6)} %select_n.23, s32[]{:T(128)S(6)} %select_n.24, s32[]{:T(128)S(6)} %select_n.25, ...), kind=kLoop, calls=%fused_computation.124 | loop fusion | bytes 898584 | tf_op jit(solution)/shard_map/dynamic_slice | solution.py:112
  60.8 0.3 maximum_select_fusion
  61.2 2.4 %fusion.83 = (bf16[96,16,128]{2,1,0:T(8,128)(2,1)}, bf16[96,16,128]{2,1,0:T(8,128)(2,1)S(1)}, bf16[96,16,128]{2,1,0:T(8,128)(2,1)S(1)}, bf16[96,16,128]{2,1,0:T(...) fusion(bf16[96,18,130]{2,1,0:T(8,128)(2,1)S(1)} %maximum_select, ...), kind=kLoop, calls=%fused_computation.125 | loop fusion | bytes 7077888 | tf_op jit(solution)/shard_map/slice | solution.py:33
  63.6 0.8 slice.251
  64.4 1.3 %copy.32 = bf16[4,34,17]{2,1,0:T(8,128)(2,1)S(1)} copy(bf16[4,34,17]{0,1,2:T(8,128)(2,1)} %slice.251) | data formatting | bytes 9248 | tf_op jit(solution)/shard_map/slice | solution.py:96
  66.1 1.7 %slice.257 = bf16[4,34,17]{0,1,2:T(8,128)(2,1)} slice(bf16[100,34,17]{0,1,2:T(8,128)(2,1)} %copy-done.13), slice={[96:100], [0:34], [0:17]} | slice | bytes 9248 | tf_op jit(solution)/shard_map/slice | solution.py:101
  67.8 1.3 %copy.38 = bf16[4,34,17]{2,1,0:T(8,128)(2,1)S(1)} copy(bf16[4,34,17]{0,1,2:T(8,128)(2,1)} %slice.257) | data formatting | bytes 9248 | tf_op jit(solution)/shard_map/slice | solution.py:101
  69.6 0.3 pad_maximum_fusion.9
  69.9 0.4 fusion.86
  70.3 0.3 fusion.85
  70.6 0.7 copy-done.17
  71.7 0.3 convolution_add_fusion.7
  72.0 0.4 copy-done.5
  72.4 0.3 convolution_add_fusion.6
  72.8 0.3 convolution_add_fusion.5
  73.4 0.4 copy-done.9
  73.8 0.3 convolution_add_fusion.3
  74.1 0.3 convolution_add_fusion.2
  74.4 0.4 copy-done.8
  74.8 0.3 fusion.11
  75.1 0.4 convolution_add_fusion
  75.5 0.3 copy-done.7
  75.8 0.3 fusion.10
  76.1 0.3 fusion.9
  76.4 0.4 copy-done.6
  76.8 0.3 fusion.8
  77.4 0.3 fusion.6
  77.7 0.4 copy-done.4
  78.1 0.3 fusion.5
  78.5 0.3 fusion.4
  78.8 0.3 fusion.3
  79.1 0.3 copy-done.12
  79.5 0.3 fusion.12
  79.8 1.2 %copy.42 = bf16[128,16,128]{2,1,0:T(8,128)(2,1)} copy(bf16[128,16,128]{0,2,1:T(8,128)(2,1)S(1)} %bitcast.196) | data formatting | bytes 1048576 | tf_op jit(solution)/shard_map/reshape | solution.py:47
  (69 shorter events, 2.7 us)
Async XLA Ops:
  0.0 1.6 %copy-start = (bf16[3,128,16,128]{3,2,1,0:T(8,128)(2,1)S(1)}, bf16[3,128,16,128]{3,2,1,0:T(8,128)(2,1)}, u32[]{:S(2)}) copy-start(bf16[3,128,16,128]{3,2,1,0:T(8,128)(2,1)} %param.7) | copy-start | bytes 4718596
  2.6 11.5 %copy-start.25 = (s32[3,2]{0,1:T(2,128)S(1)}, s32[3,2]{0,1:T(2,128)}, u32[]{:S(2)}) copy-start(s32[3,2]{0,1:T(2,128)} %param.8) | copy-start | bytes 76
  2.6 12.2 %copy-start.1 = (bf16[128,16,128]{2,1,0:T(8,128)(2,1)S(1)}, bf16[128,16,128]{2,1,0:T(8,128)(2,1)}, u32[]{:S(2)}) copy-start(bf16[128,16,128]{2,1,0:T(8,128)(2,1)} %param.6) | copy-start | bytes 1572868
  2.8 1.2 %copy-start.22 = (bf16[16,8,128]{2,1,0:T(8,128)(2,1)}, bf16[16,8,128]{2,1,0:T(8,128)(2,1)S(1)}, u32[]{:S(2)}) copy-start(bf16[16,8,128]{2,1,0:T(8,128)(2,1)S(1)} %get-tuple-element.41) | copy-start | bytes 98308
  2.8 1.2 %copy-start.23 = (bf16[16,8,128]{2,1,0:T(8,128)(2,1)}, bf16[16,8,128]{2,1,0:T(8,128)(2,1)S(1)}, u32[]{:S(2)}) copy-start(bf16[16,8,128]{2,1,0:T(8,128)(2,1)S(1)} %get-tuple-element.42) | copy-start | bytes 98308
  4.0 18.8 %collective-permute-start = (bf16[112,9,128]{2,1,0:T(8,128)(2,1)}, bf16[112,9,128]{2,1,0:T(8,128)(2,1)S(1)}, u32[]{:S(2)}, u32[]{:S(2)}) collective-permute-start(bf16[112,9,128]{2,1,0:T(8,128)(2,1)} %get-tuple-element.33), channel_id=1, source_target_pairs={{0,8},{8,16},{16,24},{24,32},{32,40},{40,48},{48,56},{56,64},{64,7... | collective-permute-start | bytes 774152 | tf_op jit(solution)/shard_map/ppermute | solution.py:17
  6.0 17.8 %collective-permute-start.1 = (bf16[112,9,128]{2,1,0:T(8,128)(2,1)}, bf16[112,9,128]{2,1,0:T(8,128)(2,1)}, u32[]{:S(2)}, u32[]{:S(2)}) collective-permute-start(bf16[112,9,128]{2,1,0:T(8,128)(2,1)} %get-tuple-element.34), channel_id=1, source_target_pairs={{8,0},{16,8},{24,16},{32,24},{40,32},{48,40},{56,48},{64,56},{72,6... | collective-permute-start | bytes 774152 | tf_op jit(solution)/shard_map/ppermute | solution.py:18
  15.3 16.2 %copy-start.2 = (bf16[128,16,128]{0,2,1:T(8,128)(2,1)}, bf16[128,16,128]{0,2,1:T(8,128)(2,1)S(1)}, u32[]{:S(2)}) copy-start(bf16[128,16,128]{0,2,1:T(8,128)(2,1)S(1)} %copy.27) | copy-start | bytes 1572868
  22.9 8.6 %copy-start.16 = (bf16[112,9,128]{2,1,0:T(8,128)(2,1)}, bf16[112,9,128]{2,1,0:T(8,128)(2,1)S(1)}, u32[]{:S(2)}) copy-start(bf16[112,9,128]{2,1,0:T(8,128)(2,1)S(1)} %collective-permute-done) | copy-start | bytes 774148
  23.0 6.7 %copy-start.18 = (bf16[128,1,128]{0,2,1:T(8,128)(2,1)}, bf16[128,1,128]{0,2,1:T(8,128)(2,1)S(1)}, u32[]{:S(2)}) copy-start(bf16[128,1,128]{0,2,1:T(8,128)(2,1)S(1)} %copy.26) | copy-start | bytes 98308
  26.0 3.7 %copy-start.20 = (bf16[128,1,128]{0,2,1:T(8,128)(2,1)}, bf16[128,1,128]{0,2,1:T(8,128)(2,1)S(1)}, u32[]{:S(2)}) copy-start(bf16[128,1,128]{0,2,1:T(8,128)(2,1)S(1)} %copy.28) | copy-start | bytes 98308
  38.3 12.2 %collective-permute-start.2 = (bf16[100,34,17]{0,1,2:T(8,128)(2,1)}, bf16[100,34,17]{0,1,2:T(8,128)(2,1)S(1)}, u32[]{:S(2)}, u32[]{:S(2)}) collective-permute-start(bf16[100,34,17]{0,1,2:T(8,128)(2,1)} %copy.31), channel_id=1, source_target_pairs={{0,1},{1,2},{2,3},{3,4},{4,5},{5,6},{6,7},{8,9},{9,10},{10,11},{11... | collective-permute-start | bytes 346808 | tf_op jit(solution)/shard_map/ppermute | solution.py:17
  44.8 9.9 %collective-permute-start.3 = (bf16[100,34,17]{0,1,2:T(8,128)(2,1)}, bf16[100,34,17]{0,1,2:T(8,128)(2,1)S(1)}, u32[]{:S(2)}, u32[]{:S(2)}) collective-permute-start(bf16[100,34,17]{0,1,2:T(8,128)(2,1)} %copy.34), channel_id=1, source_target_pairs={{1,0},{2,1},{3,2},{4,3},{5,4},{6,5},{7,6},{9,8},{10,9},{11,10},{12... | collective-permute-start | bytes 346808 | tf_op jit(solution)/shard_map/ppermute | solution.py:18
  50.5 9.4 %copy-start.14 = (bf16[100,34,17]{0,1,2:T(8,128)(2,1)}, bf16[100,34,17]{0,1,2:T(8,128)(2,1)S(1)}, u32[]{:S(2)}) copy-start(bf16[100,34,17]{0,1,2:T(8,128)(2,1)S(1)} %collective-permute-done.2) | copy-start | bytes 346804
  54.7 5.2 %copy-start.13 = (bf16[100,34,17]{0,1,2:T(8,128)(2,1)}, bf16[100,34,17]{0,1,2:T(8,128)(2,1)S(1)}, u32[]{:S(2)}) copy-start(bf16[100,34,17]{0,1,2:T(8,128)(2,1)S(1)} %collective-permute-done.3) | copy-start | bytes 346804
  59.9 0.9 %copy-start.24 = (pred[18,130]{1,0:T(8,128)(4,1)S(1)}, pred[18,130]{1,0:T(8,128)(4,1)}, u32[]{:S(2)}) copy-start(pred[18,130]{1,0:T(8,128)(4,1)} %broadcast_and_fusion) | copy-start | bytes 7024
  61.1 2.5 %copy-start.15 = (bf16[100,34,17]{0,1,2:T(8,128)(2,1)S(1)}, bf16[100,34,17]{0,1,2:T(8,128)(2,1)}, u32[]{:S(2)}) copy-start(bf16[100,34,17]{0,1,2:T(8,128)(2,1)} %copy-done.14) | copy-start | bytes 346804
  61.1 8.5 %copy-start.3 = (bf16[128,16,128]{0,2,1:T(8,128)(2,1)S(1)}, bf16[128,16,128]{0,2,1:T(8,128)(2,1)}, u32[]{:S(2)}) copy-start(bf16[128,16,128]{0,2,1:T(8,128)(2,1)} %copy-done.2) | copy-start | bytes 1572868
  61.1 8.5 %copy-start.19 = (bf16[128,1,128]{0,2,1:T(8,128)(2,1)S(1)}, bf16[128,1,128]{0,2,1:T(8,128)(2,1)}, u32[]{:S(2)}) copy-start(bf16[128,1,128]{0,2,1:T(8,128)(2,1)} %copy-done.18) | copy-start | bytes 98308
  61.1 8.5 %copy-start.21 = (bf16[128,1,128]{0,2,1:T(8,128)(2,1)S(1)}, bf16[128,1,128]{0,2,1:T(8,128)(2,1)}, u32[]{:S(2)}) copy-start(bf16[128,1,128]{0,2,1:T(8,128)(2,1)} %copy-done.20) | copy-start | bytes 98308
  70.3 1.0 %copy-start.17 = (bf16[3,3,128,224]{2,3,1,0:T(8,128)(2,1)S(1)}, bf16[3,3,128,224]{2,3,1,0:T(8,128)(2,1)}, u32[]{:S(2)}) copy-start(bf16[3,3,128,224]{2,3,1,0:T(8,128)(2,1)} %param.10) | copy-start | bytes 1548292
  70.3 1.3 %copy-start.11 = (bf16[96,16,128]{2,1,0:T(8,128)(2,1)S(1)}, bf16[96,16,128]{2,1,0:T(8,128)(2,1)}, u32[]{:S(2)}) copy-start(bf16[96,16,128]{2,1,0:T(8,128)(2,1)} %get-tuple-element.16) | copy-start | bytes 1179652
  71.4 1.1 %copy-start.5 = (bf16[128,16,128]{2,1,0:T(8,128)(2,1)S(1)}, bf16[128,16,128]{2,1,0:T(8,128)(2,1)}, u32[]{:S(2)}) copy-start(bf16[128,16,128]{2,1,0:T(8,128)(2,1)} %get-tuple-element.30) | copy-start | bytes 1572868
  71.6 1.1 %copy-start.10 = (bf16[96,16,128]{2,1,0:T(8,128)(2,1)S(1)}, bf16[96,16,128]{2,1,0:T(8,128)(2,1)}, u32[]{:S(2)}) copy-start(bf16[96,16,128]{2,1,0:T(8,128)(2,1)} %get-tuple-element.15) | copy-start | bytes 1179652
  72.8 1.0 %copy-start.9 = (bf16[96,16,128]{2,1,0:T(8,128)(2,1)S(1)}, bf16[96,16,128]{2,1,0:T(8,128)(2,1)}, u32[]{:S(2)}) copy-start(bf16[96,16,128]{2,1,0:T(8,128)(2,1)} %get-tuple-element.14) | copy-start | bytes 1179652
  73.8 1.0 %copy-start.8 = (bf16[96,16,128]{2,1,0:T(8,128)(2,1)S(1)}, bf16[96,16,128]{2,1,0:T(8,128)(2,1)}, u32[]{:S(2)}) copy-start(bf16[96,16,128]{2,1,0:T(8,128)(2,1)} %get-tuple-element.13) | copy-start | bytes 1179652
  74.8 1.0 %copy-start.7 = (bf16[96,16,128]{2,1,0:T(8,128)(2,1)S(1)}, bf16[96,16,128]{2,1,0:T(8,128)(2,1)}, u32[]{:S(2)}) copy-start(bf16[96,16,128]{2,1,0:T(8,128)(2,1)} %get-tuple-element.12) | copy-start | bytes 1179652
  75.8 1.0 %copy-start.6 = (bf16[96,16,128]{2,1,0:T(8,128)(2,1)S(1)}, bf16[96,16,128]{2,1,0:T(8,128)(2,1)}, u32[]{:S(2)}) copy-start(bf16[96,16,128]{2,1,0:T(8,128)(2,1)} %get-tuple-element.11) | copy-start | bytes 1179652
  77.1 1.0 %copy-start.4 = (bf16[128,16,128]{2,1,0:T(8,128)(2,1)S(1)}, bf16[128,16,128]{2,1,0:T(8,128)(2,1)}, u32[]{:S(2)}) copy-start(bf16[128,16,128]{2,1,0:T(8,128)(2,1)} %get-tuple-element.29) | copy-start | bytes 1572868
  78.5 1.0 %copy-start.12 = (bf16[96,16,128]{2,1,0:T(8,128)(2,1)S(1)}, bf16[96,16,128]{2,1,0:T(8,128)(2,1)}, u32[]{:S(2)}) copy-start(bf16[96,16,128]{2,1,0:T(8,128)(2,1)} %get-tuple-element.8) | copy-start | bytes 1179652
  78.5 1.0 %copy-start.26 = (f32[128]{0:T(128)S(1)}, f32[128]{0:T(128)}, u32[]{:S(2)}) copy-start(f32[128]{0:T(128)} %param.11) | copy-start | bytes 1540
where the time goes:
time: 82.3 us; the launch traced here: 81 us
  local copies, waits for them, and re-layouts  37.1 us (45%)
  starting transfers between devices  16.7 us (20%)
  other arithmetic  9.61 us (12%)
  between operations  8.16 us (10%)
  matrix products  6.74 us (8%)
  waiting for transfers between devices  2.66 us (3%)
    ppermute x2, starting transfers between devices, with_halo(): after = lax.ppermute(first, axis, down)  10.8 us
    ppermute x2, starting transfers between devices, with_halo(): before = lax.ppermute(last, axis, up)  5.93 us
    concatenate x2, other arithmetic, with_halo(): shard = jnp.concatenate([before, shard, after], axis=dim)  5.17 us
    unnamed x55, local copies, waits for them, and re-layouts  4.19 us
    slice x2, local copies, waits for them, and re-layouts, with_halo(): first = lax.slice_in_dim(shard, 0, width, axis=dim)  4.17 us
    another operation x3, local copies, waits for them, and re-layouts, body(): below_row[:, None, :]  3.68 us
    slice x2, local copies, waits for them, and re-layouts, with_halo(): last = lax.slice_in_dim(shard, length - width, length, axis=dim)  3.62 us
    dot_general x9, matrix products, conv_taps(): jnp.dot(mixer_weight[tap_row, tap_col, :, channels:], older, preferred_el...  2.99 us
  transfers between devices with their start and end apart: 4, of which 1 were waited for; matrix products, arithmetic and copies ran while one was open for 11% of the time, Pallas kernels for 0%

commit v1 on v0

v1 whole, which is shorter than its diff:
```python
import jax
import jax.numpy as jnp
from jax import lax
from jax.experimental import pallas as pl
from jax.experimental.pallas import tpu as pltpu
from jax.sharding import PartitionSpec as P

C = 128
CP = 32
FRAMES = 3
CR = 16
CC = 128
SHIFT_X = 16
SHIFT_Y = 8
REACH = SHIFT_Y + 1
WIN = CR + 2
KROW = 3 * C + 3 * FRAMES * CP
KALL = 2048
TILES = 3
SEG = 21
SEG0 = CC - SEG
VMEM_LIMIT = 48 * 1024 * 1024
f32 = jnp.float32
bf16 = jnp.bfloat16


def slots(off, axis):
    pos = [off[axis, k] > 0 for k in range(FRAMES)]
    first_pos = jnp.where(pos[0], 0, jnp.where(pos[1], 1, 2))
    last_pos = jnp.where(pos[2], 2, jnp.where(pos[1], 1, 0))
    first_neg = jnp.where(pos[0], jnp.where(pos[1], 2, 1), 0)
    last_neg = jnp.where(pos[2], jnp.where(pos[1], 0, 1), 2)
    place = [
        jnp.where(pos[k], jnp.where(first_pos == k, 0, 1), jnp.where(first_neg == k, 0, 1))
        for k in range(FRAMES)
    ]
    return pos, (first_pos, last_pos), (first_neg, last_neg), place


def lanes(shape):
    return lax.broadcasted_iota(jnp.int32, shape, len(shape) - 1)


def compress_kernel(off, hist, cur, w, red, send_a, send_b, hbuf, cbuf, fbuf, sems):
    copies = [pltpu.make_async_copy(hist.at[k], hbuf.at[k], sems.at[k]) for k in range(FRAMES)]
    copies.append(pltpu.make_async_copy(cur, cbuf, sems.at[FRAMES]))
    for copy in copies:
        copy.start()
    row = lax.axis_index("rows")
    even = row % 2 == 0
    for k in range(FRAMES):
        copies[k].wait()
        fbuf[k] = hbuf[k].astype(f32)
        x = jnp.concatenate(
            [fbuf[k, pl.ds(y, C, stride=CR), :].astype(bf16) for y in range(CR)], axis=1
        )
        r = jnp.dot(w[...], x, preferred_element_type=f32).astype(bf16)
        for y in range(CR):
            red[k, y] = r[:, y * CC : (y + 1) * CC]
    copies[FRAMES].wait()
    fbuf[0] = cbuf[...].astype(f32)
    top = fbuf[0, pl.ds(0, C, stride=CR), :].astype(bf16).reshape(C // CP, CP, CC)
    bottom = fbuf[0, pl.ds(CR - 1, C, stride=CR), :].astype(bf16).reshape(C // CP, CP, CC)
    _, posf, negf, _ = slots(off, 0)
    for send, down in ((send_a, even), (send_b, jnp.logical_not(even))):
        start = jnp.where(down, CR - REACH, 0)
        for s in range(2):
            k = jnp.where(down, posf[s], negf[s])
            for i in range(REACH):
                send[s * REACH + i] = red[k, start + i]
        send[2 * REACH : 2 * REACH + C // CP] = jnp.where(down, bottom, top)


def prepare_kernel(cur, wt, cur_t, cols, wall, fbuf):
    fbuf[...] = cur[...].astype(f32)
    lane = lanes((C, CC))
    first = jnp.zeros((C, CC), f32)
    last = jnp.zeros((C, CC), f32)
    for y in range(CR):
        t = fbuf[pl.ds(y, C, stride=CR), :]
        cur_t[y] = t.astype(bf16)
        first = jnp.where(lane == y + 1, pltpu.roll(t, y + 1, 1), first)
        last = jnp.where(lane == y + 1, pltpu.roll(t, y + 2, 1), last)
    cols[0] = first.astype(bf16)
    cols[1] = last.astype(bf16)
    parts = []
    for i in range(3):
        parts += [wt[i, j, :C, :] for j in range(3)]
        parts += [wt[i, j, C:, :] for j in range(3)]
    parts.append(jnp.zeros((KALL - 3 * KROW, C), bf16))
    tall = jnp.concatenate(parts, axis=0).astype(f32)
    for b in range(KALL // C):
        wall[:, b * C : (b + 1) * C] = tall[b * C : (b + 1) * C].T.astype(bf16)


def window_kernel(nrows, off, red, recv_a, recv_b, cols, win, edge, send_a, send_b, cb):
    row = lax.axis_index("rows")
    col = lax.axis_index("cols")
    even = row % 2 == 0
    has_above = row > 0
    has_below = row < nrows - 1
    pos, _, _, place = slots(off, 0)
    zero = jnp.zeros((REACH, CP, CC), bf16)
    for k in range(FRAMES):
        cb[k, REACH : REACH + CR] = red[k]
        at = pl.ds(place[k] * REACH, REACH)
        from_a = recv_a[at]
        from_b = recv_b[at]
        use_a = jnp.logical_xor(pos[k], even)
        ok = jnp.where(pos[k], has_above, has_below)
        halo = jnp.where(ok, jnp.where(use_a, from_a, from_b), zero)
        cb[k, pl.ds(jnp.where(pos[k], 0, REACH + CR), REACH)] = halo
    for k in range(FRAMES):
        start = SHIFT_Y - off[0, k]
        for r in range(WIN):
            v = cb[k, start + r]
            if r == 0:
                v = jnp.where(has_above, v, jnp.zeros_like(v))
            if r == WIN - 1:
                v = jnp.where(has_below, v, jnp.zeros_like(v))
            win[k, r] = v
    tail_a = recv_a[2 * REACH : 2 * REACH + C // CP].reshape(C, CC)
    tail_b = recv_b[2 * REACH : 2 * REACH + C // CP].reshape(C, CC)
    blank = jnp.zeros((C, CC), bf16)
    above = jnp.where(has_above, jnp.where(even, tail_b, tail_a), blank)
    below = jnp.where(has_below, jnp.where(even, tail_a, tail_b), blank)
    edge[0] = above
    edge[1] = below
    above = above.astype(f32)
    below = below.astype(f32)
    ceven = col % 2 == 0
    _, posf, negf, _ = slots(off, 1)
    lane = lanes((CP, CC))
    wide = lanes((C, CC))
    first = jnp.where(wide == 0, above, cols[0].astype(f32))
    first = jnp.where(wide == WIN - 1, pltpu.roll(below, WIN - 1, 1), first)
    last = jnp.where(wide == 0, pltpu.roll(above, 1, 1), cols[1].astype(f32))
    last = jnp.where(wide == WIN - 1, pltpu.roll(below, WIN, 1), last)
    for send, right in ((send_a, ceven), (send_b, jnp.logical_not(ceven))):
        back = jnp.where(right, SEG0, 0)
        for s in range(2):
            k = jnp.where(right, posf[s], negf[s])
            for t in range(TILES):
                total = jnp.zeros((CP, CC), f32)
                for q in range(WIN // TILES):
                    piece = win[k, t + TILES * q].astype(f32)
                    piece = pltpu.roll(piece, (SEG * q - back + CC) % CC, 1)
                    total = jnp.where((lane >= SEG * q) & (lane < SEG * (q + 1)), piece, total)
                send[s * TILES + t] = total.astype(bf16)
        pack = jnp.where(right, last, first)
        total = pack[:CP]
        for g in range(1, C // CP):
            total = jnp.where(lane >= CP * g, pltpu.roll(pack[CP * g : CP * (g + 1)], CP * g, 1), total)
        send[2 * TILES] = total.astype(bf16)


def join_kernel(ncols, off, win, edge, cur_t, recv_a, recv_b, wall, bias, out, x2, acc):
    col = lax.axis_index("cols")
    ceven = col % 2 == 0
    has_left = col > 0
    has_right = col < ncols - 1
    pos, _, _, place = slots(off, 1)
    lane = lanes((CP, CC))
    wide = lanes((C, CC))

    def unpack(ref):
        t = ref[2 * TILES].astype(f32)
        return jnp.concatenate(
            [t] + [pltpu.roll(t, CC - CP * g, 1) for g in range(1, C // CP)], axis=0
        )

    pack_a = unpack(recv_a)
    pack_b = unpack(recv_b)
    left = jnp.where(ceven, pack_b, pack_a)
    right = jnp.where(ceven, pack_a, pack_b)
    left = jnp.where(has_left, left, jnp.zeros_like(left))
    right = jnp.where(has_right, right, jnp.zeros_like(right))

    def put(r, at, size, value):
        if r <= WIN - CR // 2 - 1:
            x2[r * KROW + at : r * KROW + at + size, :CC] = value
        if r >= CR // 2:
            q = r - CR // 2
            x2[q * KROW + at : q * KROW + at + size, CC:] = value

    for r in range(WIN):
        if r == 0:
            here = edge[0]
        elif r == WIN - 1:
            here = edge[1]
        else:
            here = cur_t[r - 1]
        put(r, C, C, here)
        here = here.astype(f32)
        before = jnp.where(wide == 0, pltpu.roll(left, (CC - r) % CC, 1), pltpu.roll(here, 1, 1))
        after = jnp.where(
            wide == CC - 1, pltpu.roll(right, CC - 1 - r, 1), pltpu.roll(here, CC - 1, 1)
        )
        put(r, 0, C, before.astype(bf16))
        put(r, 2 * C, C, after.astype(bf16))
    for k in range(FRAMES):
        use_a = jnp.logical_xor(pos[k], ceven)
        ok = jnp.where(pos[k], has_left, has_right)
        back = jnp.where(pos[k], SEG0, 0)
        tiles = []
        for t in range(TILES):
            a = recv_a[place[k] * TILES + t].astype(f32)
            b = recv_b[place[k] * TILES + t].astype(f32)
            v = jnp.where(use_a, a, b)
            tiles.append(jnp.where(ok, v, jnp.zeros_like(v)))
        taps = []
        for j in range(3):
            s = off[1, k] + 1 - j
            lo = jnp.where(pos[k], CC - s, 0)
            hi = jnp.where(pos[k], CC, -s)
            mask = (lane >= lo) & (lane < hi)
            outside = None
            if j == 0:
                outside = jnp.logical_and(lane == 0, jnp.logical_not(has_left))
            if j == 2:
                outside = jnp.logical_and(lane == CC - 1, jnp.logical_not(has_right))
            taps.append(((s + CC) % CC, mask, outside))
        for r in range(WIN):
            t, q = r % TILES, r // TILES
            local = win[k, r].astype(f32)
            halo = pltpu.roll(tiles[t], (back - SEG * q + CC) % CC, 1)
            for j in range(3):
                s, mask, outside = taps[j]
                v = pltpu.roll(jnp.where(mask, halo, local), s, 1)
                if outside is not None:
                    v = jnp.where(outside, jnp.zeros_like(v), v)
                put(r, 3 * C + j * FRAMES * CP + k * CP, CP, v.astype(bf16))
    x2[(WIN - CR // 2) * KROW :, :] = jnp.zeros((KALL - 3 * KROW, 2 * CC), bf16)
    bias_col = jnp.broadcast_to(bias[...], (C, 2 * CC))
    for y in range(CR // 2):
        p = jnp.dot(
            wall[...], x2[y * KROW : y * KROW + KALL, :], preferred_element_type=f32
        )
        p = jnp.maximum(p + bias_col, 0.0)
        acc[pl.ds(y, C, stride=CR), :] = p[:, :CC]
        acc[pl.ds(y + CR // 2, C, stride=CR), :] = p[:, CC:]
    out[...] = acc[...].astype(bf16)


def swap(x, axis, shifted):
    size = lax.axis_size(axis)
    if shifted:
        pairs = [(i, (i - 1 if i % 2 == 0 else i + 1) % size) for i in range(size)]
    else:
        pairs = [(i, i ^ 1) for i in range(size)]
    return lax.ppermute(x, axis, pairs)


def cost(flops, bytes_accessed):
    return pl.CostEstimate(flops=flops, bytes_accessed=bytes_accessed, transcendentals=0)


def call(kernel, outs, specs, scratch, estimate):
    vmem = pl.BlockSpec(memory_space=pltpu.VMEM)
    return pl.pallas_call(
        kernel,
        out_shape=[jax.ShapeDtypeStruct(shape, bf16) for shape in outs],
        in_specs=specs,
        out_specs=[vmem] * len(outs),
        scratch_shapes=scratch,
        cost_estimate=estimate,
        compiler_params=pltpu.CompilerParams(vmem_limit_bytes=VMEM_LIMIT),
    )


def body(current_frame, history_frames, offsets, compress_weight, mixer_weight, mixer_bias):
    smem = pl.BlockSpec(memory_space=pltpu.SMEM)
    vmem = pl.BlockSpec(memory_space=pltpu.VMEM)
    hbm = pl.BlockSpec(memory_space=pl.ANY)
    off = offsets.T
    hist = history_frames.reshape(FRAMES, C * CR, CC)
    cur = current_frame.reshape(C * CR, CC)
    wt = mixer_weight.transpose(0, 1, 3, 2)
    nrows, ncols = lax.axis_size("rows"), lax.axis_size("cols")
    row_send = (2 * REACH + C // CP, CP, CC)
    col_send = (2 * TILES + 1, CP, CC)
    red, send_a, send_b = call(
        compress_kernel,
        [(FRAMES, CR, CP, CC), row_send, row_send],
        [smem, hbm, hbm, vmem],
        [
            pltpu.VMEM((FRAMES, C * CR, CC), bf16),
            pltpu.VMEM((C * CR, CC), bf16),
            pltpu.VMEM((FRAMES, C * CR, CC), f32),
            pltpu.SemaphoreType.DMA((FRAMES + 1,)),
        ],
        cost(2 * FRAMES * CP * C * CR * CC, 3 << 20),
    )(off, hist, cur, compress_weight)
    recv_a = swap(send_a, "rows", False)
    recv_b = swap(send_b, "rows", True)
    cur_t, cols, wall = call(
        prepare_kernel,
        [(CR, C, CC), (2, C, CC), (C, KALL)],
        [vmem, vmem],
        [pltpu.VMEM((C * CR, CC), f32)],
        cost(1 << 20, 3 << 20),
    )(cur, wt)
    win, edge, send_a, send_b = call(
        lambda *refs: window_kernel(nrows, *refs),
        [(FRAMES, WIN, CP, CC), (2, C, CC), col_send, col_send],
        [smem] + [vmem] * 4,
        [pltpu.VMEM((FRAMES, CR + 2 * REACH, CP, CC), bf16)],
        cost(1 << 20, 2 << 20),
    )(off, red, recv_a, recv_b, cols)
    recv_a = swap(send_a, "cols", False)
    recv_b = swap(send_b, "cols", True)
    (out,) = call(
        lambda *refs: join_kernel(ncols, *refs),
        [(C * CR, CC)],
        [smem] + [vmem] * 7,
        [
            pltpu.VMEM(((WIN - CR // 2) * KROW + KALL - 3 * KROW, 2 * CC), bf16),
            pltpu.VMEM((C * CR, CC), f32),
        ],
        cost(2 * C * KALL * CR * CC, 4 << 20),
    )(off, win, edge, cur_t, recv_a, recv_b, wall, mixer_bias.reshape(C, 1))
    return out.reshape(C, CR, CC)


def solution(mesh):
    in_specs = (P(None, "rows", "cols"), P(None, None, "rows", "cols"), P(), P(), P(), P())
    out_specs = P(None, "rows", "cols")
    return jax.shard_map(body, mesh=mesh, in_specs=in_specs, out_specs=out_specs, check_vma=False)
```

time: 82.3 us -> 30.8 us (0.37)
  the two profiles are of different devices: /device:TPU:14 before, /device:TPU:16 now
where the time goes in v1:
time: 30.8 us; the launch traced here: 30.6 us
  starting transfers between devices  10.5 us (34%)
  waiting for transfers between devices  8.18 us (27%)
  Pallas kernels  7.92 us (26%)
  local copies, waits for them, and re-layouts  3.95 us (13%)
    ppermute x4, starting transfers between devices, swap(): return lax.ppermute(x, axis, pairs)  10.5 us
    ppermute x4, waiting for transfers between devices, swap(): return lax.ppermute(x, axis, pairs)  8.18 us
    unnamed x16, local copies, waits for them, and re-layouts  3.84 us
    pallas_call x1, Pallas kernels, body(): call(lambda *refs: join_kernel(ncols, *refs), [(C * CR, CC)], [smem] + [v...  3.82 us
    pallas_call x1, Pallas kernels, body(): call(compress_kernel, [(FRAMES, CR, CP, CC), row_send, row_send], [smem,...  2.36 us
    pallas_call x1, Pallas kernels, body(): call(lambda *refs: window_kernel(nrows, *refs), [(FRAMES, WIN, CP, CC), (...  0.97 us
    pallas_call x1, Pallas kernels, body(): call(prepare_kernel, [(CR, C, CC), (2, C, CC), (C, KALL)], [vmem, vmem],...  0.77 us
  transfers between devices with their start and end apart: 4, of which 3 were waited for; matrix products, arithmetic and copies ran while one was open for 0% of the time, Pallas kernels for 3%

profile of v1, /device:TPU:16, one launch (start us, length us, event | category | flops | bytes accessed | tf_op | source)
XLA Modules:
  0.0 30.6 jit_solution(8777251149790066351)
XLA Ops:
  0.0 0.0 copy-start
  0.0 1.0 %copy-done = bf16[128,16,128]{2,1,0:T(8,128)(2,1)S(1)} copy-done((bf16[128,16,128]{2,1,0:T(8,128)(2,1)S(1)}, bf16[128,16,128]{2,1,0:T(8,128)(2,1)}, u32[]{:S(2)}) %copy-start) | copy-done | bytes 524312
  1.0 0.0 copy-start.2
  1.0 1.4 %copy-done.2 = bf16[3,128,16,128]{3,2,1,0:T(8,128)(2,1)S(1)} copy-done((bf16[3,128,16,128]{3,2,1,0:T(8,128)(2,1)S(1)}, bf16[3,128,16,128]{3,2,1,0:T(8,128)(2,1)}, u32[]{:S(2)}) %copy-start.2) | copy-done | bytes 1572888
  2.5 0.0 copy-start.4
  2.5 0.7 %copy-done.4 = bf16[32,128]{1,0:T(8,128)(2,1)S(1)} copy-done((bf16[32,128]{1,0:T(8,128)(2,1)S(1)}, bf16[32,128]{1,0:T(8,128)(2,1)}, u32[]{:S(2)}) %copy-start.4) | copy-done | bytes 8216
  3.1 0.0 copy-start.5
  3.2 0.7 %copy-done.5 = s32[3,2]{0,1:T(2,128)S(1)} copy-done((s32[3,2]{0,1:T(2,128)S(1)}, s32[3,2]{0,1:T(2,128)}, u32[]{:S(2)}) %copy-start.5) | copy-done | bytes 48
  3.8 0.0 copy-start.1
  3.8 0.0 copy-start.3
  3.8 0.0 copy-start.7
  3.8 0.0 copy-start.6
  3.8 2.4 %shard_map.64 = (bf16[3,16,32,128]{3,2,1,0:T(8,128)(2,1)S(1)}, bf16[22,32,128]{2,1,0:T(8,128)(2,1)S(1)}, bf16[22,32,128]{2,1,0:T(8,128)(2,1)S(1)}) custom-call(s32[2,3]{1,0:T(2,128)S(1)} %bitcast.10, bf16[3,2048,128]{2,1,0:T(8,128)(2,1)S(1)} %bitcast.8, bf16[2048,128]{1,0:T(8,128)(2,1)S(1)} %bitcast.6, bf16[32,128]{1,0:T(8,128)(2,1)S(1)} %copy-done.4), custom_call_target="tpu_custom_call" | custom-call | flops 50331648 | bytes 3145728 | tf_op jit(solution)/shard_map/pallas_call | solution.py:282
  6.2 0.1 collective-permute-start
  6.3 6.9 %collective-permute-start.1 = (bf16[22,32,128]{2,1,0:T(8,128)(2,1)S(1)}, bf16[22,32,128]{2,1,0:T(8,128)(2,1)S(1)}, u32[]{:S(2)}, u32[]{:S(2)}) collective-permute-start(bf16[22,32,128]{2,1,0:T(8,128)(2,1)S(1)} %get-tuple-element.17), channel_id=1, source_target_pairs={{0,248},{8,16},{16,8},{24,32},{32,24},{40,48},{48,40},{56,64},{64,... | collective-permute-start | bytes 540680 | tf_op jit(solution)/shard_map/ppermute | solution.py:251
  13.2 0.0 copy-done.1
  13.2 0.0 copy-done.3
  13.2 0.8 %shard_map.65 = (bf16[16,128,128]{2,1,0:T(8,128)(2,1)S(1)}, bf16[2,128,128]{2,1,0:T(8,128)(2,1)S(1)}, bf16[128,2048]{1,0:T(8,128)(2,1)S(1)}) custom-call(bf16[2048,128]{1,0:T(8,128)(2,1)S(1)} %bitcast.7, bf16[3,3,224,128]{3,2,1,0:T(8,128)(2,1)S(1)} %bitcast.9), custom_call_target="tpu_custom_call" | custom-call | flops 1048576 | bytes 3145728 | tf_op jit(solution)/shard_map/pallas_call | solution.py:296
  14.0 0.0 collective-permute-done.refs_2_
  14.0 2.4 %collective-permute-done.1.refs_3_ = bf16[22,32,128]{2,1,0:T(8,128)(2,1)S(1)} collective-permute-done((bf16[22,32,128]{2,1,0:T(8,128)(2,1)S(1)}, bf16[22,32,128]{2,1,0:T(8,128)(2,1)S(1)}, u32[]{:S(2)}, u32[]{:S(2)}) %collective-permute-start.1) | collective-permute-done | bytes 180256 | tf_op jit(solution)/shard_map/ppermute | solution.py:251
  16.4 1.0 %shard_map.66 = (bf16[3,18,32,128]{3,2,1,0:T(8,128)(2,1)S(1)}, bf16[2,128,128]{2,1,0:T(8,128)(2,1)S(1)}, bf16[7,32,128]{2,1,0:T(8,128)(2,1)S(1)}, bf16[7,32,128]{2,1,0:T(8,128)(2,1)S(1)}) custom-call(s32[2,3]{1,0:T(2,128)S(1)} %bitcast.11, bf16[3,16,32,128]{3,2,1,0:T(8,128)(2,1)S(1)} %get-tuple-element.15.refs_1_, ...), custom_call_target="tpu_custom_call" | custom-call | flops 1048576 | bytes 2097152 | tf_op jit(solution)/shard_map/pallas_call | solution.py:303
  17.3 2.8 %collective-permute-start.2 = (bf16[7,32,128]{2,1,0:T(8,128)(2,1)S(1)}, bf16[7,32,128]{2,1,0:T(8,128)(2,1)S(1)}, u32[]{:S(2)}, u32[]{:S(2)}) collective-permute-start(bf16[7,32,128]{2,1,0:T(8,128)(2,1)S(1)} %get-tuple-element.22), channel_id=1, source_target_pairs={{0,1},{1,0},{2,3},{3,2},{4,5},{5,4},{6,7},{7,6},{8,9},{9,8},{10,11... | collective-permute-start | bytes 172040 | tf_op jit(solution)/shard_map/ppermute | solution.py:251
  20.2 0.7 %collective-permute-start.3 = (bf16[7,32,128]{2,1,0:T(8,128)(2,1)S(1)}, bf16[7,32,128]{2,1,0:T(8,128)(2,1)S(1)}, u32[]{:S(2)}, u32[]{:S(2)}) collective-permute-start(bf16[7,32,128]{2,1,0:T(8,128)(2,1)S(1)} %get-tuple-element.23), channel_id=1, source_target_pairs={{0,7},{1,2},{2,1},{3,4},{4,3},{5,6},{6,5},{7,0},{8,15},{9,10},{10,... | collective-permute-start | bytes 172040 | tf_op jit(solution)/shard_map/ppermute | solution.py:251
  20.9 0.0 copy-done.7
  20.9 0.1 copy.7.refs_7_
  21.0 2.2 %collective-permute-done.2.refs_4_ = bf16[7,32,128]{2,1,0:T(8,128)(2,1)S(1)} collective-permute-done((bf16[7,32,128]{2,1,0:T(8,128)(2,1)S(1)}, bf16[7,32,128]{2,1,0:T(8,128)(2,1)S(1)}, u32[]{:S(2)}, u32[]{:S(2)}) %collective-permute-start.2) | collective-permute-done | bytes 57376 | tf_op jit(solution)/shard_map/ppermute | solution.py:251
  23.1 3.6 %collective-permute-done.3.refs_5_ = bf16[7,32,128]{2,1,0:T(8,128)(2,1)S(1)} collective-permute-done((bf16[7,32,128]{2,1,0:T(8,128)(2,1)S(1)}, bf16[7,32,128]{2,1,0:T(8,128)(2,1)S(1)}, u32[]{:S(2)}, u32[]{:S(2)}) %collective-permute-start.3) | collective-permute-done | bytes 57376 | tf_op jit(solution)/shard_map/ppermute | solution.py:251
  26.8 0.0 copy-done.6
  26.8 3.8 %shard_map.67 = bf16[2048,128]{1,0:T(8,128)(2,1)} custom-call(s32[2,3]{1,0:T(2,128)S(1)} %bitcast.12, bf16[3,18,32,128]{3,2,1,0:T(8,128)(2,1)S(1)} %get-tuple-element.19.refs_1_, bf16[2,128,128]{2,1,0:T(8,128)(2,1)S(1)} %get-tuple-element.20.refs_2_, bf16[16,128,128]{2,1,0:T(8,128)(2,1)S(1)} %get-tuple-element.21.refs_3_, ...), custom_call_target="tpu_custom_call" | custom-call | flops 1073741824 | bytes 4194304 | tf_op jit(solution)/shard_map/pallas_call | solution.py:312
Async XLA Ops:
  0.0 1.0 %copy-start = (bf16[128,16,128]{2,1,0:T(8,128)(2,1)S(1)}, bf16[128,16,128]{2,1,0:T(8,128)(2,1)}, u32[]{:S(2)}) copy-start(bf16[128,16,128]{2,1,0:T(8,128)(2,1)} %param.6) | copy-start | bytes 1572868
  1.0 1.4 %copy-start.2 = (bf16[3,128,16,128]{3,2,1,0:T(8,128)(2,1)S(1)}, bf16[3,128,16,128]{3,2,1,0:T(8,128)(2,1)}, u32[]{:S(2)}) copy-start(bf16[3,128,16,128]{3,2,1,0:T(8,128)(2,1)} %param.7) | copy-start | bytes 4718596
  2.5 0.7 %copy-start.4 = (bf16[32,128]{1,0:T(8,128)(2,1)S(1)}, bf16[32,128]{1,0:T(8,128)(2,1)}, u32[]{:S(2)}) copy-start(bf16[32,128]{1,0:T(8,128)(2,1)} %w.1) | copy-start | bytes 24580
  3.1 0.7 %copy-start.5 = (s32[3,2]{0,1:T(2,128)S(1)}, s32[3,2]{0,1:T(2,128)}, u32[]{:S(2)}) copy-start(s32[3,2]{0,1:T(2,128)} %param.8) | copy-start | bytes 76
  3.8 9.4 %copy-start.1 = (bf16[128,16,128]{2,1,0:T(8,128)(2,1)S(1)}, bf16[128,16,128]{2,1,0:T(8,128)(2,1)}, u32[]{:S(2)}) copy-start(bf16[128,16,128]{2,1,0:T(8,128)(2,1)} %param.6) | copy-start | bytes 1572868
  3.8 9.4 %copy-start.3 = (bf16[3,3,128,224]{2,3,1,0:T(8,128)(2,1)S(1)}, bf16[3,3,128,224]{2,3,1,0:T(8,128)(2,1)}, u32[]{:S(2)}) copy-start(bf16[3,3,128,224]{2,3,1,0:T(8,128)(2,1)} %param.10) | copy-start | bytes 1548292
  3.8 17.0 %copy-start.7 = (f32[128]{0:T(128)S(1)}, f32[128]{0:T(128)}, u32[]{:S(2)}) copy-start(f32[128]{0:T(128)} %param.11) | copy-start | bytes 1540
  3.8 22.9 %copy-start.6 = (s32[3,2]{0,1:T(2,128)S(1)}, s32[3,2]{0,1:T(2,128)}, u32[]{:S(2)}) copy-start(s32[3,2]{0,1:T(2,128)} %param.8) | copy-start | bytes 76
  6.2 7.8 %collective-permute-start = (bf16[22,32,128]{2,1,0:T(8,128)(2,1)S(1)}, bf16[22,32,128]{2,1,0:T(8,128)(2,1)S(1)}, u32[]{:S(2)}, u32[]{:S(2)}) collective-permute-start(bf16[22,32,128]{2,1,0:T(8,128)(2,1)S(1)} %get-tuple-element.16), channel_id=1, source_target_pairs={{0,8},{8,0},{16,24},{24,16},{32,40},{40,32},{48,56},{56,48},{64,72... | collective-permute-start | bytes 540680 | tf_op jit(solution)/shard_map/ppermute | solution.py:251
  6.3 10.1 %collective-permute-start.1 = (bf16[22,32,128]{2,1,0:T(8,128)(2,1)S(1)}, bf16[22,32,128]{2,1,0:T(8,128)(2,1)S(1)}, u32[]{:S(2)}, u32[]{:S(2)}) collective-permute-start(bf16[22,32,128]{2,1,0:T(8,128)(2,1)S(1)} %get-tuple-element.17), channel_id=1, source_target_pairs={{0,248},{8,16},{16,8},{24,32},{32,24},{40,48},{48,40},{56,64},{64,... | collective-permute-start | bytes 540680 | tf_op jit(solution)/shard_map/ppermute | solution.py:251
  17.3 5.8 %collective-permute-start.2 = (bf16[7,32,128]{2,1,0:T(8,128)(2,1)S(1)}, bf16[7,32,128]{2,1,0:T(8,128)(2,1)S(1)}, u32[]{:S(2)}, u32[]{:S(2)}) collective-permute-start(bf16[7,32,128]{2,1,0:T(8,128)(2,1)S(1)} %get-tuple-element.22), channel_id=1, source_target_pairs={{0,1},{1,0},{2,3},{3,2},{4,5},{5,4},{6,7},{7,6},{8,9},{9,8},{10,11... | collective-permute-start | bytes 172040 | tf_op jit(solution)/shard_map/ppermute | solution.py:251
  20.2 6.6 %collective-permute-start.3 = (bf16[7,32,128]{2,1,0:T(8,128)(2,1)S(1)}, bf16[7,32,128]{2,1,0:T(8,128)(2,1)S(1)}, u32[]{:S(2)}, u32[]{:S(2)}) collective-permute-start(bf16[7,32,128]{2,1,0:T(8,128)(2,1)S(1)} %get-tuple-element.23), channel_id=1, source_target_pairs={{0,7},{1,2},{2,1},{3,4},{4,3},{5,6},{6,5},{7,0},{8,15},{9,10},{10,... | collective-permute-start | bytes 172040 | tf_op jit(solution)/shard_map/ppermute | solution.py:251

commit v2 on v1

--- a/solution.py
+++ b/solution.py
@@ -41,13 +41,20 @@
     return lax.broadcasted_iota(jnp.int32, shape, len(shape) - 1)
 
 
-def compress_kernel(off, hist, cur, w, red, send_a, send_b, hbuf, cbuf, fbuf, sems):
+def compress_kernel(
+    off_hbm, hist, cur, w_hbm, red, send_a, send_b, off, w, hbuf, cbuf, fbuf, sems
+):
     copies = [pltpu.make_async_copy(hist.at[k], hbuf.at[k], sems.at[k]) for k in range(FRAMES)]
     copies.append(pltpu.make_async_copy(cur, cbuf, sems.at[FRAMES]))
-    for copy in copies:
+    small = [
+        pltpu.make_async_copy(w_hbm, w, sems.at[FRAMES + 1]),
+        pltpu.make_async_copy(off_hbm, off, sems.at[FRAMES + 2]),
+    ]
+    for copy in small[:1] + copies + small[1:]:
         copy.start()
     row = lax.axis_index("rows")
     even = row % 2 == 0
+    small[0].wait()
     for k in range(FRAMES):
         copies[k].wait()
         fbuf[k] = hbuf[k].astype(f32)
@@ -61,6 +68,7 @@
     fbuf[0] = cbuf[...].astype(f32)
     top = fbuf[0, pl.ds(0, C, stride=CR), :].astype(bf16).reshape(C // CP, CP, CC)
     bottom = fbuf[0, pl.ds(CR - 1, C, stride=CR), :].astype(bf16).reshape(C // CP, CP, CC)
+    small[1].wait()
     _, posf, negf, _ = slots(off, 0)
     for send, down in ((send_a, even), (send_b, jnp.logical_not(even))):
         start = jnp.where(down, CR - REACH, 0)
@@ -271,7 +279,7 @@
 def body(current_frame, history_frames, offsets, compress_weight, mixer_weight, mixer_bias):
     smem = pl.BlockSpec(memory_space=pltpu.SMEM)
     vmem = pl.BlockSpec(memory_space=pltpu.VMEM)
-    hbm = pl.BlockSpec(memory_space=pl.ANY)
+    hbm = pl.BlockSpec(memory_space=pltpu.HBM)
     off = offsets.T
     hist = history_frames.reshape(FRAMES, C * CR, CC)
     cur = current_frame.reshape(C * CR, CC)
@@ -282,15 +290,17 @@
     red, send_a, send_b = call(
         compress_kernel,
         [(FRAMES, CR, CP, CC), row_send, row_send],
-        [smem, hbm, hbm, vmem],
+        [hbm] * 4,
         [
+            pltpu.SMEM((2, FRAMES), jnp.int32),
+            pltpu.VMEM((CP, C), bf16),
             pltpu.VMEM((FRAMES, C * CR, CC), bf16),
             pltpu.VMEM((C * CR, CC), bf16),
             pltpu.VMEM((FRAMES, C * CR, CC), f32),
-            pltpu.SemaphoreType.DMA((FRAMES + 1,)),
+            pltpu.SemaphoreType.DMA((FRAMES + 3,)),
         ],
         cost(2 * FRAMES * CP * C * CR * CC, 3 << 20),
-    )(off, hist, cur, compress_weight)
+    )(*[pltpu.with_memory_space_constraint(v, pltpu.HBM) for v in (off, hist, cur, compress_weight)])
     recv_a = swap(send_a, "rows", False)
     recv_b = swap(send_b, "rows", True)
     cur_t, cols, wall = call(

time: 30.8 us -> 27.3 us (0.89)
  local copies, waits for them, and re-layouts: 3.95 us -> 0.13 us
  Pallas kernels: 7.92 us -> 8.37 us
    unnamed x16 -> x8, local copies, waits for them, and re-layouts: 3.84 us -> 0.02 us
    pallas_call x1, Pallas kernels: 2.36 us -> 2.82 us  [body(): call(compress_kernel, [(FRAMES, CR, CP, CC), row_send, row_send], [hbm] *...]
where the time goes in v2:
time: 27.3 us; the launch traced here: 27.2 us
  starting transfers between devices  10.5 us (38%)
  Pallas kernels  8.37 us (31%)
  waiting for transfers between devices  8.18 us (30%)
    ppermute x4, starting transfers between devices, swap(): return lax.ppermute(x, axis, pairs)  10.5 us
    ppermute x4, waiting for transfers between devices, swap(): return lax.ppermute(x, axis, pairs)  8.18 us
    pallas_call x1, Pallas kernels, body(): call(lambda *refs: join_kernel(ncols, *refs), [(C * CR, CC)], [smem] + [v...  3.82 us
    pallas_call x1, Pallas kernels, body(): call(compress_kernel, [(FRAMES, CR, CP, CC), row_send, row_send], [hbm] *...  2.82 us
    pallas_call x1, Pallas kernels, body(): call(lambda *refs: window_kernel(nrows, *refs), [(FRAMES, WIN, CP, CC), (...  0.97 us
    pallas_call x1, Pallas kernels, body(): call(prepare_kernel, [(CR, C, CC), (2, C, CC), (C, KALL)], [vmem, vmem],...  0.76 us
  transfers between devices with their start and end apart: 4, of which 3 were waited for; matrix products, arithmetic and copies ran while one was open for 0% of the time, Pallas kernels for 3%

profile of v2, /device:TPU:16, one launch (start us, length us, event | category | flops | bytes accessed | tf_op | source)
XLA Modules:
  0.0 27.2 jit_solution(7593595305540984637)
XLA Ops:
  0.0 0.0 copy-start
  0.0 0.0 copy-start.1
  0.0 0.0 copy-start.2
  0.0 0.0 copy-start.3
  0.0 2.8 %shard_map.64 = (bf16[3,16,32,128]{3,2,1,0:T(8,128)(2,1)S(1)}, bf16[22,32,128]{2,1,0:T(8,128)(2,1)S(1)}, bf16[22,32,128]{2,1,0:T(8,128)(2,1)S(1)}) custom-call(s32[2,3]{1,0:T(2,128)} %bitcast.9, bf16[3,2048,128]{2,1,0:T(8,128)(2,1)} %bitcast.12, bf16[2048,128]{1,0:T(8,128)(2,1)} %bitcast.6, bf16[32,128]{1,0:T(8,128)(2,1)} %w_hbm.1), custom_call_target="tpu_custom_call" | custom-call | flops 50331648 | bytes 3145728 | tf_op jit(solution)/shard_map/pallas_call | solution.py:290
  2.8 0.1 collective-permute-start
  2.9 6.9 %collective-permute-start.1 = (bf16[22,32,128]{2,1,0:T(8,128)(2,1)S(1)}, bf16[22,32,128]{2,1,0:T(8,128)(2,1)S(1)}, u32[]{:S(2)}, u32[]{:S(2)}) collective-permute-start(bf16[22,32,128]{2,1,0:T(8,128)(2,1)S(1)} %get-tuple-element.17), channel_id=1, source_target_pairs={{0,248},{8,16},{16,8},{24,32},{32,24},{40,48},{48,40},{56,64},{64,... | collective-permute-start | bytes 540680 | tf_op jit(solution)/shard_map/ppermute | solution.py:259
  9.8 0.0 copy-done
  9.8 0.0 copy-done.1
  9.8 0.8 %shard_map.65 = (bf16[16,128,128]{2,1,0:T(8,128)(2,1)S(1)}, bf16[2,128,128]{2,1,0:T(8,128)(2,1)S(1)}, bf16[128,2048]{1,0:T(8,128)(2,1)S(1)}) custom-call(bf16[2048,128]{1,0:T(8,128)(2,1)S(1)} %bitcast.7, bf16[3,3,224,128]{3,2,1,0:T(8,128)(2,1)S(1)} %bitcast.8), custom_call_target="tpu_custom_call" | custom-call | flops 1048576 | bytes 3145728 | tf_op jit(solution)/shard_map/pallas_call | solution.py:306
  10.6 0.0 collective-permute-done.refs_2_
  10.6 2.4 %collective-permute-done.1.refs_3_ = bf16[22,32,128]{2,1,0:T(8,128)(2,1)S(1)} collective-permute-done((bf16[22,32,128]{2,1,0:T(8,128)(2,1)S(1)}, bf16[22,32,128]{2,1,0:T(8,128)(2,1)S(1)}, u32[]{:S(2)}, u32[]{:S(2)}) %collective-permute-start.1) | collective-permute-done | bytes 180256 | tf_op jit(solution)/shard_map/ppermute | solution.py:259
  13.0 0.0 copy-done.2
  13.0 1.0 %shard_map.66 = (bf16[3,18,32,128]{3,2,1,0:T(8,128)(2,1)S(1)}, bf16[2,128,128]{2,1,0:T(8,128)(2,1)S(1)}, bf16[7,32,128]{2,1,0:T(8,128)(2,1)S(1)}, bf16[7,32,128]{2,1,0:T(8,128)(2,1)S(1)}) custom-call(s32[2,3]{1,0:T(2,128)S(1)} %bitcast.10, bf16[3,16,32,128]{3,2,1,0:T(8,128)(2,1)S(1)} %get-tuple-element.15.refs_1_, ...), custom_call_target="tpu_custom_call" | custom-call | flops 1048576 | bytes 2097152 | tf_op jit(solution)/shard_map/pallas_call | solution.py:313
  14.0 2.8 %collective-permute-start.2 = (bf16[7,32,128]{2,1,0:T(8,128)(2,1)S(1)}, bf16[7,32,128]{2,1,0:T(8,128)(2,1)S(1)}, u32[]{:S(2)}, u32[]{:S(2)}) collective-permute-start(bf16[7,32,128]{2,1,0:T(8,128)(2,1)S(1)} %get-tuple-element.22), channel_id=1, source_target_pairs={{0,1},{1,0},{2,3},{3,2},{4,5},{5,4},{6,7},{7,6},{8,9},{9,8},{10,11... | collective-permute-start | bytes 172040 | tf_op jit(solution)/shard_map/ppermute | solution.py:259
  16.8 0.7 %collective-permute-start.3 = (bf16[7,32,128]{2,1,0:T(8,128)(2,1)S(1)}, bf16[7,32,128]{2,1,0:T(8,128)(2,1)S(1)}, u32[]{:S(2)}, u32[]{:S(2)}) collective-permute-start(bf16[7,32,128]{2,1,0:T(8,128)(2,1)S(1)} %get-tuple-element.23), channel_id=1, source_target_pairs={{0,7},{1,2},{2,1},{3,4},{4,3},{5,6},{6,5},{7,0},{8,15},{9,10},{10,... | collective-permute-start | bytes 172040 | tf_op jit(solution)/shard_map/ppermute | solution.py:259
  17.5 0.0 copy-done.3
  17.5 0.1 copy.7.refs_7_
  17.6 2.1 %collective-permute-done.2.refs_4_ = bf16[7,32,128]{2,1,0:T(8,128)(2,1)S(1)} collective-permute-done((bf16[7,32,128]{2,1,0:T(8,128)(2,1)S(1)}, bf16[7,32,128]{2,1,0:T(8,128)(2,1)S(1)}, u32[]{:S(2)}, u32[]{:S(2)}) %collective-permute-start.2) | collective-permute-done | bytes 57376 | tf_op jit(solution)/shard_map/ppermute | solution.py:259
  19.8 3.6 %collective-permute-done.3.refs_5_ = bf16[7,32,128]{2,1,0:T(8,128)(2,1)S(1)} collective-permute-done((bf16[7,32,128]{2,1,0:T(8,128)(2,1)S(1)}, bf16[7,32,128]{2,1,0:T(8,128)(2,1)S(1)}, u32[]{:S(2)}, u32[]{:S(2)}) %collective-permute-start.3) | collective-permute-done | bytes 57376 | tf_op jit(solution)/shard_map/ppermute | solution.py:259
  23.4 3.8 %shard_map.67 = bf16[2048,128]{1,0:T(8,128)(2,1)} custom-call(s32[2,3]{1,0:T(2,128)S(1)} %bitcast.11, bf16[3,18,32,128]{3,2,1,0:T(8,128)(2,1)S(1)} %get-tuple-element.19.refs_1_, bf16[2,128,128]{2,1,0:T(8,128)(2,1)S(1)} %get-tuple-element.20.refs_2_, bf16[16,128,128]{2,1,0:T(8,128)(2,1)S(1)} %get-tuple-element.21.refs_3_, ...), custom_call_target="tpu_custom_call" | custom-call | flops 1073741824 | bytes 4194304 | tf_op jit(solution)/shard_map/pallas_call | solution.py:322
Async XLA Ops:
  0.0 9.8 %copy-start = (bf16[128,16,128]{2,1,0:T(8,128)(2,1)S(1)}, bf16[128,16,128]{2,1,0:T(8,128)(2,1)}, u32[]{:S(2)}) copy-start(bf16[128,16,128]{2,1,0:T(8,128)(2,1)} %param.6) | copy-start | bytes 1572868
  0.0 9.8 %copy-start.1 = (bf16[3,3,128,224]{2,3,1,0:T(8,128)(2,1)S(1)}, bf16[3,3,128,224]{2,3,1,0:T(8,128)(2,1)}, u32[]{:S(2)}) copy-start(bf16[3,3,128,224]{2,3,1,0:T(8,128)(2,1)} %param.10) | copy-start | bytes 1548292
  0.0 13.0 %copy-start.2 = (s32[3,2]{0,1:T(2,128)S(1)}, s32[3,2]{0,1:T(2,128)}, u32[]{:S(2)}) copy-start(s32[3,2]{0,1:T(2,128)} %param.8) | copy-start | bytes 76
  0.0 17.5 %copy-start.3 = (f32[128]{0:T(128)S(1)}, f32[128]{0:T(128)}, u32[]{:S(2)}) copy-start(f32[128]{0:T(128)} %param.11) | copy-start | bytes 1540
  2.8 7.8 %collective-permute-start = (bf16[22,32,128]{2,1,0:T(8,128)(2,1)S(1)}, bf16[22,32,128]{2,1,0:T(8,128)(2,1)S(1)}, u32[]{:S(2)}, u32[]{:S(2)}) collective-permute-start(bf16[22,32,128]{2,1,0:T(8,128)(2,1)S(1)} %get-tuple-element.16), channel_id=1, source_target_pairs={{0,8},{8,0},{16,24},{24,16},{32,40},{40,32},{48,56},{56,48},{64,72... | collective-permute-start | bytes 540680 | tf_op jit(solution)/shard_map/ppermute | solution.py:259
  2.9 10.1 %collective-permute-start.1 = (bf16[22,32,128]{2,1,0:T(8,128)(2,1)S(1)}, bf16[22,32,128]{2,1,0:T(8,128)(2,1)S(1)}, u32[]{:S(2)}, u32[]{:S(2)}) collective-permute-start(bf16[22,32,128]{2,1,0:T(8,128)(2,1)S(1)} %get-tuple-element.17), channel_id=1, source_target_pairs={{0,248},{8,16},{16,8},{24,32},{32,24},{40,48},{48,40},{56,64},{64,... | collective-permute-start | bytes 540680 | tf_op jit(solution)/shard_map/ppermute | solution.py:259
  14.0 5.8 %collective-permute-start.2 = (bf16[7,32,128]{2,1,0:T(8,128)(2,1)S(1)}, bf16[7,32,128]{2,1,0:T(8,128)(2,1)S(1)}, u32[]{:S(2)}, u32[]{:S(2)}) collective-permute-start(bf16[7,32,128]{2,1,0:T(8,128)(2,1)S(1)} %get-tuple-element.22), channel_id=1, source_target_pairs={{0,1},{1,0},{2,3},{3,2},{4,5},{5,4},{6,7},{7,6},{8,9},{9,8},{10,11... | collective-permute-start | bytes 172040 | tf_op jit(solution)/shard_map/ppermute | solution.py:259
  16.8 6.6 %collective-permute-start.3 = (bf16[7,32,128]{2,1,0:T(8,128)(2,1)S(1)}, bf16[7,32,128]{2,1,0:T(8,128)(2,1)S(1)}, u32[]{:S(2)}, u32[]{:S(2)}) collective-permute-start(bf16[7,32,128]{2,1,0:T(8,128)(2,1)S(1)} %get-tuple-element.23), channel_id=1, source_target_pairs={{0,7},{1,2},{2,1},{3,4},{4,3},{5,6},{6,5},{7,0},{8,15},{9,10},{10,... | collective-permute-start | bytes 172040 | tf_op jit(solution)/shard_map/ppermute | solution.py:259

commit v3 on v2

v3 whole, which is shorter than its diff:
```python
import jax
import jax.numpy as jnp
from jax import lax
from jax.experimental import pallas as pl
from jax.experimental.pallas import tpu as pltpu
from jax.sharding import PartitionSpec as P

C = 128
CP = 32
FRAMES = 3
CR = 16
CC = 128
SHIFT_X = 16
SHIFT_Y = 8
REACH = SHIFT_Y + 1
WIN = CR + 2
KROW = 3 * C + 3 * FRAMES * CP
KALL = 2048
EROW = 2 * C + 3 * FRAMES * CP
KEDGE = 1664
TILES = 3
SEG = 21
SEG0 = CC - SEG
VMEM_LIMIT = 48 * 1024 * 1024
f32 = jnp.float32
bf16 = jnp.bfloat16


def slots(off, axis):
    pos = [off[axis, k] > 0 for k in range(FRAMES)]
    first_pos = jnp.where(pos[0], 0, jnp.where(pos[1], 1, 2))
    last_pos = jnp.where(pos[2], 2, jnp.where(pos[1], 1, 0))
    first_neg = jnp.where(pos[0], jnp.where(pos[1], 2, 1), 0)
    last_neg = jnp.where(pos[2], jnp.where(pos[1], 0, 1), 2)
    place = [
        jnp.where(pos[k], jnp.where(first_pos == k, 0, 1), jnp.where(first_neg == k, 0, 1))
        for k in range(FRAMES)
    ]
    return pos, (first_pos, last_pos), (first_neg, last_neg), place


def lanes(shape):
    return lax.broadcasted_iota(jnp.int32, shape, len(shape) - 1)


def compress_kernel(
    off_hbm, hist, cur, w_hbm, red, send_a, send_b, off, w, hbuf, cbuf, fbuf, sems
):
    copies = [pltpu.make_async_copy(hist.at[k], hbuf.at[k], sems.at[k]) for k in range(FRAMES)]
    copies.append(pltpu.make_async_copy(cur, cbuf, sems.at[FRAMES]))
    small = [
        pltpu.make_async_copy(w_hbm, w, sems.at[FRAMES + 1]),
        pltpu.make_async_copy(off_hbm, off, sems.at[FRAMES + 2]),
    ]
    for copy in small[:1] + copies + small[1:]:
        copy.start()
    row = lax.axis_index("rows")
    even = row % 2 == 0
    small[0].wait()
    for k in range(FRAMES):
        copies[k].wait()
        fbuf[k] = hbuf[k].astype(f32)
        x = jnp.concatenate(
            [fbuf[k, pl.ds(y, C, stride=CR), :].astype(bf16) for y in range(CR)], axis=1
        )
        r = jnp.dot(w[...], x, preferred_element_type=f32).astype(bf16)
        for y in range(CR):
            red[k, y] = r[:, y * CC : (y + 1) * CC]
    copies[FRAMES].wait()
    fbuf[0] = cbuf[...].astype(f32)
    top = fbuf[0, pl.ds(0, C, stride=CR), :].astype(bf16).reshape(C // CP, CP, CC)
    bottom = fbuf[0, pl.ds(CR - 1, C, stride=CR), :].astype(bf16).reshape(C // CP, CP, CC)
    small[1].wait()
    _, posf, negf, _ = slots(off, 0)
    for send, down in ((send_a, even), (send_b, jnp.logical_not(even))):
        start = jnp.where(down, CR - REACH, 0)
        for s in range(2):
            k = jnp.where(down, posf[s], negf[s])
            for i in range(REACH):
                send[s * REACH + i] = red[k, start + i]
        send[2 * REACH : 2 * REACH + C // CP] = jnp.where(down, bottom, top)


def spot(r):
    return SEG * (r // TILES) + r % TILES


def segment_lane(shape):
    lane = lanes(shape)
    base = jnp.zeros(shape, jnp.int32)
    for m in range(1, CC // SEG + 1):
        base = jnp.where(lane >= SEG * m, SEG * m, base)
    return lane - base


def prepare_kernel(cur, wt, cur_t, cols, wall, wedge, fbuf):
    fbuf[...] = cur[...].astype(f32)
    lane = lanes((C, CC))
    first = jnp.zeros((C, CC), f32)
    last = jnp.zeros((C, CC), f32)
    for y in range(CR):
        t = fbuf[pl.ds(y, C, stride=CR), :]
        cur_t[y] = t.astype(bf16)
        at = spot(y + 1)
        first = jnp.where(lane == at, pltpu.roll(t, at, 1), first)
        last = jnp.where(lane == at, pltpu.roll(t, at + 1, 1), last)
    cols[0] = first.astype(bf16)
    cols[1] = last.astype(bf16)
    for dest, taps, size in ((wall, (0, 1, 2), KALL), (wedge, (0, 2), KEDGE)):
        parts = []
        for i in range(3):
            parts += [wt[i, j, :C, :] for j in taps]
            parts += [wt[i, j, C:, :] for j in range(3)]
        parts.append(jnp.zeros((size - sum(p.shape[0] for p in parts), C), bf16))
        tall = jnp.concatenate(parts, axis=0).astype(f32)
        for b in range(size // C):
            dest[:, b * C : (b + 1) * C] = tall[b * C : (b + 1) * C].T.astype(bf16)


def row_halo(nrows, off, red, recv_a, recv_b, cb):
    row = lax.axis_index("rows")
    even = row % 2 == 0
    has_above = row > 0
    has_below = row < nrows - 1
    pos, _, _, place = slots(off, 0)
    zero = jnp.zeros((REACH, CP, CC), bf16)
    for k in range(FRAMES):
        cb[k, REACH : REACH + CR] = red[k]
        at = pl.ds(place[k] * REACH, REACH)
        from_a = recv_a[at]
        from_b = recv_b[at]
        use_a = jnp.logical_xor(pos[k], even)
        ok = jnp.where(pos[k], has_above, has_below)
        halo = jnp.where(ok, jnp.where(use_a, from_a, from_b), zero)
        cb[k, pl.ds(jnp.where(pos[k], 0, REACH + CR), REACH)] = halo
    tail_a = recv_a[2 * REACH : 2 * REACH + C // CP].reshape(C, CC)
    tail_b = recv_b[2 * REACH : 2 * REACH + C // CP].reshape(C, CC)
    blank = jnp.zeros((C, CC), bf16)
    above = jnp.where(has_above, jnp.where(even, tail_b, tail_a), blank)
    below = jnp.where(has_below, jnp.where(even, tail_a, tail_b), blank)
    return above, below, has_above, has_below


def window_row(off, cb, k, r, has_above, has_below):
    v = cb[k, SHIFT_Y - off[0, k] + r]
    if r == 0:
        v = jnp.where(has_above, v, jnp.zeros_like(v))
    if r == WIN - 1:
        v = jnp.where(has_below, v, jnp.zeros_like(v))
    return v


def pack_kernel(nrows, off, red, recv_a, recv_b, cols, send_a, send_b, cb):
    above, below, has_above, has_below = row_halo(nrows, off, red, recv_a, recv_b, cb)
    above = above.astype(f32)
    below = below.astype(f32)
    ceven = lax.axis_index("cols") % 2 == 0
    _, posf, negf, _ = slots(off, 1)
    lane = lanes((CP, CC))
    inner = segment_lane((CP, CC))
    wide = lanes((C, CC))
    end = spot(WIN - 1)
    first = jnp.where(wide == 0, above, cols[0].astype(f32))
    first = jnp.where(wide == end, pltpu.roll(below, end, 1), first)
    last = jnp.where(wide == 0, pltpu.roll(above, 1, 1), cols[1].astype(f32))
    last = jnp.where(wide == end, pltpu.roll(below, end + 1, 1), last)
    for send, right in ((send_a, ceven), (send_b, jnp.logical_not(ceven))):
        back = jnp.where(right, SEG0, 0)
        for s in range(2):
            k = jnp.where(right, posf[s], negf[s])
            for t in range(TILES):
                total = jnp.zeros((CP, CC), f32)
                for q in range(WIN // TILES):
                    piece = window_row(off, cb, k, t + TILES * q, has_above, has_below)
                    piece = pltpu.roll(piece.astype(f32), (SEG * q - back + CC) % CC, 1)
                    total = piece if q == 0 else jnp.where(lane >= SEG * q, piece, total)
                send[s * TILES + t] = total.astype(bf16)
        pack = jnp.where(right, last, first)
        total = pack[:CP]
        for g in range(1, C // CP):
            moved = pltpu.roll(pack[CP * g : CP * (g + 1)], TILES * g, 1)
            total = jnp.where(inner >= TILES * g, moved, total)
        send[2 * TILES] = total.astype(bf16)


def local_kernel(nrows, ncols, off, red, recv_a, recv_b, cur_t, wall, bias, part, cb, x2):
    above, below, has_above, has_below = row_halo(nrows, off, red, recv_a, recv_b, cb)
    col = lax.axis_index("cols")
    has_left = col > 0
    has_right = col < ncols - 1
    pos, _, _, _ = slots(off, 1)
    lane = lanes((CP, CC))
    wide = lanes((C, CC))

    def put(r, at, size, value):
        if r <= WIN - CR // 2 - 1:
            x2[r * KROW + at : r * KROW + at + size, :CC] = value
        if r >= CR // 2:
            q = r - CR // 2
            x2[q * KROW + at : q * KROW + at + size, CC:] = value

    taps = []
    for k in range(FRAMES):
        for j in range(3):
            s = off[1, k] + 1 - j
            lo = jnp.where(pos[k], s, 0)
            hi = jnp.where(pos[k], CC, CC + s)
            if j == 0:
                lo = jnp.where(has_left, lo, jnp.maximum(lo, 1))
            if j == 2:
                hi = jnp.where(has_right, hi, jnp.minimum(hi, CC - 1))
            taps.append(((s + CC) % CC, (lane >= lo) & (lane < hi)))
    for r in range(WIN):
        here = above if r == 0 else below if r == WIN - 1 else cur_t[r - 1]
        put(r, C, C, here)
        here = here.astype(f32)
        zero = jnp.zeros_like(here)
        put(r, 0, C, jnp.where(wide == 0, zero, pltpu.roll(here, 1, 1)).astype(bf16))
        put(r, 2 * C, C, jnp.where(wide == CC - 1, zero, pltpu.roll(here, CC - 1, 1)).astype(bf16))
        for k in range(FRAMES):
            own = window_row(off, cb, k, r, has_above, has_below).astype(f32)
            for j in range(3):
                s, mask = taps[3 * k + j]
                v = jnp.where(mask, pltpu.roll(own, s, 1), jnp.zeros_like(own))
                put(r, 3 * C + j * FRAMES * CP + k * CP, CP, v.astype(bf16))
    x2[(WIN - CR // 2) * KROW :, :] = jnp.zeros((KALL - 3 * KROW, 2 * CC), bf16)
    bias_col = jnp.broadcast_to(bias[...], (C, 2 * CC))
    for y in range(CR // 2):
        p = jnp.dot(
            wall[...], x2[y * KROW : y * KROW + KALL, :], preferred_element_type=f32
        )
        part[y] = p + bias_col


def finish_kernel(ncols, off, recv_a, recv_b, part, wedge, out, xx, acc):
    col = lax.axis_index("cols")
    ceven = col % 2 == 0
    has_left = col > 0
    has_right = col < ncols - 1
    pos, _, _, place = slots(off, 1)
    inner = segment_lane((CP, CC))
    zero = jnp.zeros((CP, CC), bf16)
    cur_a = recv_a[2 * TILES].astype(f32)
    cur_b = recv_b[2 * TILES].astype(f32)
    left = jnp.where(ceven, cur_b, cur_a)
    right = jnp.where(ceven, cur_a, cur_b)
    left = jnp.where(has_left, left, jnp.zeros_like(left))
    right = jnp.where(has_right, right, jnp.zeros_like(right))
    frames = []
    for k in range(FRAMES):
        use_a = jnp.logical_xor(pos[k], ceven)
        ok = jnp.where(pos[k], has_left, has_right)
        tiles = []
        for t in range(TILES):
            v = jnp.where(use_a, recv_a[place[k] * TILES + t], recv_b[place[k] * TILES + t])
            tiles.append(jnp.where(ok, v, zero).astype(f32))
        masks = []
        for j in range(3):
            s = off[1, k] + 1 - j
            lo = jnp.where(pos[k], 0, SEG + s)
            hi = jnp.where(pos[k], s, SEG)
            mask = (inner >= lo) & (inner < hi)
            masks.append((jnp.where(pos[k], s - SEG, s + SEG), mask))
        frames.append((tiles, masks))
    for u in range(TILES + 2):
        base = u * EROW
        back = SEG * (u // TILES)
        shift = back + u % TILES
        for g in range(C // CP):
            rows = slice(base + g * CP, base + (g + 1) * CP)
            v = pltpu.roll(left, (2 * CC - shift - TILES * g) % CC, 1)
            xx[rows, :CC] = jnp.where(inner == 0, v, 0.0).astype(bf16)
            xx[rows, CC:] = zero
            rows = slice(base + C + g * CP, base + C + (g + 1) * CP)
            v = pltpu.roll(right, (2 * CC + SEG - 1 - shift - TILES * g) % CC, 1)
            xx[rows, :CC] = zero
            xx[rows, CC:] = jnp.where(inner == SEG - 1, v, 0.0).astype(bf16)
        for k in range(FRAMES):
            tiles, masks = frames[k]
            for j in range(3):
                move, mask = masks[j]
                v = pltpu.roll(tiles[u % TILES], (move - back + 2 * CC) % CC, 1)
                v = jnp.where(mask, v, 0.0).astype(bf16)
                at = base + 2 * C + j * FRAMES * CP + k * CP
                xx[at : at + CP, :CC] = jnp.where(pos[k], v, zero)
                xx[at : at + CP, CC:] = jnp.where(pos[k], zero, v)
    xx[(TILES + 2) * EROW :, :] = jnp.zeros((KEDGE - 3 * EROW, 2 * CC), bf16)
    wide = lanes((C, CC))
    for t in range(TILES):
        p = jnp.dot(
            wedge[...], xx[t * EROW : t * EROW + KEDGE, :], preferred_element_type=f32
        )
        for y in range(t, CR, TILES):
            q = y // TILES
            lft = pltpu.roll(p[:, :CC], (CC - SEG * q) % CC, 1)
            rgt = pltpu.roll(p[:, CC:], (SEG0 - SEG * q) % CC, 1)
            v = jnp.where(wide < SEG, lft, jnp.where(wide >= SEG0, rgt, 0.0))
            at = 0 if y < CR // 2 else CC
            v = jnp.maximum(part[y % (CR // 2), :, at : at + CC] + v, 0.0)
            acc[pl.ds(y, C, stride=CR), :] = v
    out[...] = acc[...].astype(bf16)


def swap(x, axis, shifted):
    size = lax.axis_size(axis)
    if shifted:
        pairs = [(i, (i - 1 if i % 2 == 0 else i + 1) % size) for i in range(size)]
    else:
        pairs = [(i, i ^ 1) for i in range(size)]
    return lax.ppermute(x, axis, pairs)


def cost(flops, bytes_accessed):
    return pl.CostEstimate(flops=flops, bytes_accessed=bytes_accessed, transcendentals=0)


def call(kernel, outs, specs, scratch, estimate):
    vmem = pl.BlockSpec(memory_space=pltpu.VMEM)
    return pl.pallas_call(
        kernel,
        out_shape=[jax.ShapeDtypeStruct(*out) for out in outs],
        in_specs=specs,
        out_specs=[vmem] * len(outs),
        scratch_shapes=scratch,
        cost_estimate=estimate,
        compiler_params=pltpu.CompilerParams(vmem_limit_bytes=VMEM_LIMIT),
    )


def body(current_frame, history_frames, offsets, compress_weight, mixer_weight, mixer_bias):
    smem = pl.BlockSpec(memory_space=pltpu.SMEM)
    vmem = pl.BlockSpec(memory_space=pltpu.VMEM)
    hbm = pl.BlockSpec(memory_space=pltpu.HBM)
    off = offsets.T
    hist = history_frames.reshape(FRAMES, C * CR, CC)
    cur = current_frame.reshape(C * CR, CC)
    wt = mixer_weight.transpose(0, 1, 3, 2)
    nrows, ncols = lax.axis_size("rows"), lax.axis_size("cols")
    row_send = (2 * REACH + C // CP, CP, CC)
    col_send = (2 * TILES + 1, CP, CC)
    red, send_a, send_b = call(
        compress_kernel,
        [((FRAMES, CR, CP, CC), bf16), (row_send, bf16), (row_send, bf16)],
        [hbm] * 4,
        [
            pltpu.SMEM((2, FRAMES), jnp.int32),
            pltpu.VMEM((CP, C), bf16),
            pltpu.VMEM((FRAMES, C * CR, CC), bf16),
            pltpu.VMEM((C * CR, CC), bf16),
            pltpu.VMEM((FRAMES, C * CR, CC), f32),
            pltpu.SemaphoreType.DMA((FRAMES + 3,)),
        ],
        cost(2 * FRAMES * CP * C * CR * CC, 3 << 20),
    )(*[pltpu.with_memory_space_constraint(v, pltpu.HBM) for v in (off, hist, cur, compress_weight)])
    recv_a = swap(send_a, "rows", False)
    recv_b = swap(send_b, "rows", True)
    cur_t, cols, wall, wedge = call(
        prepare_kernel,
        [((CR, C, CC), bf16), ((2, C, CC), bf16), ((C, KALL), bf16), ((C, KEDGE), bf16)],
        [vmem, vmem],
        [pltpu.VMEM((C * CR, CC), f32)],
        cost(1 << 20, 3 << 20),
    )(cur, wt)
    halo_rows = pltpu.VMEM((FRAMES, CR + 2 * REACH, CP, CC), bf16)
    csend_a, csend_b = call(
        lambda *refs: pack_kernel(nrows, *refs),
        [(col_send, bf16), (col_send, bf16)],
        [smem] + [vmem] * 4,
        [halo_rows],
        cost(1 << 20, 2 << 20),
    )(off, red, recv_a, recv_b, cols)
    crecv_a = swap(csend_a, "cols", False)
    crecv_b = swap(csend_b, "cols", True)
    (part,) = call(
        lambda *refs: local_kernel(nrows, ncols, *refs),
        [((CR // 2, C, 2 * CC), f32)],
        [smem] + [vmem] * 6,
        [halo_rows, pltpu.VMEM(((WIN - CR // 2) * KROW + KALL - 3 * KROW, 2 * CC), bf16)],
        cost(2 * C * KALL * CR * CC, 4 << 20),
    )(off, red, recv_a, recv_b, cur_t, wall, mixer_bias.reshape(C, 1))
    (out,) = call(
        lambda *refs: finish_kernel(ncols, *refs),
        [((C * CR, CC), bf16)],
        [smem] + [vmem] * 4,
        [
            pltpu.VMEM(((TILES + 2) * EROW + KEDGE - 3 * EROW, 2 * CC), bf16),
            pltpu.VMEM((C * CR, CC), f32),
        ],
        cost(1 << 20, 2 << 20),
    )(off, crecv_a, crecv_b, part, wedge)
    return out.reshape(C, CR, CC)


def solution(mesh):
    in_specs = (P(None, "rows", "cols"), P(None, None, "rows", "cols"), P(), P(), P(), P())
    out_specs = P(None, "rows", "cols")
    return jax.shard_map(body, mesh=mesh, in_specs=in_specs, out_specs=out_specs, check_vma=False)
```

time: 27.3 us -> 25.9 us (0.949)
  waiting for transfers between devices: 8.18 us -> 5.7 us
  Pallas kernels: 8.37 us -> 9.47 us
    ppermute x4, waiting for transfers between devices: 8.18 us -> 5.7 us  [swap(): return lax.ppermute(x, axis, pairs)]
    pallas_call x4 -> x5, Pallas kernels: 8.37 us -> 9.47 us  [the longest x1 2.82 us: body(): call(compress_kernel, [((FRAMES, CR, CP, CC), bf16), (row_send, bf16), (r...]
  transfers between devices with their start and end apart: 4 -> 4, of which waited for: 3 -> 2; matrix products, arithmetic and copies ran while one was open for 0% -> 0% of each run, Pallas kernels for 3% -> 12%
where the time goes in v3:
time: 25.9 us
  starting transfers between devices  10.5 us (41%)
  Pallas kernels  9.47 us (37%)
  waiting for transfers between devices  5.7 us (22%)
    ppermute x4, starting transfers between devices, swap(): return lax.ppermute(x, axis, pairs)  10.5 us
    ppermute x4, waiting for transfers between devices, swap(): return lax.ppermute(x, axis, pairs)  5.7 us
    pallas_call x1, Pallas kernels, body(): call(compress_kernel, [((FRAMES, CR, CP, CC), bf16), (row_send, bf16), (r...  2.82 us
    pallas_call x1, Pallas kernels, body(): call(lambda *refs: finish_kernel(ncols, *refs), [((C * CR, CC), bf16)], [...  2.5 us
    pallas_call x1, Pallas kernels, body(): call(lambda *refs: local_kernel(nrows, ncols, *refs), [((CR // 2, C, 2 *...  2.33 us
    pallas_call x1, Pallas kernels, body(): call(lambda *refs: pack_kernel(nrows, *refs), [(col_send, bf16), (col_sen...  0.94 us
    pallas_call x1, Pallas kernels, body(): call(prepare_kernel, [((CR, C, CC), bf16), ((2, C, CC), bf16), ((C, KALL)...  0.9 us
  transfers between devices with their start and end apart: 4, of which 2 were waited for; matrix products, arithmetic and copies ran while one was open for 0% of the time, Pallas kernels for 12%

profile of v3, /device:TPU:16, one launch (start us, length us, event | category | flops | bytes accessed | tf_op | source)
XLA Modules:
  0.0 25.9 jit_solution(8667971614015190807)
XLA Ops:
  0.0 0.0 copy-start
  0.0 0.0 copy-start.3
  0.0 0.0 copy-start.1
  0.0 0.0 copy-start.2
  0.0 2.8 %shard_map.64 = (bf16[3,16,32,128]{3,2,1,0:T(8,128)(2,1)S(1)}, bf16[22,32,128]{2,1,0:T(8,128)(2,1)S(1)}, bf16[22,32,128]{2,1,0:T(8,128)(2,1)S(1)}) custom-call(s32[2,3]{1,0:T(2,128)} %bitcast.9, bf16[3,2048,128]{2,1,0:T(8,128)(2,1)} %bitcast.13, bf16[2048,128]{1,0:T(8,128)(2,1)} %bitcast.6, bf16[32,128]{1,0:T(8,128)(2,1)} %w_hbm.1), custom_call_target="tpu_custom_call" | custom-call | flops 50331648 | bytes 3145728 | tf_op jit(solution)/shard_map/pallas_call | solution.py:341
  2.8 0.1 collective-permute-start
  2.9 6.9 %collective-permute-start.1 = (bf16[22,32,128]{2,1,0:T(8,128)(2,1)S(1)}, bf16[22,32,128]{2,1,0:T(8,128)(2,1)S(1)}, u32[]{:S(2)}, u32[]{:S(2)}) collective-permute-start(bf16[22,32,128]{2,1,0:T(8,128)(2,1)S(1)} %get-tuple-element.16), channel_id=1, source_target_pairs={{0,248},{8,16},{16,8},{24,32},{32,24},{40,48},{48,40},{56,64},{64,... | collective-permute-start | bytes 540680 | tf_op jit(solution)/shard_map/ppermute | solution.py:310
  9.8 0.0 copy-done.3
  9.8 0.1 copy.7.refs_6_
  9.9 0.0 copy-done
  9.9 0.0 copy-done.1
  10.0 0.9 %shard_map.65 = (bf16[16,128,128]{2,1,0:T(8,128)(2,1)S(1)}, bf16[2,128,128]{2,1,0:T(8,128)(2,1)S(1)}, bf16[128,2048]{1,0:T(8,128)(2,1)S(1)}, bf16[128,1664]{1,0:T(8,128)(2,1)S(1)}) custom-call(bf16[2048,128]{1,0:T(8,128)(2,1)S(1)} %bitcast.7, bf16[3,3,224,128]{3,2,1,0:T(8,128)(2,1)S(1)} %bitcast.8), custom_call_target="tpu_custom_call" | custom-call | flops 1048576 | bytes 3145728 | tf_op jit(solution)/shard_map/pallas_call | solution.py:357
  10.9 0.0 collective-permute-done.refs_2_
  10.9 2.1 %collective-permute-done.1.refs_3_ = bf16[22,32,128]{2,1,0:T(8,128)(2,1)S(1)} collective-permute-done((bf16[22,32,128]{2,1,0:T(8,128)(2,1)S(1)}, bf16[22,32,128]{2,1,0:T(8,128)(2,1)S(1)}, u32[]{:S(2)}, u32[]{:S(2)}) %collective-permute-start.1) | collective-permute-done | bytes 180256 | tf_op jit(solution)/shard_map/ppermute | solution.py:310
  13.0 0.0 copy-done.2
  13.0 0.9 %shard_map.66 = (bf16[7,32,128]{2,1,0:T(8,128)(2,1)S(1)}, bf16[7,32,128]{2,1,0:T(8,128)(2,1)S(1)}) custom-call(s32[2,3]{1,0:T(2,128)S(1)} %bitcast.10, bf16[3,16,32,128]{3,2,1,0:T(8,128)(2,1)S(1)} %get-tuple-element.14.refs_1_, bf16[22,32,128]{2,1,0:T(8,128)(2,1)S(1)} %collective-permute-done.refs_2_, ...), custom_call_target="tpu_custom_call" | custom-call | flops 1048576 | bytes 2097152 | tf_op jit(solution)/shard_map/pallas_call | solution.py:365
  14.0 2.8 %collective-permute-start.2 = (bf16[7,32,128]{2,1,0:T(8,128)(2,1)S(1)}, bf16[7,32,128]{2,1,0:T(8,128)(2,1)S(1)}, u32[]{:S(2)}, u32[]{:S(2)}) collective-permute-start(bf16[7,32,128]{2,1,0:T(8,128)(2,1)S(1)} %get-tuple-element.18), channel_id=1, source_target_pairs={{0,1},{1,0},{2,3},{3,2},{4,5},{5,4},{6,7},{7,6},{8,9},{9,8},{10,11... | collective-permute-start | bytes 172040 | tf_op jit(solution)/shard_map/ppermute | solution.py:310
  16.8 0.7 %collective-permute-start.3 = (bf16[7,32,128]{2,1,0:T(8,128)(2,1)S(1)}, bf16[7,32,128]{2,1,0:T(8,128)(2,1)S(1)}, u32[]{:S(2)}, u32[]{:S(2)}) collective-permute-start(bf16[7,32,128]{2,1,0:T(8,128)(2,1)S(1)} %get-tuple-element.19), channel_id=1, source_target_pairs={{0,7},{1,2},{2,1},{3,4},{4,3},{5,6},{6,5},{7,0},{8,15},{9,10},{10,... | collective-permute-start | bytes 172040 | tf_op jit(solution)/shard_map/ppermute | solution.py:310
  17.5 2.3 %shard_map.67.refs_3_ = f32[8,128,256]{2,1,0:T(8,128)S(1)} custom-call(s32[2,3]{1,0:T(2,128)S(1)} %bitcast.11, bf16[3,16,32,128]{3,2,1,0:T(8,128)(2,1)S(1)} %get-tuple-element.14.refs_1_, bf16[22,32,128]{2,1,0:T(8,128)(2,1)S(1)} %collective-permute-done.refs_2_, bf16[22,32,128]{2,1,0:T(8,128)(2,1)S(1)} %collective-permute-done.1.refs_3_, ...), custom_call_target="tpu_custom_call" | custom-call | flops 1073741824 | bytes 4194304 | tf_op jit(solution)/shard_map/pallas_call | solution.py:374
  19.8 0.0 collective-permute-done.2.refs_1_
  19.8 3.6 %collective-permute-done.3.refs_2_ = bf16[7,32,128]{2,1,0:T(8,128)(2,1)S(1)} collective-permute-done((bf16[7,32,128]{2,1,0:T(8,128)(2,1)S(1)}, bf16[7,32,128]{2,1,0:T(8,128)(2,1)S(1)}, u32[]{:S(2)}, u32[]{:S(2)}) %collective-permute-start.3) | collective-permute-done | bytes 57376 | tf_op jit(solution)/shard_map/ppermute | solution.py:310
  23.4 2.5 %shard_map.68 = bf16[2048,128]{1,0:T(8,128)(2,1)} custom-call(s32[2,3]{1,0:T(2,128)S(1)} %bitcast.12, bf16[7,32,128]{2,1,0:T(8,128)(2,1)S(1)} %collective-permute-done.2.refs_1_, bf16[7,32,128]{2,1,0:T(8,128)(2,1)S(1)} %collective-permute-done.3.refs_2_, f32[8,128,256]{2,1,0:T(8,128)S(1)} %shard_map.67.refs_3_, bf16[128,1664]{1,0:T(8,128)(2,1)S(1)} %get-tuple-element.22.refs_4_), custom_call_target="tpu_custom_call" | custom-call | flops 1048576 | bytes 2097152 | tf_op jit(solution)/shard_map/pallas_call | solution.py:381
Async XLA Ops:
  0.0 9.9 %copy-start = (bf16[128,16,128]{2,1,0:T(8,128)(2,1)S(1)}, bf16[128,16,128]{2,1,0:T(8,128)(2,1)}, u32[]{:S(2)}) copy-start(bf16[128,16,128]{2,1,0:T(8,128)(2,1)} %param.6) | copy-start | bytes 1572868
  0.0 9.8 %copy-start.3 = (f32[128]{0:T(128)S(1)}, f32[128]{0:T(128)}, u32[]{:S(2)}) copy-start(f32[128]{0:T(128)} %param.11) | copy-start | bytes 1540
  0.0 9.9 %copy-start.1 = (bf16[3,3,128,224]{2,3,1,0:T(8,128)(2,1)S(1)}, bf16[3,3,128,224]{2,3,1,0:T(8,128)(2,1)}, u32[]{:S(2)}) copy-start(bf16[3,3,128,224]{2,3,1,0:T(8,128)(2,1)} %param.10) | copy-start | bytes 1548292
  0.0 13.0 %copy-start.2 = (s32[3,2]{0,1:T(2,128)S(1)}, s32[3,2]{0,1:T(2,128)}, u32[]{:S(2)}) copy-start(s32[3,2]{0,1:T(2,128)} %param.8) | copy-start | bytes 76
  2.8 8.0 %collective-permute-start = (bf16[22,32,128]{2,1,0:T(8,128)(2,1)S(1)}, bf16[22,32,128]{2,1,0:T(8,128)(2,1)S(1)}, u32[]{:S(2)}, u32[]{:S(2)}) collective-permute-start(bf16[22,32,128]{2,1,0:T(8,128)(2,1)S(1)} %get-tuple-element.15), channel_id=1, source_target_pairs={{0,8},{8,0},{16,24},{24,16},{32,40},{40,32},{48,56},{56,48},{64,72... | collective-permute-start | bytes 540680 | tf_op jit(solution)/shard_map/ppermute | solution.py:310
  2.9 10.1 %collective-permute-start.1 = (bf16[22,32,128]{2,1,0:T(8,128)(2,1)S(1)}, bf16[22,32,128]{2,1,0:T(8,128)(2,1)S(1)}, u32[]{:S(2)}, u32[]{:S(2)}) collective-permute-start(bf16[22,32,128]{2,1,0:T(8,128)(2,1)S(1)} %get-tuple-element.16), channel_id=1, source_target_pairs={{0,248},{8,16},{16,8},{24,32},{32,24},{40,48},{48,40},{56,64},{64,... | collective-permute-start | bytes 540680 | tf_op jit(solution)/shard_map/ppermute | solution.py:310
  14.0 5.8 %collective-permute-start.2 = (bf16[7,32,128]{2,1,0:T(8,128)(2,1)S(1)}, bf16[7,32,128]{2,1,0:T(8,128)(2,1)S(1)}, u32[]{:S(2)}, u32[]{:S(2)}) collective-permute-start(bf16[7,32,128]{2,1,0:T(8,128)(2,1)S(1)} %get-tuple-element.18), channel_id=1, source_target_pairs={{0,1},{1,0},{2,3},{3,2},{4,5},{5,4},{6,7},{7,6},{8,9},{9,8},{10,11... | collective-permute-start | bytes 172040 | tf_op jit(solution)/shard_map/ppermute | solution.py:310
  16.8 6.6 %collective-permute-start.3 = (bf16[7,32,128]{2,1,0:T(8,128)(2,1)S(1)}, bf16[7,32,128]{2,1,0:T(8,128)(2,1)S(1)}, u32[]{:S(2)}, u32[]{:S(2)}) collective-permute-start(bf16[7,32,128]{2,1,0:T(8,128)(2,1)S(1)} %get-tuple-element.19), channel_id=1, source_target_pairs={{0,7},{1,2},{2,1},{3,4},{4,3},{5,6},{6,5},{7,0},{8,15},{9,10},{10,... | collective-permute-start | bytes 172040 | tf_op jit(solution)/shard_map/ppermute | solution.py:310

commit v4 on v3

--- a/solution.py
+++ b/solution.py
@@ -27,7 +27,7 @@
 
 
 def slots(off, axis):
-    pos = [off[axis, k] > 0 for k in range(FRAMES)]
+    pos = [off[axis][k] > 0 for k in range(FRAMES)]
     first_pos = jnp.where(pos[0], 0, jnp.where(pos[1], 1, 2))
     last_pos = jnp.where(pos[2], 2, jnp.where(pos[1], 1, 0))
     first_neg = jnp.where(pos[0], jnp.where(pos[1], 2, 1), 0)
@@ -37,6 +37,14 @@
         for k in range(FRAMES)
     ]
     return pos, (first_pos, last_pos), (first_neg, last_neg), place
+
+
+def scalars(ref):
+    return [[ref[axis, k] for k in range(FRAMES)] for axis in range(2)]
+
+
+def pick(values, k):
+    return jnp.where(k == 0, values[0], jnp.where(k == 1, values[1], values[2]))
 
 
 def lanes(shape):
@@ -71,7 +79,7 @@
     top = fbuf[0, pl.ds(0, C, stride=CR), :].astype(bf16).reshape(C // CP, CP, CC)
     bottom = fbuf[0, pl.ds(CR - 1, C, stride=CR), :].astype(bf16).reshape(C // CP, CP, CC)
     small[1].wait()
-    _, posf, negf, _ = slots(off, 0)
+    _, posf, negf, _ = slots(scalars(off), 0)
     for send, down in ((send_a, even), (send_b, jnp.logical_not(even))):
         start = jnp.where(down, CR - REACH, 0)
         for s in range(2):
@@ -141,8 +149,8 @@
     return above, below, has_above, has_below
 
 
-def window_row(off, cb, k, r, has_above, has_below):
-    v = cb[k, SHIFT_Y - off[0, k] + r]
+def window_row(dy, cb, k, r, has_above, has_below):
+    v = cb[k, SHIFT_Y - dy + r]
     if r == 0:
         v = jnp.where(has_above, v, jnp.zeros_like(v))
     if r == WIN - 1:
@@ -151,6 +159,7 @@
 
 
 def pack_kernel(nrows, off, red, recv_a, recv_b, cols, send_a, send_b, cb):
+    off = scalars(off)
     above, below, has_above, has_below = row_halo(nrows, off, red, recv_a, recv_b, cb)
     above = above.astype(f32)
     below = below.astype(f32)
@@ -168,10 +177,11 @@
         back = jnp.where(right, SEG0, 0)
         for s in range(2):
             k = jnp.where(right, posf[s], negf[s])
+            dy = pick(off[0], k)
             for t in range(TILES):
                 total = jnp.zeros((CP, CC), f32)
                 for q in range(WIN // TILES):
-                    piece = window_row(off, cb, k, t + TILES * q, has_above, has_below)
+                    piece = window_row(dy, cb, k, t + TILES * q, has_above, has_below)
                     piece = pltpu.roll(piece.astype(f32), (SEG * q - back + CC) % CC, 1)
                     total = piece if q == 0 else jnp.where(lane >= SEG * q, piece, total)
                 send[s * TILES + t] = total.astype(bf16)
@@ -184,6 +194,7 @@
 
 
 def local_kernel(nrows, ncols, off, red, recv_a, recv_b, cur_t, wall, bias, part, cb, x2):
+    off = scalars(off)
     above, below, has_above, has_below = row_halo(nrows, off, red, recv_a, recv_b, cb)
     col = lax.axis_index("cols")
     has_left = col > 0
@@ -202,7 +213,7 @@
     taps = []
     for k in range(FRAMES):
         for j in range(3):
-            s = off[1, k] + 1 - j
+            s = off[1][k] + 1 - j
             lo = jnp.where(pos[k], s, 0)
             hi = jnp.where(pos[k], CC, CC + s)
             if j == 0:
@@ -218,7 +229,7 @@
         put(r, 0, C, jnp.where(wide == 0, zero, pltpu.roll(here, 1, 1)).astype(bf16))
         put(r, 2 * C, C, jnp.where(wide == CC - 1, zero, pltpu.roll(here, CC - 1, 1)).astype(bf16))
         for k in range(FRAMES):
-            own = window_row(off, cb, k, r, has_above, has_below).astype(f32)
+            own = window_row(off[0][k], cb, k, r, has_above, has_below).astype(f32)
             for j in range(3):
                 s, mask = taps[3 * k + j]
                 v = jnp.where(mask, pltpu.roll(own, s, 1), jnp.zeros_like(own))
@@ -233,6 +244,7 @@
 
 
 def finish_kernel(ncols, off, recv_a, recv_b, part, wedge, out, xx, acc):
+    off = scalars(off)
     col = lax.axis_index("cols")
     ceven = col % 2 == 0
     has_left = col > 0
@@ -256,7 +268,7 @@
             tiles.append(jnp.where(ok, v, zero).astype(f32))
         masks = []
         for j in range(3):
-            s = off[1, k] + 1 - j
+            s = off[1][k] + 1 - j
             lo = jnp.where(pos[k], 0, SEG + s)
             hi = jnp.where(pos[k], s, SEG)
             mask = (inner >= lo) & (inner < hi)
@@ -328,7 +340,6 @@
 
 
 def body(current_frame, history_frames, offsets, compress_weight, mixer_weight, mixer_bias):
-    smem = pl.BlockSpec(memory_space=pltpu.SMEM)
     vmem = pl.BlockSpec(memory_space=pltpu.VMEM)
     hbm = pl.BlockSpec(memory_space=pltpu.HBM)
     off = offsets.T
@@ -365,7 +376,7 @@
     csend_a, csend_b = call(
         lambda *refs: pack_kernel(nrows, *refs),
         [(col_send, bf16), (col_send, bf16)],
-        [smem] + [vmem] * 4,
+        [vmem] * 5,
         [halo_rows],
         cost(1 << 20, 2 << 20),
     )(off, red, recv_a, recv_b, cols)
@@ -374,14 +385,14 @@
     (part,) = call(
         lambda *refs: local_kernel(nrows, ncols, *refs),
         [((CR // 2, C, 2 * CC), f32)],
-        [smem] + [vmem] * 6,
+        [vmem] * 7,
         [halo_rows, pltpu.VMEM(((WIN - CR // 2) * KROW + KALL - 3 * KROW, 2 * CC), bf16)],
         cost(2 * C * KALL * CR * CC, 4 << 20),
     )(off, red, recv_a, recv_b, cur_t, wall, mixer_bias.reshape(C, 1))
     (out,) = call(
         lambda *refs: finish_kernel(ncols, *refs),
         [((C * CR, CC), bf16)],
-        [smem] + [vmem] * 4,
+        [vmem] * 5,
         [
             pltpu.VMEM(((TILES + 2) * EROW + KEDGE - 3 * EROW, 2 * CC), bf16),
             pltpu.VMEM((C * CR, CC), f32),

time: 25.9 us -> 25 us (0.965)
  Pallas kernels: 9.47 us -> 7.9 us
  waiting for transfers between devices: 5.7 us -> 6.33 us
    ppermute x4, waiting for transfers between devices: 5.7 us -> 6.33 us  [swap(): return lax.ppermute(x, axis, pairs)]
    pallas_call x1, Pallas kernels: 2.33 us -> 1.76 us  [body(): call(lambda *refs: local_kernel(nrows, ncols, *refs), [((CR // 2, C, 2 *...]
    pallas_call x1, Pallas kernels: 2.5 us -> 1.97 us  [body(): call(lambda *refs: finish_kernel(ncols, *refs), [((C * CR, CC), bf16)], [...]
    pallas_call x1, Pallas kernels: 0.94 us -> 0.45 us  [body(): call(lambda *refs: pack_kernel(nrows, *refs), [(col_send, bf16), (col_sen...]
  transfers between devices with their start and end apart: 4 -> 4, of which waited for: 2 -> 3; matrix products, arithmetic and copies ran while one was open for 0% -> 0% of each run, Pallas kernels for 12% -> 11%
where the time goes in v4:
time: 25 us; the launch traced here: 24.9 us
  starting transfers between devices  10.5 us (42%)
  Pallas kernels  7.9 us (32%)
  waiting for transfers between devices  6.33 us (25%)
    ppermute x4, starting transfers between devices, swap(): return lax.ppermute(x, axis, pairs)  10.5 us
    ppermute x4, waiting for transfers between devices, swap(): return lax.ppermute(x, axis, pairs)  6.33 us
    pallas_call x1, Pallas kernels, body(): call(compress_kernel, [((FRAMES, CR, CP, CC), bf16), (row_send, bf16), (r...  2.82 us
    pallas_call x1, Pallas kernels, body(): call(lambda *refs: finish_kernel(ncols, *refs), [((C * CR, CC), bf16)], [...  1.97 us
    pallas_call x1, Pallas kernels, body(): call(lambda *refs: local_kernel(nrows, ncols, *refs), [((CR // 2, C, 2 *...  1.76 us
    pallas_call x1, Pallas kernels, body(): call(prepare_kernel, [((CR, C, CC), bf16), ((2, C, CC), bf16), ((C, KALL)...  0.9 us
  transfers between devices with their start and end apart: 4, of which 3 were waited for; matrix products, arithmetic and copies ran while one was open for 0% of the time, Pallas kernels for 11%

profile of v4, /device:TPU:16, one launch (start us, length us, event | category | flops | bytes accessed | tf_op | source)
XLA Modules:
  0.0 24.9 jit_solution(13258159712596293973)
XLA Ops:
  0.0 0.0 copy-start
  0.0 0.0 copy-start.3
  0.0 0.0 copy-start.1
  0.0 0.0 copy-start.2
  0.0 2.8 %shard_map.64 = (bf16[3,16,32,128]{3,2,1,0:T(8,128)(2,1)S(1)}, bf16[22,32,128]{2,1,0:T(8,128)(2,1)S(1)}, bf16[22,32,128]{2,1,0:T(8,128)(2,1)S(1)}) custom-call(s32[2,3]{1,0:T(2,128)} %bitcast.9, bf16[3,2048,128]{2,1,0:T(8,128)(2,1)} %bitcast.13, bf16[2048,128]{1,0:T(8,128)(2,1)} %bitcast.6, bf16[32,128]{1,0:T(8,128)(2,1)} %w_hbm.1), custom_call_target="tpu_custom_call" | custom-call | flops 50331648 | bytes 3145728 | tf_op jit(solution)/shard_map/pallas_call | solution.py:352
  2.8 0.1 collective-permute-start
  2.9 6.9 %collective-permute-start.1 = (bf16[22,32,128]{2,1,0:T(8,128)(2,1)S(1)}, bf16[22,32,128]{2,1,0:T(8,128)(2,1)S(1)}, u32[]{:S(2)}, u32[]{:S(2)}) collective-permute-start(bf16[22,32,128]{2,1,0:T(8,128)(2,1)S(1)} %get-tuple-element.16), channel_id=1, source_target_pairs={{0,248},{8,16},{16,8},{24,32},{32,24},{40,48},{48,40},{56,64},{64,... | collective-permute-start | bytes 540680 | tf_op jit(solution)/shard_map/ppermute | solution.py:322
  9.8 0.0 copy-done.3
  9.8 0.1 copy.7.refs_6_
  9.9 0.0 copy-done
  9.9 0.0 copy-done.1
  10.0 0.9 %shard_map.65 = (bf16[16,128,128]{2,1,0:T(8,128)(2,1)S(1)}, bf16[2,128,128]{2,1,0:T(8,128)(2,1)S(1)}, bf16[128,2048]{1,0:T(8,128)(2,1)S(1)}, bf16[128,1664]{1,0:T(8,128)(2,1)S(1)}) custom-call(bf16[2048,128]{1,0:T(8,128)(2,1)S(1)} %bitcast.7, bf16[3,3,224,128]{3,2,1,0:T(8,128)(2,1)S(1)} %bitcast.8), custom_call_target="tpu_custom_call" | custom-call | flops 1048576 | bytes 3145728 | tf_op jit(solution)/shard_map/pallas_call | solution.py:368
  10.9 0.0 collective-permute-done.refs_2_
  10.9 2.1 %collective-permute-done.1.refs_3_ = bf16[22,32,128]{2,1,0:T(8,128)(2,1)S(1)} collective-permute-done((bf16[22,32,128]{2,1,0:T(8,128)(2,1)S(1)}, bf16[22,32,128]{2,1,0:T(8,128)(2,1)S(1)}, u32[]{:S(2)}, u32[]{:S(2)}) %collective-permute-start.1) | collective-permute-done | bytes 180256 | tf_op jit(solution)/shard_map/ppermute | solution.py:322
  13.0 0.0 copy-done.2
  13.0 0.5 %shard_map.66 = (bf16[7,32,128]{2,1,0:T(8,128)(2,1)S(1)}, bf16[7,32,128]{2,1,0:T(8,128)(2,1)S(1)}) custom-call(s32[2,3]{1,0:T(2,128)S(1)} %bitcast.10, bf16[3,16,32,128]{3,2,1,0:T(8,128)(2,1)S(1)} %get-tuple-element.14.refs_1_, bf16[22,32,128]{2,1,0:T(8,128)(2,1)S(1)} %collective-permute-done.refs_2_, ...), custom_call_target="tpu_custom_call" | custom-call | flops 1048576 | bytes 2097152 | tf_op jit(solution)/shard_map/pallas_call | solution.py:376
  13.5 2.9 %collective-permute-start.2 = (bf16[7,32,128]{2,1,0:T(8,128)(2,1)S(1)}, bf16[7,32,128]{2,1,0:T(8,128)(2,1)S(1)}, u32[]{:S(2)}, u32[]{:S(2)}) collective-permute-start(bf16[7,32,128]{2,1,0:T(8,128)(2,1)S(1)} %get-tuple-element.18), channel_id=1, source_target_pairs={{0,1},{1,0},{2,3},{3,2},{4,5},{5,4},{6,7},{7,6},{8,9},{9,8},{10,11... | collective-permute-start | bytes 172040 | tf_op jit(solution)/shard_map/ppermute | solution.py:322
  16.4 0.6 %collective-permute-start.3 = (bf16[7,32,128]{2,1,0:T(8,128)(2,1)S(1)}, bf16[7,32,128]{2,1,0:T(8,128)(2,1)S(1)}, u32[]{:S(2)}, u32[]{:S(2)}) collective-permute-start(bf16[7,32,128]{2,1,0:T(8,128)(2,1)S(1)} %get-tuple-element.19), channel_id=1, source_target_pairs={{0,7},{1,2},{2,1},{3,4},{4,3},{5,6},{6,5},{7,0},{8,15},{9,10},{10,... | collective-permute-start | bytes 172040 | tf_op jit(solution)/shard_map/ppermute | solution.py:322
  17.0 1.8 %shard_map.67.refs_3_ = f32[8,128,256]{2,1,0:T(8,128)S(1)} custom-call(s32[2,3]{1,0:T(2,128)S(1)} %bitcast.11, bf16[3,16,32,128]{3,2,1,0:T(8,128)(2,1)S(1)} %get-tuple-element.14.refs_1_, bf16[22,32,128]{2,1,0:T(8,128)(2,1)S(1)} %collective-permute-done.refs_2_, bf16[22,32,128]{2,1,0:T(8,128)(2,1)S(1)} %collective-permute-done.1.refs_3_, ...), custom_call_target="tpu_custom_call" | custom-call | flops 1073741824 | bytes 4194304 | tf_op jit(solution)/shard_map/pallas_call | solution.py:385
  18.7 0.5 %collective-permute-done.2.refs_1_ = bf16[7,32,128]{2,1,0:T(8,128)(2,1)S(1)} collective-permute-done((bf16[7,32,128]{2,1,0:T(8,128)(2,1)S(1)}, bf16[7,32,128]{2,1,0:T(8,128)(2,1)S(1)}, u32[]{:S(2)}, u32[]{:S(2)}) %collective-permute-start.2) | collective-permute-done | bytes 57376 | tf_op jit(solution)/shard_map/ppermute | solution.py:322
  19.2 3.7 %collective-permute-done.3.refs_2_ = bf16[7,32,128]{2,1,0:T(8,128)(2,1)S(1)} collective-permute-done((bf16[7,32,128]{2,1,0:T(8,128)(2,1)S(1)}, bf16[7,32,128]{2,1,0:T(8,128)(2,1)S(1)}, u32[]{:S(2)}, u32[]{:S(2)}) %collective-permute-start.3) | collective-permute-done | bytes 57376 | tf_op jit(solution)/shard_map/ppermute | solution.py:322
  22.9 2.0 %shard_map.68 = bf16[2048,128]{1,0:T(8,128)(2,1)} custom-call(s32[2,3]{1,0:T(2,128)S(1)} %bitcast.12, bf16[7,32,128]{2,1,0:T(8,128)(2,1)S(1)} %collective-permute-done.2.refs_1_, bf16[7,32,128]{2,1,0:T(8,128)(2,1)S(1)} %collective-permute-done.3.refs_2_, f32[8,128,256]{2,1,0:T(8,128)S(1)} %shard_map.67.refs_3_, bf16[128,1664]{1,0:T(8,128)(2,1)S(1)} %get-tuple-element.22.refs_4_), custom_call_target="tpu_custom_call" | custom-call | flops 1048576 | bytes 2097152 | tf_op jit(solution)/shard_map/pallas_call | solution.py:392
Async XLA Ops:
  0.0 9.9 %copy-start = (bf16[128,16,128]{2,1,0:T(8,128)(2,1)S(1)}, bf16[128,16,128]{2,1,0:T(8,128)(2,1)}, u32[]{:S(2)}) copy-start(bf16[128,16,128]{2,1,0:T(8,128)(2,1)} %param.6) | copy-start | bytes 1572868
  0.0 9.8 %copy-start.3 = (f32[128]{0:T(128)S(1)}, f32[128]{0:T(128)}, u32[]{:S(2)}) copy-start(f32[128]{0:T(128)} %param.11) | copy-start | bytes 1540
  0.0 9.9 %copy-start.1 = (bf16[3,3,128,224]{2,3,1,0:T(8,128)(2,1)S(1)}, bf16[3,3,128,224]{2,3,1,0:T(8,128)(2,1)}, u32[]{:S(2)}) copy-start(bf16[3,3,128,224]{2,3,1,0:T(8,128)(2,1)} %param.10) | copy-start | bytes 1548292
  0.0 13.0 %copy-start.2 = (s32[3,2]{0,1:T(2,128)S(1)}, s32[3,2]{0,1:T(2,128)}, u32[]{:S(2)}) copy-start(s32[3,2]{0,1:T(2,128)} %param.8) | copy-start | bytes 76
  2.8 8.0 %collective-permute-start = (bf16[22,32,128]{2,1,0:T(8,128)(2,1)S(1)}, bf16[22,32,128]{2,1,0:T(8,128)(2,1)S(1)}, u32[]{:S(2)}, u32[]{:S(2)}) collective-permute-start(bf16[22,32,128]{2,1,0:T(8,128)(2,1)S(1)} %get-tuple-element.15), channel_id=1, source_target_pairs={{0,8},{8,0},{16,24},{24,16},{32,40},{40,32},{48,56},{56,48},{64,72... | collective-permute-start | bytes 540680 | tf_op jit(solution)/shard_map/ppermute | solution.py:322
  2.9 10.1 %collective-permute-start.1 = (bf16[22,32,128]{2,1,0:T(8,128)(2,1)S(1)}, bf16[22,32,128]{2,1,0:T(8,128)(2,1)S(1)}, u32[]{:S(2)}, u32[]{:S(2)}) collective-permute-start(bf16[22,32,128]{2,1,0:T(8,128)(2,1)S(1)} %get-tuple-element.16), channel_id=1, source_target_pairs={{0,248},{8,16},{16,8},{24,32},{32,24},{40,48},{48,40},{56,64},{64,... | collective-permute-start | bytes 540680 | tf_op jit(solution)/shard_map/ppermute | solution.py:322
  13.5 5.8 %collective-permute-start.2 = (bf16[7,32,128]{2,1,0:T(8,128)(2,1)S(1)}, bf16[7,32,128]{2,1,0:T(8,128)(2,1)S(1)}, u32[]{:S(2)}, u32[]{:S(2)}) collective-permute-start(bf16[7,32,128]{2,1,0:T(8,128)(2,1)S(1)} %get-tuple-element.18), channel_id=1, source_target_pairs={{0,1},{1,0},{2,3},{3,2},{4,5},{5,4},{6,7},{7,6},{8,9},{9,8},{10,11... | collective-permute-start | bytes 172040 | tf_op jit(solution)/shard_map/ppermute | solution.py:322
  16.4 6.6 %collective-permute-start.3 = (bf16[7,32,128]{2,1,0:T(8,128)(2,1)S(1)}, bf16[7,32,128]{2,1,0:T(8,128)(2,1)S(1)}, u32[]{:S(2)}, u32[]{:S(2)}) collective-permute-start(bf16[7,32,128]{2,1,0:T(8,128)(2,1)S(1)} %get-tuple-element.19), channel_id=1, source_target_pairs={{0,7},{1,2},{2,1},{3,4},{4,3},{5,6},{6,5},{7,0},{8,15},{9,10},{10,... | collective-permute-start | bytes 172040 | tf_op jit(solution)/shard_map/ppermute | solution.py:322

commit v5 on v4

--- a/solution.py
+++ b/solution.py
@@ -52,7 +52,7 @@
 
 
 def compress_kernel(
-    off_hbm, hist, cur, w_hbm, red, send_a, send_b, off, w, hbuf, cbuf, fbuf, sems
+    off_hbm, hist, cur, w_hbm, red, send_a, send_b, off, w, hbuf, cbuf, sems
 ):
     copies = [pltpu.make_async_copy(hist.at[k], hbuf.at[k], sems.at[k]) for k in range(FRAMES)]
     copies.append(pltpu.make_async_copy(cur, cbuf, sems.at[FRAMES]))
@@ -67,17 +67,15 @@
     small[0].wait()
     for k in range(FRAMES):
         copies[k].wait()
-        fbuf[k] = hbuf[k].astype(f32)
-        x = jnp.concatenate(
-            [fbuf[k, pl.ds(y, C, stride=CR), :].astype(bf16) for y in range(CR)], axis=1
-        )
+        by_row = jnp.swapaxes(hbuf[k].reshape(C, CR, CC), 0, 1)
+        x = jnp.concatenate([by_row[y] for y in range(CR)], axis=1)
         r = jnp.dot(w[...], x, preferred_element_type=f32).astype(bf16)
         for y in range(CR):
             red[k, y] = r[:, y * CC : (y + 1) * CC]
     copies[FRAMES].wait()
-    fbuf[0] = cbuf[...].astype(f32)
-    top = fbuf[0, pl.ds(0, C, stride=CR), :].astype(bf16).reshape(C // CP, CP, CC)
-    bottom = fbuf[0, pl.ds(CR - 1, C, stride=CR), :].astype(bf16).reshape(C // CP, CP, CC)
+    by_row = jnp.swapaxes(cbuf[...].reshape(C, CR, CC), 0, 1)
+    top = by_row[0].reshape(C // CP, CP, CC)
+    bottom = by_row[CR - 1].reshape(C // CP, CP, CC)
     small[1].wait()
     _, posf, negf, _ = slots(scalars(off), 0)
     for send, down in ((send_a, even), (send_b, jnp.logical_not(even))):
@@ -243,7 +241,7 @@
         part[y] = p + bias_col
 
 
-def finish_kernel(ncols, off, recv_a, recv_b, part, wedge, out, xx, acc):
+def finish_kernel(ncols, off, recv_b, recv_a, part, wedge, out, xx, acc):
     off = scalars(off)
     col = lax.axis_index("cols")
     ceven = col % 2 == 0
@@ -313,13 +311,26 @@
     out[...] = acc[...].astype(bf16)
 
 
+def partner(i, size, shifted):
+    if not shifted:
+        return i ^ 1
+    j = i - 1 if i % 2 == 0 else i + 1
+    return j if 0 <= j < size else None
+
+
 def swap(x, axis, shifted):
-    size = lax.axis_size(axis)
-    if shifted:
-        pairs = [(i, (i - 1 if i % 2 == 0 else i + 1) % size) for i in range(size)]
-    else:
-        pairs = [(i, i ^ 1) for i in range(size)]
-    return lax.ppermute(x, axis, pairs)
+    nrows, ncols = lax.axis_size("rows"), lax.axis_size("cols")
+    pairs = []
+    for r in range(nrows):
+        for c in range(ncols):
+            if axis == "rows":
+                to = partner(r, nrows, shifted)
+                to = (r, c ^ 1) if to is None else (to, c)
+            else:
+                to = partner(c, ncols, shifted)
+                to = (r ^ 1, c) if to is None else (r, to)
+            pairs.append((r * ncols + c, to[0] * ncols + to[1]))
+    return lax.ppermute(x, ("rows", "cols"), pairs)
 
 
 def cost(flops, bytes_accessed):
@@ -358,7 +369,6 @@
             pltpu.VMEM((CP, C), bf16),
             pltpu.VMEM((FRAMES, C * CR, CC), bf16),
             pltpu.VMEM((C * CR, CC), bf16),
-            pltpu.VMEM((FRAMES, C * CR, CC), f32),
             pltpu.SemaphoreType.DMA((FRAMES + 3,)),
         ],
         cost(2 * FRAMES * CP * C * CR * CC, 3 << 20),
@@ -380,8 +390,8 @@
         [halo_rows],
         cost(1 << 20, 2 << 20),
     )(off, red, recv_a, recv_b, cols)
+    crecv_b = swap(csend_b, "cols", True)
     crecv_a = swap(csend_a, "cols", False)
-    crecv_b = swap(csend_b, "cols", True)
     (part,) = call(
         lambda *refs: local_kernel(nrows, ncols, *refs),
         [((CR // 2, C, 2 * CC), f32)],
@@ -398,7 +408,7 @@
             pltpu.VMEM((C * CR, CC), f32),
         ],
         cost(1 << 20, 2 << 20),
-    )(off, crecv_a, crecv_b, part, wedge)
+    )(off, crecv_b, crecv_a, part, wedge)
     return out.reshape(C, CR, CC)
 
 

time: 25 us -> 22.5 us (0.900)
  the two profiles are of different devices: /device:TPU:16 before, /device:TPU:14 now
where the time goes in v5:
time: 22.5 us; the launch traced here: 22.2 us
  starting transfers between devices  9.82 us (44%)
  Pallas kernels  7.38 us (33%)
  waiting for transfers between devices  4.76 us (21%)
    ppermute x4, starting transfers between devices, swap(): return lax.ppermute(x, ('rows', 'cols'), pairs)  9.82 us
    ppermute x4, waiting for transfers between devices, swap(): return lax.ppermute(x, ('rows', 'cols'), pairs)  4.76 us
    pallas_call x1, Pallas kernels, body(): call(compress_kernel, [((FRAMES, CR, CP, CC), bf16), (row_send, bf16), (r...  2.3 us
    pallas_call x1, Pallas kernels, body(): call(lambda *refs: finish_kernel(ncols, *refs), [((C * CR, CC), bf16)], [...  1.97 us
    pallas_call x1, Pallas kernels, body(): call(lambda *refs: local_kernel(nrows, ncols, *refs), [((CR // 2, C, 2 *...  1.76 us
    pallas_call x1, Pallas kernels, body(): call(prepare_kernel, [((CR, C, CC), bf16), ((2, C, CC), bf16), ((C, KALL)...  0.9 us
    pallas_call x1, Pallas kernels, body(): call(lambda *refs: pack_kernel(nrows, *refs), [(col_send, bf16), (col_sen...  0.45 us
  transfers between devices with their start and end apart: 4, of which 3 were waited for; matrix products, arithmetic and copies ran while one was open for 1% of the time, Pallas kernels for 12%

profile of v5, /device:TPU:14, one launch (start us, length us, event | category | flops | bytes accessed | tf_op | source)
XLA Modules:
  0.0 22.2 jit_solution(4350690660316475729)
XLA Ops:
  0.0 0.0 copy-start
  0.0 0.0 copy-start.3
  0.0 0.0 copy-start.1
  0.0 0.0 copy-start.2
  0.0 2.3 %shard_map.64 = (bf16[3,16,32,128]{3,2,1,0:T(8,128)(2,1)S(1)}, bf16[22,32,128]{2,1,0:T(8,128)(2,1)S(1)}, bf16[22,32,128]{2,1,0:T(8,128)(2,1)S(1)}) custom-call(s32[2,3]{1,0:T(2,128)} %bitcast.9, bf16[3,2048,128]{2,1,0:T(8,128)(2,1)} %bitcast.13, bf16[2048,128]{1,0:T(8,128)(2,1)} %bitcast.6, bf16[32,128]{1,0:T(8,128)(2,1)} %w_hbm.1), custom_call_target="tpu_custom_call" | custom-call | flops 50331648 | bytes 3145728 | tf_op jit(solution)/shard_map/pallas_call | solution.py:363
  2.3 0.1 collective-permute-start
  2.4 6.2 %collective-permute-start.1 = (bf16[22,32,128]{2,1,0:T(8,128)(2,1)S(1)}, bf16[22,32,128]{2,1,0:T(8,128)(2,1)S(1)}, u32[]{:S(2)}, u32[]{:S(2)}) collective-permute-start(bf16[22,32,128]{2,1,0:T(8,128)(2,1)S(1)} %get-tuple-element.16), channel_id=1, source_target_pairs={{0,1},{1,0},{2,3},{3,2},{4,5},{5,4},{6,7},{7,6},{8,16},{9,17},{10,... | collective-permute-start | bytes 540680 | tf_op jit(solution)/shard_map/ppermute | solution.py:333
  8.6 0.0 copy-done.3
  8.7 0.1 copy.7.refs_6_
  8.8 0.0 copy-done
  8.8 0.0 copy-done.1
  8.8 0.9 %shard_map.65 = (bf16[16,128,128]{2,1,0:T(8,128)(2,1)S(1)}, bf16[2,128,128]{2,1,0:T(8,128)(2,1)S(1)}, bf16[128,2048]{1,0:T(8,128)(2,1)S(1)}, bf16[128,1664]{1,0:T(8,128)(2,1)S(1)}) custom-call(bf16[2048,128]{1,0:T(8,128)(2,1)S(1)} %bitcast.7, bf16[3,3,224,128]{3,2,1,0:T(8,128)(2,1)S(1)} %bitcast.8), custom_call_target="tpu_custom_call" | custom-call | flops 1048576 | bytes 3145728 | tf_op jit(solution)/shard_map/pallas_call | solution.py:378
  9.7 0.0 collective-permute-done.refs_2_
  9.7 2.2 %collective-permute-done.1.refs_3_ = bf16[22,32,128]{2,1,0:T(8,128)(2,1)S(1)} collective-permute-done((bf16[22,32,128]{2,1,0:T(8,128)(2,1)S(1)}, bf16[22,32,128]{2,1,0:T(8,128)(2,1)S(1)}, u32[]{:S(2)}, u32[]{:S(2)}) %collective-permute-start.1) | collective-permute-done | bytes 180256 | tf_op jit(solution)/shard_map/ppermute | solution.py:333
  11.8 0.0 copy-done.2
  11.8 0.5 %shard_map.66 = (bf16[7,32,128]{2,1,0:T(8,128)(2,1)S(1)}, bf16[7,32,128]{2,1,0:T(8,128)(2,1)S(1)}) custom-call(s32[2,3]{1,0:T(2,128)S(1)} %bitcast.10, bf16[3,16,32,128]{3,2,1,0:T(8,128)(2,1)S(1)} %get-tuple-element.14.refs_1_, bf16[22,32,128]{2,1,0:T(8,128)(2,1)S(1)} %collective-permute-done.refs_2_, ...), custom_call_target="tpu_custom_call" | custom-call | flops 1048576 | bytes 2097152 | tf_op jit(solution)/shard_map/pallas_call | solution.py:386
  12.3 2.2 %collective-permute-start.2 = (bf16[7,32,128]{2,1,0:T(8,128)(2,1)S(1)}, bf16[7,32,128]{2,1,0:T(8,128)(2,1)S(1)}, u32[]{:S(2)}, u32[]{:S(2)}) collective-permute-start(bf16[7,32,128]{2,1,0:T(8,128)(2,1)S(1)} %get-tuple-element.18), channel_id=1, source_target_pairs={{0,8},{1,2},{2,1},{3,4},{4,3},{5,6},{6,5},{7,15},{8,0},{9,10},{10,... | collective-permute-start | bytes 172040 | tf_op jit(solution)/shard_map/ppermute | solution.py:333
  14.5 1.3 %collective-permute-start.3 = (bf16[7,32,128]{2,1,0:T(8,128)(2,1)S(1)}, bf16[7,32,128]{2,1,0:T(8,128)(2,1)S(1)}, u32[]{:S(2)}, u32[]{:S(2)}) collective-permute-start(bf16[7,32,128]{2,1,0:T(8,128)(2,1)S(1)} %get-tuple-element.19), channel_id=1, source_target_pairs={{0,1},{1,0},{2,3},{3,2},{4,5},{5,4},{6,7},{7,6},{8,9},{9,8},{10,11... | collective-permute-start | bytes 172040 | tf_op jit(solution)/shard_map/ppermute | solution.py:333
  15.8 1.8 %shard_map.67.refs_3_ = f32[8,128,256]{2,1,0:T(8,128)S(1)} custom-call(s32[2,3]{1,0:T(2,128)S(1)} %bitcast.11, bf16[3,16,32,128]{3,2,1,0:T(8,128)(2,1)S(1)} %get-tuple-element.14.refs_1_, bf16[22,32,128]{2,1,0:T(8,128)(2,1)S(1)} %collective-permute-done.refs_2_, bf16[22,32,128]{2,1,0:T(8,128)(2,1)S(1)} %collective-permute-done.1.refs_3_, ...), custom_call_target="tpu_custom_call" | custom-call | flops 1073741824 | bytes 4194304 | tf_op jit(solution)/shard_map/pallas_call | solution.py:395
  17.6 1.4 %collective-permute-done.2.refs_1_ = bf16[7,32,128]{2,1,0:T(8,128)(2,1)S(1)} collective-permute-done((bf16[7,32,128]{2,1,0:T(8,128)(2,1)S(1)}, bf16[7,32,128]{2,1,0:T(8,128)(2,1)S(1)}, u32[]{:S(2)}, u32[]{:S(2)}) %collective-permute-start.2) | collective-permute-done | bytes 57376 | tf_op jit(solution)/shard_map/ppermute | solution.py:333
  19.0 1.2 %collective-permute-done.3.refs_2_ = bf16[7,32,128]{2,1,0:T(8,128)(2,1)S(1)} collective-permute-done((bf16[7,32,128]{2,1,0:T(8,128)(2,1)S(1)}, bf16[7,32,128]{2,1,0:T(8,128)(2,1)S(1)}, u32[]{:S(2)}, u32[]{:S(2)}) %collective-permute-start.3) | collective-permute-done | bytes 57376 | tf_op jit(solution)/shard_map/ppermute | solution.py:333
  20.2 2.0 %shard_map.68 = bf16[2048,128]{1,0:T(8,128)(2,1)} custom-call(s32[2,3]{1,0:T(2,128)S(1)} %bitcast.12, bf16[7,32,128]{2,1,0:T(8,128)(2,1)S(1)} %collective-permute-done.2.refs_1_, bf16[7,32,128]{2,1,0:T(8,128)(2,1)S(1)} %collective-permute-done.3.refs_2_, f32[8,128,256]{2,1,0:T(8,128)S(1)} %shard_map.67.refs_3_, bf16[128,1664]{1,0:T(8,128)(2,1)S(1)} %get-tuple-element.22.refs_4_), custom_call_target="tpu_custom_call" | custom-call | flops 1048576 | bytes 2097152 | tf_op jit(solution)/shard_map/pallas_call | solution.py:402
Async XLA Ops:
  0.0 8.8 %copy-start = (bf16[128,16,128]{2,1,0:T(8,128)(2,1)S(1)}, bf16[128,16,128]{2,1,0:T(8,128)(2,1)}, u32[]{:S(2)}) copy-start(bf16[128,16,128]{2,1,0:T(8,128)(2,1)} %param.6) | copy-start | bytes 1572868
  0.0 8.6 %copy-start.3 = (f32[128]{0:T(128)S(1)}, f32[128]{0:T(128)}, u32[]{:S(2)}) copy-start(f32[128]{0:T(128)} %param.11) | copy-start | bytes 1540
  0.0 8.8 %copy-start.1 = (bf16[3,3,128,224]{2,3,1,0:T(8,128)(2,1)S(1)}, bf16[3,3,128,224]{2,3,1,0:T(8,128)(2,1)}, u32[]{:S(2)}) copy-start(bf16[3,3,128,224]{2,3,1,0:T(8,128)(2,1)} %param.10) | copy-start | bytes 1548292
  0.0 11.8 %copy-start.2 = (s32[3,2]{0,1:T(2,128)S(1)}, s32[3,2]{0,1:T(2,128)}, u32[]{:S(2)}) copy-start(s32[3,2]{0,1:T(2,128)} %param.8) | copy-start | bytes 76
  2.3 7.4 %collective-permute-start = (bf16[22,32,128]{2,1,0:T(8,128)(2,1)S(1)}, bf16[22,32,128]{2,1,0:T(8,128)(2,1)S(1)}, u32[]{:S(2)}, u32[]{:S(2)}) collective-permute-start(bf16[22,32,128]{2,1,0:T(8,128)(2,1)S(1)} %get-tuple-element.15), channel_id=1, source_target_pairs={{0,8},{1,9},{2,10},{3,11},{4,12},{5,13},{6,14},{7,15},{8,0},{9,1},... | collective-permute-start | bytes 540680 | tf_op jit(solution)/shard_map/ppermute | solution.py:333
  2.4 9.4 %collective-permute-start.1 = (bf16[22,32,128]{2,1,0:T(8,128)(2,1)S(1)}, bf16[22,32,128]{2,1,0:T(8,128)(2,1)S(1)}, u32[]{:S(2)}, u32[]{:S(2)}) collective-permute-start(bf16[22,32,128]{2,1,0:T(8,128)(2,1)S(1)} %get-tuple-element.16), channel_id=1, source_target_pairs={{0,1},{1,0},{2,3},{3,2},{4,5},{5,4},{6,7},{7,6},{8,16},{9,17},{10,... | collective-permute-start | bytes 540680 | tf_op jit(solution)/shard_map/ppermute | solution.py:333
  12.3 6.7 %collective-permute-start.2 = (bf16[7,32,128]{2,1,0:T(8,128)(2,1)S(1)}, bf16[7,32,128]{2,1,0:T(8,128)(2,1)S(1)}, u32[]{:S(2)}, u32[]{:S(2)}) collective-permute-start(bf16[7,32,128]{2,1,0:T(8,128)(2,1)S(1)} %get-tuple-element.18), channel_id=1, source_target_pairs={{0,8},{1,2},{2,1},{3,4},{4,3},{5,6},{6,5},{7,15},{8,0},{9,10},{10,... | collective-permute-start | bytes 172040 | tf_op jit(solution)/shard_map/ppermute | solution.py:333
  14.5 5.7 %collective-permute-start.3 = (bf16[7,32,128]{2,1,0:T(8,128)(2,1)S(1)}, bf16[7,32,128]{2,1,0:T(8,128)(2,1)S(1)}, u32[]{:S(2)}, u32[]{:S(2)}) collective-permute-start(bf16[7,32,128]{2,1,0:T(8,128)(2,1)S(1)} %get-tuple-element.19), channel_id=1, source_target_pairs={{0,1},{1,0},{2,3},{3,2},{4,5},{5,4},{6,7},{7,6},{8,9},{9,8},{10,11... | collective-permute-start | bytes 172040 | tf_op jit(solution)/shard_map/ppermute | solution.py:333

commit v6 on v5

--- a/solution.py
+++ b/solution.py
@@ -16,6 +16,7 @@
 WIN = CR + 2
 KROW = 3 * C + 3 * FRAMES * CP
 KALL = 2048
+PARTS = 4
 EROW = 2 * C + 3 * FRAMES * CP
 KEDGE = 1664
 TILES = 3
@@ -156,7 +157,7 @@
     return v
 
 
-def pack_kernel(nrows, off, red, recv_a, recv_b, cols, send_a, send_b, cb):
+def pack_kernel(nrows, off, red, recv_b, recv_a, cols, send_a, send_b, cb):
     off = scalars(off)
     above, below, has_above, has_below = row_halo(nrows, off, red, recv_a, recv_b, cb)
     above = above.astype(f32)
@@ -191,7 +192,7 @@
         send[2 * TILES] = total.astype(bf16)
 
 
-def local_kernel(nrows, ncols, off, red, recv_a, recv_b, cur_t, wall, bias, part, cb, x2):
+def local_kernel(nrows, ncols, off, red, recv_b, recv_a, cur_t, wall, bias, part, cb, x2):
     off = scalars(off)
     above, below, has_above, has_below = row_halo(nrows, off, red, recv_a, recv_b, cb)
     col = lax.axis_index("cols")
@@ -241,7 +242,7 @@
         part[y] = p + bias_col
 
 
-def finish_kernel(ncols, off, recv_b, recv_a, part, wedge, out, xx, acc):
+def finish_kernel(ncols, off, recv_b, recv_a, part, wedge, out, xx, acc, corr, done, sems):
     off = scalars(off)
     col = lax.axis_index("cols")
     ceven = col % 2 == 0
@@ -295,20 +296,28 @@
                 xx[at : at + CP, :CC] = jnp.where(pos[k], v, zero)
                 xx[at : at + CP, CC:] = jnp.where(pos[k], zero, v)
     xx[(TILES + 2) * EROW :, :] = jnp.zeros((KEDGE - 3 * EROW, 2 * CC), bf16)
-    wide = lanes((C, CC))
     for t in range(TILES):
-        p = jnp.dot(
+        corr[t] = jnp.dot(
             wedge[...], xx[t * EROW : t * EROW + KEDGE, :], preferred_element_type=f32
         )
-        for y in range(t, CR, TILES):
+    wide = lanes((C // PARTS, CC))
+    copies = []
+    for n in range(PARTS):
+        rows = slice(n * C // PARTS, (n + 1) * C // PARTS)
+        for y in range(CR):
             q = y // TILES
-            lft = pltpu.roll(p[:, :CC], (CC - SEG * q) % CC, 1)
-            rgt = pltpu.roll(p[:, CC:], (SEG0 - SEG * q) % CC, 1)
+            lft = pltpu.roll(corr[y % TILES, rows, :CC], (CC - SEG * q) % CC, 1)
+            rgt = pltpu.roll(corr[y % TILES, rows, CC:], (SEG0 - SEG * q) % CC, 1)
             v = jnp.where(wide < SEG, lft, jnp.where(wide >= SEG0, rgt, 0.0))
             at = 0 if y < CR // 2 else CC
-            v = jnp.maximum(part[y % (CR // 2), :, at : at + CC] + v, 0.0)
-            acc[pl.ds(y, C, stride=CR), :] = v
-    out[...] = acc[...].astype(bf16)
+            v = jnp.maximum(part[y % (CR // 2), rows, at : at + CC] + v, 0.0)
+            acc[pl.ds(n * C * CR // PARTS + y, C // PARTS, stride=CR), :] = v
+        piece = pl.ds(n * C * CR // PARTS, C * CR // PARTS)
+        done[piece] = acc[piece].astype(bf16)
+        copies.append(pltpu.make_async_copy(done.at[piece], out.at[piece], sems.at[n]))
+        copies[-1].start()
+    for copy in copies:
+        copy.wait()
 
 
 def partner(i, size, shifted):
@@ -325,7 +334,7 @@
         for c in range(ncols):
             if axis == "rows":
                 to = partner(r, nrows, shifted)
-                to = (r, c ^ 1) if to is None else (to, c)
+                to = (r, c ^ 2) if to is None else (to, c)
             else:
                 to = partner(c, ncols, shifted)
                 to = (r ^ 1, c) if to is None else (r, to)
@@ -337,13 +346,13 @@
     return pl.CostEstimate(flops=flops, bytes_accessed=bytes_accessed, transcendentals=0)
 
 
-def call(kernel, outs, specs, scratch, estimate):
+def call(kernel, outs, specs, scratch, estimate, place=None):
     vmem = pl.BlockSpec(memory_space=pltpu.VMEM)
     return pl.pallas_call(
         kernel,
         out_shape=[jax.ShapeDtypeStruct(*out) for out in outs],
         in_specs=specs,
-        out_specs=[vmem] * len(outs),
+        out_specs=[place or vmem] * len(outs),
         scratch_shapes=scratch,
         cost_estimate=estimate,
         compiler_params=pltpu.CompilerParams(vmem_limit_bytes=VMEM_LIMIT),
@@ -389,7 +398,7 @@
         [vmem] * 5,
         [halo_rows],
         cost(1 << 20, 2 << 20),
-    )(off, red, recv_a, recv_b, cols)
+    )(off, red, recv_b, recv_a, cols)
     crecv_b = swap(csend_b, "cols", True)
     crecv_a = swap(csend_a, "cols", False)
     (part,) = call(
@@ -398,7 +407,7 @@
         [vmem] * 7,
         [halo_rows, pltpu.VMEM(((WIN - CR // 2) * KROW + KALL - 3 * KROW, 2 * CC), bf16)],
         cost(2 * C * KALL * CR * CC, 4 << 20),
-    )(off, red, recv_a, recv_b, cur_t, wall, mixer_bias.reshape(C, 1))
+    )(off, red, recv_b, recv_a, cur_t, wall, mixer_bias.reshape(C, 1))
     (out,) = call(
         lambda *refs: finish_kernel(ncols, *refs),
         [((C * CR, CC), bf16)],
@@ -406,8 +415,12 @@
         [
             pltpu.VMEM(((TILES + 2) * EROW + KEDGE - 3 * EROW, 2 * CC), bf16),
             pltpu.VMEM((C * CR, CC), f32),
+            pltpu.VMEM((TILES, C, 2 * CC), f32),
+            pltpu.VMEM((C * CR, CC), bf16),
+            pltpu.SemaphoreType.DMA((PARTS,)),
         ],
         cost(1 << 20, 2 << 20),
+        hbm,
     )(off, crecv_b, crecv_a, part, wedge)
     return out.reshape(C, CR, CC)
 

time: 22.5 us -> 21.6 us (0.960)
  starting transfers between devices: 9.82 us -> 9.15 us
    ppermute x4, starting transfers between devices: 9.82 us -> 9.15 us  [swap(): return lax.ppermute(x, ('rows', 'cols'), pairs)]
where the time goes in v6:
time: 21.6 us; the launch traced here: 21.4 us
  starting transfers between devices  9.15 us (42%)
  Pallas kernels  7.28 us (34%)
  waiting for transfers between devices  4.77 us (22%)
    ppermute x4, starting transfers between devices, swap(): return lax.ppermute(x, ('rows', 'cols'), pairs)  9.15 us
    ppermute x4, waiting for transfers between devices, swap(): return lax.ppermute(x, ('rows', 'cols'), pairs)  4.77 us
    pallas_call x1, Pallas kernels, body(): call(compress_kernel, [((FRAMES, CR, CP, CC), bf16), (row_send, bf16), (r...  2.3 us
    pallas_call x1, Pallas kernels, body(): call(lambda *refs: finish_kernel(ncols, *refs), [((C * CR, CC), bf16)], [...  1.88 us
    pallas_call x1, Pallas kernels, body(): call(lambda *refs: local_kernel(nrows, ncols, *refs), [((CR // 2, C, 2 *...  1.76 us
    pallas_call x1, Pallas kernels, body(): call(prepare_kernel, [((CR, C, CC), bf16), ((2, C, CC), bf16), ((C, KALL)...  0.9 us
    pallas_call x1, Pallas kernels, body(): call(lambda *refs: pack_kernel(nrows, *refs), [(col_send, bf16), (col_sen...  0.45 us
  transfers between devices with their start and end apart: 4, of which 3 were waited for; matrix products, arithmetic and copies ran while one was open for 1% of the time, Pallas kernels for 12%

profile of v6, /device:TPU:14, one launch (start us, length us, event | category | flops | bytes accessed | tf_op | source)
XLA Modules:
  0.0 21.4 jit_solution(10705670253993118205)
XLA Ops:
  0.0 0.0 copy-start
  0.0 0.0 copy-start.3
  0.0 0.0 copy-start.1
  0.0 0.0 copy-start.2
  0.0 2.3 %shard_map.64 = (bf16[3,16,32,128]{3,2,1,0:T(8,128)(2,1)S(1)}, bf16[22,32,128]{2,1,0:T(8,128)(2,1)S(1)}, bf16[22,32,128]{2,1,0:T(8,128)(2,1)S(1)}) custom-call(s32[2,3]{1,0:T(2,128)} %bitcast.9, bf16[3,2048,128]{2,1,0:T(8,128)(2,1)} %bitcast.13, bf16[2048,128]{1,0:T(8,128)(2,1)} %bitcast.6, bf16[32,128]{1,0:T(8,128)(2,1)} %w_hbm.1), custom_call_target="tpu_custom_call" | custom-call | flops 50331648 | bytes 3145728 | tf_op jit(solution)/shard_map/pallas_call | solution.py:372
  2.3 5.6 %collective-permute-start = (bf16[22,32,128]{2,1,0:T(8,128)(2,1)S(1)}, bf16[22,32,128]{2,1,0:T(8,128)(2,1)S(1)}, u32[]{:S(2)}, u32[]{:S(2)}) collective-permute-start(bf16[22,32,128]{2,1,0:T(8,128)(2,1)S(1)} %get-tuple-element.15), channel_id=1, source_target_pairs={{0,2},{1,3},{2,0},{3,1},{4,6},{5,7},{6,4},{7,5},{8,16},{9,17},{10,... | collective-permute-start | bytes 540680 | tf_op jit(solution)/shard_map/ppermute | solution.py:342
  8.0 0.0 collective-permute-start.1
  8.0 0.0 copy-done.3
  8.0 0.1 copy.7.refs_6_
  8.1 0.0 copy-done
  8.1 0.0 copy-done.1
  8.1 0.9 %shard_map.65 = (bf16[16,128,128]{2,1,0:T(8,128)(2,1)S(1)}, bf16[2,128,128]{2,1,0:T(8,128)(2,1)S(1)}, bf16[128,2048]{1,0:T(8,128)(2,1)S(1)}, bf16[128,1664]{1,0:T(8,128)(2,1)S(1)}) custom-call(bf16[2048,128]{1,0:T(8,128)(2,1)S(1)} %bitcast.7, bf16[3,3,224,128]{3,2,1,0:T(8,128)(2,1)S(1)} %bitcast.8), custom_call_target="tpu_custom_call" | custom-call | flops 1048576 | bytes 3145728 | tf_op jit(solution)/shard_map/pallas_call | solution.py:387
  9.0 2.1 %collective-permute-done.refs_2_ = bf16[22,32,128]{2,1,0:T(8,128)(2,1)S(1)} collective-permute-done((bf16[22,32,128]{2,1,0:T(8,128)(2,1)S(1)}, bf16[22,32,128]{2,1,0:T(8,128)(2,1)S(1)}, u32[]{:S(2)}, u32[]{:S(2)}) %collective-permute-start) | collective-permute-done | bytes 180256 | tf_op jit(solution)/shard_map/ppermute | solution.py:342
  11.2 0.0 collective-permute-done.1.refs_3_
  11.2 0.0 copy-done.2
  11.2 0.5 %shard_map.66 = (bf16[7,32,128]{2,1,0:T(8,128)(2,1)S(1)}, bf16[7,32,128]{2,1,0:T(8,128)(2,1)S(1)}) custom-call(s32[2,3]{1,0:T(2,128)S(1)} %bitcast.10, bf16[3,16,32,128]{3,2,1,0:T(8,128)(2,1)S(1)} %get-tuple-element.14.refs_1_, bf16[22,32,128]{2,1,0:T(8,128)(2,1)S(1)} %collective-permute-done.refs_2_, ...), custom_call_target="tpu_custom_call" | custom-call | flops 1048576 | bytes 2097152 | tf_op jit(solution)/shard_map/pallas_call | solution.py:395
  11.6 2.2 %collective-permute-start.2 = (bf16[7,32,128]{2,1,0:T(8,128)(2,1)S(1)}, bf16[7,32,128]{2,1,0:T(8,128)(2,1)S(1)}, u32[]{:S(2)}, u32[]{:S(2)}) collective-permute-start(bf16[7,32,128]{2,1,0:T(8,128)(2,1)S(1)} %get-tuple-element.18), channel_id=1, source_target_pairs={{0,8},{1,2},{2,1},{3,4},{4,3},{5,6},{6,5},{7,15},{8,0},{9,10},{10,... | collective-permute-start | bytes 172040 | tf_op jit(solution)/shard_map/ppermute | solution.py:342
  13.8 1.3 %collective-permute-start.3 = (bf16[7,32,128]{2,1,0:T(8,128)(2,1)S(1)}, bf16[7,32,128]{2,1,0:T(8,128)(2,1)S(1)}, u32[]{:S(2)}, u32[]{:S(2)}) collective-permute-start(bf16[7,32,128]{2,1,0:T(8,128)(2,1)S(1)} %get-tuple-element.19), channel_id=1, source_target_pairs={{0,1},{1,0},{2,3},{3,2},{4,5},{5,4},{6,7},{7,6},{8,9},{9,8},{10,11... | collective-permute-start | bytes 172040 | tf_op jit(solution)/shard_map/ppermute | solution.py:342
  15.1 1.8 %shard_map.67.refs_3_ = f32[8,128,256]{2,1,0:T(8,128)S(1)} custom-call(s32[2,3]{1,0:T(2,128)S(1)} %bitcast.11, bf16[3,16,32,128]{3,2,1,0:T(8,128)(2,1)S(1)} %get-tuple-element.14.refs_1_, bf16[22,32,128]{2,1,0:T(8,128)(2,1)S(1)} %collective-permute-done.refs_2_, bf16[22,32,128]{2,1,0:T(8,128)(2,1)S(1)} %collective-permute-done.1.refs_3_, ...), custom_call_target="tpu_custom_call" | custom-call | flops 1073741824 | bytes 4194304 | tf_op jit(solution)/shard_map/pallas_call | solution.py:404
  16.9 1.4 %collective-permute-done.2.refs_1_ = bf16[7,32,128]{2,1,0:T(8,128)(2,1)S(1)} collective-permute-done((bf16[7,32,128]{2,1,0:T(8,128)(2,1)S(1)}, bf16[7,32,128]{2,1,0:T(8,128)(2,1)S(1)}, u32[]{:S(2)}, u32[]{:S(2)}) %collective-permute-start.2) | collective-permute-done | bytes 57376 | tf_op jit(solution)/shard_map/ppermute | solution.py:342
  18.3 1.2 %collective-permute-done.3.refs_2_ = bf16[7,32,128]{2,1,0:T(8,128)(2,1)S(1)} collective-permute-done((bf16[7,32,128]{2,1,0:T(8,128)(2,1)S(1)}, bf16[7,32,128]{2,1,0:T(8,128)(2,1)S(1)}, u32[]{:S(2)}, u32[]{:S(2)}) %collective-permute-start.3) | collective-permute-done | bytes 57376 | tf_op jit(solution)/shard_map/ppermute | solution.py:342
  19.5 1.9 %shard_map.68 = bf16[2048,128]{1,0:T(8,128)(2,1)} custom-call(s32[2,3]{1,0:T(2,128)S(1)} %bitcast.12, bf16[7,32,128]{2,1,0:T(8,128)(2,1)S(1)} %collective-permute-done.2.refs_1_, bf16[7,32,128]{2,1,0:T(8,128)(2,1)S(1)} %collective-permute-done.3.refs_2_, f32[8,128,256]{2,1,0:T(8,128)S(1)} %shard_map.67.refs_3_, bf16[128,1664]{1,0:T(8,128)(2,1)S(1)} %get-tuple-element.22.refs_4_), custom_call_target="tpu_custom_call" | custom-call | flops 1048576 | bytes 2097152 | tf_op jit(solution)/shard_map/pallas_call | solution.py:411
Async XLA Ops:
  0.0 8.1 %copy-start = (bf16[128,16,128]{2,1,0:T(8,128)(2,1)S(1)}, bf16[128,16,128]{2,1,0:T(8,128)(2,1)}, u32[]{:S(2)}) copy-start(bf16[128,16,128]{2,1,0:T(8,128)(2,1)} %param.6) | copy-start | bytes 1572868
  0.0 8.0 %copy-start.3 = (f32[128]{0:T(128)S(1)}, f32[128]{0:T(128)}, u32[]{:S(2)}) copy-start(f32[128]{0:T(128)} %param.11) | copy-start | bytes 1540
  0.0 8.1 %copy-start.1 = (bf16[3,3,128,224]{2,3,1,0:T(8,128)(2,1)S(1)}, bf16[3,3,128,224]{2,3,1,0:T(8,128)(2,1)}, u32[]{:S(2)}) copy-start(bf16[3,3,128,224]{2,3,1,0:T(8,128)(2,1)} %param.10) | copy-start | bytes 1548292
  0.0 11.1 %copy-start.2 = (s32[3,2]{0,1:T(2,128)S(1)}, s32[3,2]{0,1:T(2,128)}, u32[]{:S(2)}) copy-start(s32[3,2]{0,1:T(2,128)} %param.8) | copy-start | bytes 76
  2.3 8.8 %collective-permute-start = (bf16[22,32,128]{2,1,0:T(8,128)(2,1)S(1)}, bf16[22,32,128]{2,1,0:T(8,128)(2,1)S(1)}, u32[]{:S(2)}, u32[]{:S(2)}) collective-permute-start(bf16[22,32,128]{2,1,0:T(8,128)(2,1)S(1)} %get-tuple-element.15), channel_id=1, source_target_pairs={{0,2},{1,3},{2,0},{3,1},{4,6},{5,7},{6,4},{7,5},{8,16},{9,17},{10,... | collective-permute-start | bytes 540680 | tf_op jit(solution)/shard_map/ppermute | solution.py:342
  8.0 3.2 %collective-permute-start.1 = (bf16[22,32,128]{2,1,0:T(8,128)(2,1)S(1)}, bf16[22,32,128]{2,1,0:T(8,128)(2,1)S(1)}, u32[]{:S(2)}, u32[]{:S(2)}) collective-permute-start(bf16[22,32,128]{2,1,0:T(8,128)(2,1)S(1)} %get-tuple-element.16), channel_id=1, source_target_pairs={{0,8},{1,9},{2,10},{3,11},{4,12},{5,13},{6,14},{7,15},{8,0},{9,1},... | collective-permute-start | bytes 540680 | tf_op jit(solution)/shard_map/ppermute | solution.py:342
  11.6 6.7 %collective-permute-start.2 = (bf16[7,32,128]{2,1,0:T(8,128)(2,1)S(1)}, bf16[7,32,128]{2,1,0:T(8,128)(2,1)S(1)}, u32[]{:S(2)}, u32[]{:S(2)}) collective-permute-start(bf16[7,32,128]{2,1,0:T(8,128)(2,1)S(1)} %get-tuple-element.18), channel_id=1, source_target_pairs={{0,8},{1,2},{2,1},{3,4},{4,3},{5,6},{6,5},{7,15},{8,0},{9,10},{10,... | collective-permute-start | bytes 172040 | tf_op jit(solution)/shard_map/ppermute | solution.py:342
  13.8 5.7 %collective-permute-start.3 = (bf16[7,32,128]{2,1,0:T(8,128)(2,1)S(1)}, bf16[7,32,128]{2,1,0:T(8,128)(2,1)S(1)}, u32[]{:S(2)}, u32[]{:S(2)}) collective-permute-start(bf16[7,32,128]{2,1,0:T(8,128)(2,1)S(1)} %get-tuple-element.19), channel_id=1, source_target_pairs={{0,1},{1,0},{2,3},{3,2},{4,5},{5,4},{6,7},{7,6},{8,9},{9,8},{10,11... | collective-permute-start | bytes 172040 | tf_op jit(solution)/shard_map/ppermute | solution.py:342

commit v7 on v6

--- a/solution.py
+++ b/solution.py
@@ -13,6 +13,9 @@
 SHIFT_X = 16
 SHIFT_Y = 8
 REACH = SHIFT_Y + 1
+PER = 6
+EDGE = 5
+LAST = 8
 WIN = CR + 2
 KROW = 3 * C + 3 * FRAMES * CP
 KALL = 2048
@@ -53,7 +56,7 @@
 
 
 def compress_kernel(
-    off_hbm, hist, cur, w_hbm, red, send_a, send_b, off, w, hbuf, cbuf, sems
+    off_hbm, hist, cur, w_hbm, red, edge_a, rows0_a, rows1_a, first_b, second_b, off, w, hbuf, cbuf, sems
 ):
     copies = [pltpu.make_async_copy(hist.at[k], hbuf.at[k], sems.at[k]) for k in range(FRAMES)]
     copies.append(pltpu.make_async_copy(cur, cbuf, sems.at[FRAMES]))
@@ -78,14 +81,34 @@
     top = by_row[0].reshape(C // CP, CP, CC)
     bottom = by_row[CR - 1].reshape(C // CP, CP, CC)
     small[1].wait()
-    _, posf, negf, _ = slots(scalars(off), 0)
-    for send, down in ((send_a, even), (send_b, jnp.logical_not(even))):
+    offs = scalars(off)
+    _, posf, negf, _ = slots(offs, 0)
+    lane = lanes((CP, CC))
+    for (row0, row1, edge, at, tail, tail_at), down in (
+        ((rows0_a, rows1_a, edge_a, 0, edge_a, EDGE), even),
+        ((first_b, second_b, first_b, REACH, second_b, REACH), jnp.logical_not(even)),
+    ):
         start = jnp.where(down, CR - REACH, 0)
+        border = jnp.where(down, bottom, top)
         for s in range(2):
             k = jnp.where(down, posf[s], negf[s])
-            for i in range(REACH):
-                send[s * REACH + i] = red[k, start + i]
-        send[2 * REACH : 2 * REACH + C // CP] = jnp.where(down, bottom, top)
+            back = jnp.where(pick(offs[1], k) > 0, SEG0, 0)
+            for h in range(REACH):
+                (row0, row1)[s][h] = red[k, start + h]
+            for n in range(2):
+                total = None
+                for q in range(min(PER, REACH - PER * n)):
+                    piece = red[k, start + PER * n + q].astype(f32)
+                    piece = pltpu.roll(piece, (SEG * q - back + CC) % CC, 1)
+                    total = piece if q == 0 else jnp.where(lane >= SEG * q, piece, total)
+                edge[at + 2 * s + n] = total.astype(bf16)
+        tail[tail_at : tail_at + C // CP] = border
+        total = jnp.zeros((CP, CC), f32)
+        for g in range(C // CP):
+            piece = border[g].astype(f32)
+            total = jnp.where(lane == g, pltpu.roll(piece, g, 1), total)
+            total = jnp.where(lane == LAST + g, pltpu.roll(piece, LAST + g + 1, 1), total)
+        edge[at + 4] = total.astype(bf16)
 
 
 def spot(r):
@@ -124,7 +147,7 @@
             dest[:, b * C : (b + 1) * C] = tall[b * C : (b + 1) * C].T.astype(bf16)
 
 
-def row_halo(nrows, off, red, recv_a, recv_b, cb):
+def row_halo(nrows, off, red, edge_a, rows0_a, rows1_a, first_b, second_b, cb):
     row = lax.axis_index("rows")
     even = row % 2 == 0
     has_above = row > 0
@@ -133,15 +156,14 @@
     zero = jnp.zeros((REACH, CP, CC), bf16)
     for k in range(FRAMES):
         cb[k, REACH : REACH + CR] = red[k]
-        at = pl.ds(place[k] * REACH, REACH)
-        from_a = recv_a[at]
-        from_b = recv_b[at]
+        from_a = jnp.where(place[k] == 0, rows0_a[...], rows1_a[...])
+        from_b = jnp.where(place[k] == 0, first_b[:REACH], second_b[:REACH])
         use_a = jnp.logical_xor(pos[k], even)
         ok = jnp.where(pos[k], has_above, has_below)
         halo = jnp.where(ok, jnp.where(use_a, from_a, from_b), zero)
         cb[k, pl.ds(jnp.where(pos[k], 0, REACH + CR), REACH)] = halo
-    tail_a = recv_a[2 * REACH : 2 * REACH + C // CP].reshape(C, CC)
-    tail_b = recv_b[2 * REACH : 2 * REACH + C // CP].reshape(C, CC)
+    tail_a = edge_a[EDGE:].reshape(C, CC)
+    tail_b = second_b[REACH:].reshape(C, CC)
     blank = jnp.zeros((C, CC), bf16)
     above = jnp.where(has_above, jnp.where(even, tail_b, tail_a), blank)
     below = jnp.where(has_below, jnp.where(even, tail_a, tail_b), blank)
@@ -157,44 +179,76 @@
     return v
 
 
-def pack_kernel(nrows, off, red, recv_b, recv_a, cols, send_a, send_b, cb):
+def pack_kernel(nrows, off, red, first_b, edge_a, cols, send_a, send_b, cb):
     off = scalars(off)
-    above, below, has_above, has_below = row_halo(nrows, off, red, recv_a, recv_b, cb)
-    above = above.astype(f32)
-    below = below.astype(f32)
+    row = lax.axis_index("rows")
+    even = row % 2 == 0
+    has_above = row > 0
+    has_below = row < nrows - 1
+    _, _, _, place = slots(off, 0)
+    zero = jnp.zeros((CP, CC), bf16)
+    corner_a = edge_a[4]
+    corner_b = first_b[REACH + 4]
+    above = jnp.where(has_above, jnp.where(even, corner_b, corner_a), zero).astype(f32)
+    below = jnp.where(has_below, jnp.where(even, corner_a, corner_b), zero).astype(f32)
     ceven = lax.axis_index("cols") % 2 == 0
     _, posf, negf, _ = slots(off, 1)
     lane = lanes((CP, CC))
     inner = segment_lane((CP, CC))
-    wide = lanes((C, CC))
     end = spot(WIN - 1)
-    first = jnp.where(wide == 0, above, cols[0].astype(f32))
-    first = jnp.where(wide == end, pltpu.roll(below, end, 1), first)
-    last = jnp.where(wide == 0, pltpu.roll(above, 1, 1), cols[1].astype(f32))
-    last = jnp.where(wide == end, pltpu.roll(below, end + 1, 1), last)
+
+    def column(which, at):
+        parts = []
+        for g in range(C // CP):
+            v = cols[which, CP * g : CP * (g + 1)].astype(f32)
+            v = jnp.where(lane == 0, pltpu.roll(above, (CC - at - g) % CC, 1), v)
+            v = jnp.where(lane == end, pltpu.roll(below, (CC + end - at - g) % CC, 1), v)
+            parts.append(v)
+        return parts
+
+    first = column(0, 0)
+    last = column(1, LAST)
     for send, right in ((send_a, ceven), (send_b, jnp.logical_not(ceven))):
         back = jnp.where(right, SEG0, 0)
         for s in range(2):
             k = jnp.where(right, posf[s], negf[s])
             dy = pick(off[0], k)
+            before = dy > 0
+            near = 2 * pick(place, k)
+            use_a = jnp.logical_xor(before, even)
+            ok = jnp.where(before, has_above, has_below)
+            halo = []
+            for n in range(2):
+                v = jnp.where(use_a, edge_a[near + n], first_b[REACH + near + n])
+                halo.append(jnp.where(ok, v, zero).astype(f32))
+            n = 2 * (send is send_b) + s
+            cb[n, REACH : REACH + CR] = red[k]
+            at = jnp.where(before, 0, REACH + CR)
+            for h in range(REACH):
+                shift = (back - SEG * (h % PER) + CC) % CC
+                cb[n, at + h] = pltpu.roll(halo[h // PER], shift, 1).astype(bf16)
             for t in range(TILES):
-                total = jnp.zeros((CP, CC), f32)
+                total = None
                 for q in range(WIN // TILES):
-                    piece = window_row(dy, cb, k, t + TILES * q, has_above, has_below)
+                    piece = window_row(dy, cb, n, t + TILES * q, has_above, has_below)
                     piece = pltpu.roll(piece.astype(f32), (SEG * q - back + CC) % CC, 1)
                     total = piece if q == 0 else jnp.where(lane >= SEG * q, piece, total)
                 send[s * TILES + t] = total.astype(bf16)
-        pack = jnp.where(right, last, first)
-        total = pack[:CP]
+        total = jnp.where(right, last[0], first[0])
         for g in range(1, C // CP):
-            moved = pltpu.roll(pack[CP * g : CP * (g + 1)], TILES * g, 1)
+            moved = pltpu.roll(jnp.where(right, last[g], first[g]), TILES * g, 1)
             total = jnp.where(inner >= TILES * g, moved, total)
         send[2 * TILES] = total.astype(bf16)
 
 
-def local_kernel(nrows, ncols, off, red, recv_b, recv_a, cur_t, wall, bias, part, cb, x2):
+def local_kernel(
+    nrows, ncols, off, red, first_b, second_b, edge_a, rows0_a, rows1_a, *rest
+):
+    cur_t, wall, bias, part, cb, x2 = rest
     off = scalars(off)
-    above, below, has_above, has_below = row_halo(nrows, off, red, recv_a, recv_b, cb)
+    above, below, has_above, has_below = row_halo(
+        nrows, off, red, edge_a, rows0_a, rows1_a, first_b, second_b, cb
+    )
     col = lax.axis_index("cols")
     has_left = col > 0
     has_right = col < ncols - 1
@@ -367,11 +421,17 @@
     cur = current_frame.reshape(C * CR, CC)
     wt = mixer_weight.transpose(0, 1, 3, 2)
     nrows, ncols = lax.axis_size("rows"), lax.axis_size("cols")
-    row_send = (2 * REACH + C // CP, CP, CC)
     col_send = (2 * TILES + 1, CP, CC)
-    red, send_a, send_b = call(
+    red, edge_a, rows0_a, rows1_a, first_b, second_b = call(
         compress_kernel,
-        [((FRAMES, CR, CP, CC), bf16), (row_send, bf16), (row_send, bf16)],
+        [
+            ((FRAMES, CR, CP, CC), bf16),
+            ((EDGE + C // CP, CP, CC), bf16),
+            ((REACH, CP, CC), bf16),
+            ((REACH, CP, CC), bf16),
+            ((REACH + EDGE, CP, CC), bf16),
+            ((REACH + C // CP, CP, CC), bf16),
+        ],
         [hbm] * 4,
         [
             pltpu.SMEM((2, FRAMES), jnp.int32),
@@ -382,8 +442,11 @@
         ],
         cost(2 * FRAMES * CP * C * CR * CC, 3 << 20),
     )(*[pltpu.with_memory_space_constraint(v, pltpu.HBM) for v in (off, hist, cur, compress_weight)])
-    recv_a = swap(send_a, "rows", False)
-    recv_b = swap(send_b, "rows", True)
+    edge_a = swap(edge_a, "rows", False)
+    rows0_a = swap(rows0_a, "rows", False)
+    rows1_a = swap(rows1_a, "rows", False)
+    first_b = swap(first_b, "rows", True)
+    second_b = swap(second_b, "rows", True)
     cur_t, cols, wall, wedge = call(
         prepare_kernel,
         [((CR, C, CC), bf16), ((2, C, CC), bf16), ((C, KALL), bf16), ((C, KEDGE), bf16)],
@@ -396,18 +459,18 @@
         lambda *refs: pack_kernel(nrows, *refs),
         [(col_send, bf16), (col_send, bf16)],
         [vmem] * 5,
-        [halo_rows],
+        [pltpu.VMEM((4, CR + 2 * REACH, CP, CC), bf16)],
         cost(1 << 20, 2 << 20),
-    )(off, red, recv_b, recv_a, cols)
+    )(off, red, first_b, edge_a, cols)
     crecv_b = swap(csend_b, "cols", True)
     crecv_a = swap(csend_a, "cols", False)
     (part,) = call(
         lambda *refs: local_kernel(nrows, ncols, *refs),
         [((CR // 2, C, 2 * CC), f32)],
-        [vmem] * 7,
+        [vmem] * 10,
         [halo_rows, pltpu.VMEM(((WIN - CR // 2) * KROW + KALL - 3 * KROW, 2 * CC), bf16)],
         cost(2 * C * KALL * CR * CC, 4 << 20),
-    )(off, red, recv_b, recv_a, cur_t, wall, mixer_bias.reshape(C, 1))
+    )(off, red, first_b, second_b, edge_a, rows0_a, rows1_a, cur_t, wall, mixer_bias.reshape(C, 1))
     (out,) = call(
         lambda *refs: finish_kernel(ncols, *refs),
         [((C * CR, CC), bf16)],

time: 21.6 us -> 21.3 us (0.986)
  waiting for transfers between devices: 4.77 us -> 3.37 us
  starting transfers between devices: 9.15 us -> 9.76 us
  Pallas kernels: 7.28 us -> 7.68 us
    ppermute x4 -> x7, waiting for transfers between devices: 4.77 us -> 3.37 us  [swap(): return lax.ppermute(x, ('rows', 'cols'), pairs)]
    ppermute x4 -> x7, starting transfers between devices: 9.15 us -> 9.76 us  [swap(): return lax.ppermute(x, ('rows', 'cols'), pairs)]
  transfers between devices with their start and end apart: 4 -> 7, of which waited for: 3 -> 3; matrix products, arithmetic and copies ran while one was open for 1% -> 1% of each run, Pallas kernels for 12% -> 16%
where the time goes in v7:
time: 21.3 us; the launch traced here: 21 us
  starting transfers between devices  9.76 us (46%)
  Pallas kernels  7.68 us (36%)
  waiting for transfers between devices  3.37 us (16%)
    ppermute x7, starting transfers between devices, swap(): return lax.ppermute(x, ('rows', 'cols'), pairs)  9.76 us
    ppermute x7, waiting for transfers between devices, swap(): return lax.ppermute(x, ('rows', 'cols'), pairs)  3.37 us
    pallas_call x1, Pallas kernels, body(): call(compress_kernel, [((FRAMES, CR, CP, CC), bf16), ((EDGE + C // CP, CP...  2.46 us
    pallas_call x1, Pallas kernels, body(): call(lambda *refs: finish_kernel(ncols, *refs), [((C * CR, CC), bf16)], [...  1.88 us
    pallas_call x1, Pallas kernels, body(): call(lambda *refs: local_kernel(nrows, ncols, *refs), [((CR // 2, C, 2 *...  1.84 us
    pallas_call x1, Pallas kernels, body(): call(prepare_kernel, [((CR, C, CC), bf16), ((2, C, CC), bf16), ((C, KALL)...  0.9 us
    pallas_call x1, Pallas kernels, body(): call(lambda *refs: pack_kernel(nrows, *refs), [(col_send, bf16), (col_sen...  0.61 us
  transfers between devices with their start and end apart: 7, of which 3 were waited for; matrix products, arithmetic and copies ran while one was open for 1% of the time, Pallas kernels for 16%

profile of v7, /device:TPU:14, one launch (start us, length us, event | category | flops | bytes accessed | tf_op | source)
XLA Modules:
  0.0 21.0 jit_solution(8902504742347466110)
XLA Ops:
  0.0 0.0 copy-start
  0.0 0.0 copy-start.3
  0.0 0.0 copy-start.1
  0.0 0.0 copy-start.2
  0.0 2.5 %shard_map.64 = (bf16[3,16,32,128]{3,2,1,0:T(8,128)(2,1)S(1)}, bf16[9,32,128]{2,1,0:T(8,128)(2,1)S(1)}, bf16[9,32,128]{2,1,0:T(8,128)(2,1)S(1)}, bf16[9,32,128]{...) custom-call(s32[2,3]{1,0:T(2,128)} %bitcast.9, ...), custom_call_target="tpu_custom_call" | custom-call | flops 50331648 | bytes 3145728 | tf_op jit(solution)/shard_map/pallas_call | solution.py:425
  2.5 5.6 %collective-permute-start = (bf16[14,32,128]{2,1,0:T(8,128)(2,1)S(1)}, bf16[14,32,128]{2,1,0:T(8,128)(2,1)S(1)}, u32[]{:S(2)}, u32[]{:S(2)}) collective-permute-start(bf16[14,32,128]{2,1,0:T(8,128)(2,1)S(1)} %get-tuple-element.18), channel_id=1, source_target_pairs={{0,2},{1,3},{2,0},{3,1},{4,6},{5,7},{6,4},{7,5},{8,16},{9,17},{10,... | collective-permute-start | bytes 344072 | tf_op jit(solution)/shard_map/ppermute | solution.py:396
  8.1 0.1 collective-permute-start.4
  8.2 0.0 collective-permute-start.1
  8.2 0.5 %collective-permute-start.5 = (bf16[9,32,128]{2,1,0:T(8,128)(2,1)S(1)}, bf16[9,32,128]{2,1,0:T(8,128)(2,1)S(1)}, u32[]{:S(2)}, u32[]{:S(2)}) collective-permute-start(bf16[9,32,128]{2,1,0:T(8,128)(2,1)S(1)} %get-tuple-element.24), channel_id=1, source_target_pairs={{0,8},{1,9},{2,10},{3,11},{4,12},{5,13},{6,14},{7,15},{8,0},{9,1},... | collective-permute-start | bytes 221192 | tf_op jit(solution)/shard_map/ppermute | solution.py:396
  8.7 0.0 collective-permute-start.6
  8.7 0.0 copy-done.3
  8.8 0.1 copy.7.refs_9_
  8.9 0.0 copy-done
  8.9 0.0 copy-done.1
  8.9 0.9 %shard_map.65 = (bf16[16,128,128]{2,1,0:T(8,128)(2,1)S(1)}, bf16[2,128,128]{2,1,0:T(8,128)(2,1)S(1)}, bf16[128,2048]{1,0:T(8,128)(2,1)S(1)}, bf16[128,1664]{1,0:T(8,128)(2,1)S(1)}) custom-call(bf16[2048,128]{1,0:T(8,128)(2,1)S(1)} %bitcast.7, bf16[3,3,224,128]{3,2,1,0:T(8,128)(2,1)S(1)} %bitcast.8), custom_call_target="tpu_custom_call" | custom-call | flops 1048576 | bytes 3145728 | tf_op jit(solution)/shard_map/pallas_call | solution.py:450
  9.8 0.0 collective-permute-done.1.refs_3_.refs_4_
  9.8 0.8 %collective-permute-done.refs_2_ = bf16[14,32,128]{2,1,0:T(8,128)(2,1)S(1)} collective-permute-done((bf16[14,32,128]{2,1,0:T(8,128)(2,1)S(1)}, bf16[14,32,128]{2,1,0:T(8,128)(2,1)S(1)}, u32[]{:S(2)}, u32[]{:S(2)}) %collective-permute-start) | collective-permute-done | bytes 114720 | tf_op jit(solution)/shard_map/ppermute | solution.py:396
  10.6 0.0 copy-done.2
  10.6 0.6 %shard_map.66 = (bf16[7,32,128]{2,1,0:T(8,128)(2,1)S(1)}, bf16[7,32,128]{2,1,0:T(8,128)(2,1)S(1)}) custom-call(s32[2,3]{1,0:T(2,128)S(1)} %bitcast.10, bf16[3,16,32,128]{3,2,1,0:T(8,128)(2,1)S(1)} %get-tuple-element.17.refs_1_, bf16[14,32,128]{2,1,0:T(8,128)(2,1)S(1)} %collective-permute-done.refs_2_, ...), custom_call_target="tpu_custom_call" | custom-call | flops 1048576 | bytes 2097152 | tf_op jit(solution)/shard_map/pallas_call | solution.py:458
  11.2 2.2 %collective-permute-start.2 = (bf16[7,32,128]{2,1,0:T(8,128)(2,1)S(1)}, bf16[7,32,128]{2,1,0:T(8,128)(2,1)S(1)}, u32[]{:S(2)}, u32[]{:S(2)}) collective-permute-start(bf16[7,32,128]{2,1,0:T(8,128)(2,1)S(1)} %get-tuple-element.21), channel_id=1, source_target_pairs={{0,8},{1,2},{2,1},{3,4},{4,3},{5,6},{6,5},{7,15},{8,0},{9,10},{10,... | collective-permute-start | bytes 172040 | tf_op jit(solution)/shard_map/ppermute | solution.py:396
  13.4 1.3 %collective-permute-start.3 = (bf16[7,32,128]{2,1,0:T(8,128)(2,1)S(1)}, bf16[7,32,128]{2,1,0:T(8,128)(2,1)S(1)}, u32[]{:S(2)}, u32[]{:S(2)}) collective-permute-start(bf16[7,32,128]{2,1,0:T(8,128)(2,1)S(1)} %get-tuple-element.22), channel_id=1, source_target_pairs={{0,1},{1,0},{2,3},{3,2},{4,5},{5,4},{6,7},{7,6},{8,9},{9,8},{10,11... | collective-permute-start | bytes 172040 | tf_op jit(solution)/shard_map/ppermute | solution.py:396
  14.7 0.0 collective-permute-done.5.refs_5_
  14.7 0.0 collective-permute-done.6.refs_6_
  14.7 0.0 collective-permute-done.4.refs_3_
  14.7 1.8 %shard_map.67.refs_3_ = f32[8,128,256]{2,1,0:T(8,128)S(1)} custom-call(s32[2,3]{1,0:T(2,128)S(1)} %bitcast.11, bf16[3,16,32,128]{3,2,1,0:T(8,128)(2,1)S(1)} %get-tuple-element.17.refs_1_, bf16[14,32,128]{2,1,0:T(8,128)(2,1)S(1)} %collective-permute-done.refs_2_, bf16[13,32,128]{2,1,0:T(8,128)(2,1)S(1)} %collective-permute-done.4.refs_3_, ...), custom_call_target="tpu_custom_call" | custom-call | flops 1073741824 | bytes 4194304 | tf_op jit(solution)/shard_map/pallas_call | solution.py:467
  16.6 1.6 %collective-permute-done.2.refs_1_ = bf16[7,32,128]{2,1,0:T(8,128)(2,1)S(1)} collective-permute-done((bf16[7,32,128]{2,1,0:T(8,128)(2,1)S(1)}, bf16[7,32,128]{2,1,0:T(8,128)(2,1)S(1)}, u32[]{:S(2)}, u32[]{:S(2)}) %collective-permute-start.2) | collective-permute-done | bytes 57376 | tf_op jit(solution)/shard_map/ppermute | solution.py:396
  18.2 0.9 %collective-permute-done.3.refs_2_ = bf16[7,32,128]{2,1,0:T(8,128)(2,1)S(1)} collective-permute-done((bf16[7,32,128]{2,1,0:T(8,128)(2,1)S(1)}, bf16[7,32,128]{2,1,0:T(8,128)(2,1)S(1)}, u32[]{:S(2)}, u32[]{:S(2)}) %collective-permute-start.3) | collective-permute-done | bytes 57376 | tf_op jit(solution)/shard_map/ppermute | solution.py:396
  19.1 1.9 %shard_map.68 = bf16[2048,128]{1,0:T(8,128)(2,1)} custom-call(s32[2,3]{1,0:T(2,128)S(1)} %bitcast.12, bf16[7,32,128]{2,1,0:T(8,128)(2,1)S(1)} %collective-permute-done.2.refs_1_, bf16[7,32,128]{2,1,0:T(8,128)(2,1)S(1)} %collective-permute-done.3.refs_2_, f32[8,128,256]{2,1,0:T(8,128)S(1)} %shard_map.67.refs_3_, bf16[128,1664]{1,0:T(8,128)(2,1)S(1)} %get-tuple-element.28.refs_4_), custom_call_target="tpu_custom_call" | custom-call | flops 1048576 | bytes 2097152 | tf_op jit(solution)/shard_map/pallas_call | solution.py:474
Async XLA Ops:
  0.0 8.9 %copy-start = (bf16[128,16,128]{2,1,0:T(8,128)(2,1)S(1)}, bf16[128,16,128]{2,1,0:T(8,128)(2,1)}, u32[]{:S(2)}) copy-start(bf16[128,16,128]{2,1,0:T(8,128)(2,1)} %param.6) | copy-start | bytes 1572868
  0.0 8.7 %copy-start.3 = (f32[128]{0:T(128)S(1)}, f32[128]{0:T(128)}, u32[]{:S(2)}) copy-start(f32[128]{0:T(128)} %param.11) | copy-start | bytes 1540
  0.0 8.9 %copy-start.1 = (bf16[3,3,128,224]{2,3,1,0:T(8,128)(2,1)S(1)}, bf16[3,3,128,224]{2,3,1,0:T(8,128)(2,1)}, u32[]{:S(2)}) copy-start(bf16[3,3,128,224]{2,3,1,0:T(8,128)(2,1)} %param.10) | copy-start | bytes 1548292
  0.0 10.6 %copy-start.2 = (s32[3,2]{0,1:T(2,128)S(1)}, s32[3,2]{0,1:T(2,128)}, u32[]{:S(2)}) copy-start(s32[3,2]{0,1:T(2,128)} %param.8) | copy-start | bytes 76
  2.5 8.1 %collective-permute-start = (bf16[14,32,128]{2,1,0:T(8,128)(2,1)S(1)}, bf16[14,32,128]{2,1,0:T(8,128)(2,1)S(1)}, u32[]{:S(2)}, u32[]{:S(2)}) collective-permute-start(bf16[14,32,128]{2,1,0:T(8,128)(2,1)S(1)} %get-tuple-element.18), channel_id=1, source_target_pairs={{0,2},{1,3},{2,0},{3,1},{4,6},{5,7},{6,4},{7,5},{8,16},{9,17},{10,... | collective-permute-start | bytes 344072 | tf_op jit(solution)/shard_map/ppermute | solution.py:396
  8.1 6.6 %collective-permute-start.4 = (bf16[13,32,128]{2,1,0:T(8,128)(2,1)S(1)}, bf16[13,32,128]{2,1,0:T(8,128)(2,1)S(1)}, u32[]{:S(2)}, u32[]{:S(2)}) collective-permute-start(bf16[13,32,128]{2,1,0:T(8,128)(2,1)S(1)} %get-tuple-element.23), channel_id=1, source_target_pairs={{0,2},{1,3},{2,0},{3,1},{4,6},{5,7},{6,4},{7,5},{8,16},{9,17},{10,... | collective-permute-start | bytes 319496 | tf_op jit(solution)/shard_map/ppermute | solution.py:396
  8.2 1.5 %collective-permute-start.1 = (bf16[9,32,128]{2,1,0:T(8,128)(2,1)S(1)}, bf16[9,32,128]{2,1,0:T(8,128)(2,1)S(1)}, u32[]{:S(2)}, u32[]{:S(2)}) collective-permute-start(bf16[9,32,128]{2,1,0:T(8,128)(2,1)S(1)} %get-tuple-element.19), channel_id=1, source_target_pairs={{0,8},{1,9},{2,10},{3,11},{4,12},{5,13},{6,14},{7,15},{8,0},{9,1},... | collective-permute-start | bytes 221192 | tf_op jit(solution)/shard_map/ppermute | solution.py:396
  8.2 6.5 %collective-permute-start.5 = (bf16[9,32,128]{2,1,0:T(8,128)(2,1)S(1)}, bf16[9,32,128]{2,1,0:T(8,128)(2,1)S(1)}, u32[]{:S(2)}, u32[]{:S(2)}) collective-permute-start(bf16[9,32,128]{2,1,0:T(8,128)(2,1)S(1)} %get-tuple-element.24), channel_id=1, source_target_pairs={{0,8},{1,9},{2,10},{3,11},{4,12},{5,13},{6,14},{7,15},{8,0},{9,1},... | collective-permute-start | bytes 221192 | tf_op jit(solution)/shard_map/ppermute | solution.py:396
  8.7 6.0 %collective-permute-start.6 = (bf16[9,32,128]{2,1,0:T(8,128)(2,1)S(1)}, bf16[9,32,128]{2,1,0:T(8,128)(2,1)S(1)}, u32[]{:S(2)}, u32[]{:S(2)}) collective-permute-start(bf16[9,32,128]{2,1,0:T(8,128)(2,1)S(1)} %get-tuple-element.25), channel_id=1, source_target_pairs={{0,8},{1,9},{2,10},{3,11},{4,12},{5,13},{6,14},{7,15},{8,0},{9,1},... | collective-permute-start | bytes 221192 | tf_op jit(solution)/shard_map/ppermute | solution.py:396
  11.2 7.0 %collective-permute-start.2 = (bf16[7,32,128]{2,1,0:T(8,128)(2,1)S(1)}, bf16[7,32,128]{2,1,0:T(8,128)(2,1)S(1)}, u32[]{:S(2)}, u32[]{:S(2)}) collective-permute-start(bf16[7,32,128]{2,1,0:T(8,128)(2,1)S(1)} %get-tuple-element.21), channel_id=1, source_target_pairs={{0,8},{1,2},{2,1},{3,4},{4,3},{5,6},{6,5},{7,15},{8,0},{9,10},{10,... | collective-permute-start | bytes 172040 | tf_op jit(solution)/shard_map/ppermute | solution.py:396
  13.4 5.7 %collective-permute-start.3 = (bf16[7,32,128]{2,1,0:T(8,128)(2,1)S(1)}, bf16[7,32,128]{2,1,0:T(8,128)(2,1)S(1)}, u32[]{:S(2)}, u32[]{:S(2)}) collective-permute-start(bf16[7,32,128]{2,1,0:T(8,128)(2,1)S(1)} %get-tuple-element.22), channel_id=1, source_target_pairs={{0,1},{1,0},{2,3},{3,2},{4,5},{5,4},{6,7},{7,6},{8,9},{9,8},{10,11... | collective-permute-start | bytes 172040 | tf_op jit(solution)/shard_map/ppermute | solution.py:396

commit v8 on v7

--- a/solution.py
+++ b/solution.py
@@ -19,7 +19,7 @@
 WIN = CR + 2
 KROW = 3 * C + 3 * FRAMES * CP
 KALL = 2048
-PARTS = 4
+PARTS = 8
 EROW = 2 * C + 3 * FRAMES * CP
 KEDGE = 1664
 TILES = 3

time: 21.3 us -> 21.3 us (level)
  no operation moved by 1% of the time
where the time goes in v8:
time: 21.3 us; the launch traced here: 21 us
  starting transfers between devices  9.76 us (46%)
  Pallas kernels  7.68 us (36%)
  waiting for transfers between devices  3.37 us (16%)
    ppermute x7, starting transfers between devices, swap(): return lax.ppermute(x, ('rows', 'cols'), pairs)  9.76 us
    ppermute x7, waiting for transfers between devices, swap(): return lax.ppermute(x, ('rows', 'cols'), pairs)  3.37 us
    pallas_call x1, Pallas kernels, body(): call(compress_kernel, [((FRAMES, CR, CP, CC), bf16), ((EDGE + C // CP, CP...  2.46 us
    pallas_call x1, Pallas kernels, body(): call(lambda *refs: finish_kernel(ncols, *refs), [((C * CR, CC), bf16)], [...  1.89 us
    pallas_call x1, Pallas kernels, body(): call(lambda *refs: local_kernel(nrows, ncols, *refs), [((CR // 2, C, 2 *...  1.83 us
    pallas_call x1, Pallas kernels, body(): call(prepare_kernel, [((CR, C, CC), bf16), ((2, C, CC), bf16), ((C, KALL)...  0.9 us
    pallas_call x1, Pallas kernels, body(): call(lambda *refs: pack_kernel(nrows, *refs), [(col_send, bf16), (col_sen...  0.6 us
  transfers between devices with their start and end apart: 7, of which 3 were waited for; matrix products, arithmetic and copies ran while one was open for 1% of the time, Pallas kernels for 16%

profile of v8, /device:TPU:14, one launch (start us, length us, event | category | flops | bytes accessed | tf_op | source)
XLA Modules:
  0.0 21.0 jit_solution(11689778091883260140)
XLA Ops:
  0.0 0.0 copy-start
  0.0 0.0 copy-start.3
  0.0 0.0 copy-start.1
  0.0 0.0 copy-start.2
  0.0 2.5 %shard_map.64 = (bf16[3,16,32,128]{3,2,1,0:T(8,128)(2,1)S(1)}, bf16[9,32,128]{2,1,0:T(8,128)(2,1)S(1)}, bf16[9,32,128]{2,1,0:T(8,128)(2,1)S(1)}, bf16[9,32,128]{...) custom-call(s32[2,3]{1,0:T(2,128)} %bitcast.9, ...), custom_call_target="tpu_custom_call" | custom-call | flops 50331648 | bytes 3145728 | tf_op jit(solution)/shard_map/pallas_call | solution.py:425
  2.5 5.6 %collective-permute-start = (bf16[14,32,128]{2,1,0:T(8,128)(2,1)S(1)}, bf16[14,32,128]{2,1,0:T(8,128)(2,1)S(1)}, u32[]{:S(2)}, u32[]{:S(2)}) collective-permute-start(bf16[14,32,128]{2,1,0:T(8,128)(2,1)S(1)} %get-tuple-element.18), channel_id=1, source_target_pairs={{0,2},{1,3},{2,0},{3,1},{4,6},{5,7},{6,4},{7,5},{8,16},{9,17},{10,... | collective-permute-start | bytes 344072 | tf_op jit(solution)/shard_map/ppermute | solution.py:396
  8.1 0.1 collective-permute-start.4
  8.2 0.0 collective-permute-start.1
  8.2 0.5 %collective-permute-start.5 = (bf16[9,32,128]{2,1,0:T(8,128)(2,1)S(1)}, bf16[9,32,128]{2,1,0:T(8,128)(2,1)S(1)}, u32[]{:S(2)}, u32[]{:S(2)}) collective-permute-start(bf16[9,32,128]{2,1,0:T(8,128)(2,1)S(1)} %get-tuple-element.24), channel_id=1, source_target_pairs={{0,8},{1,9},{2,10},{3,11},{4,12},{5,13},{6,14},{7,15},{8,0},{9,1},... | collective-permute-start | bytes 221192 | tf_op jit(solution)/shard_map/ppermute | solution.py:396
  8.7 0.0 collective-permute-start.6
  8.7 0.0 copy-done.3
  8.8 0.1 copy.7.refs_9_
  8.9 0.0 copy-done
  8.9 0.0 copy-done.1
  8.9 0.9 %shard_map.65 = (bf16[16,128,128]{2,1,0:T(8,128)(2,1)S(1)}, bf16[2,128,128]{2,1,0:T(8,128)(2,1)S(1)}, bf16[128,2048]{1,0:T(8,128)(2,1)S(1)}, bf16[128,1664]{1,0:T(8,128)(2,1)S(1)}) custom-call(bf16[2048,128]{1,0:T(8,128)(2,1)S(1)} %bitcast.7, bf16[3,3,224,128]{3,2,1,0:T(8,128)(2,1)S(1)} %bitcast.8), custom_call_target="tpu_custom_call" | custom-call | flops 1048576 | bytes 3145728 | tf_op jit(solution)/shard_map/pallas_call | solution.py:450
  9.8 0.0 collective-permute-done.1.refs_3_.refs_4_
  9.8 0.8 %collective-permute-done.refs_2_ = bf16[14,32,128]{2,1,0:T(8,128)(2,1)S(1)} collective-permute-done((bf16[14,32,128]{2,1,0:T(8,128)(2,1)S(1)}, bf16[14,32,128]{2,1,0:T(8,128)(2,1)S(1)}, u32[]{:S(2)}, u32[]{:S(2)}) %collective-permute-start) | collective-permute-done | bytes 114720 | tf_op jit(solution)/shard_map/ppermute | solution.py:396
  10.6 0.0 copy-done.2
  10.6 0.6 %shard_map.66 = (bf16[7,32,128]{2,1,0:T(8,128)(2,1)S(1)}, bf16[7,32,128]{2,1,0:T(8,128)(2,1)S(1)}) custom-call(s32[2,3]{1,0:T(2,128)S(1)} %bitcast.10, bf16[3,16,32,128]{3,2,1,0:T(8,128)(2,1)S(1)} %get-tuple-element.17.refs_1_, bf16[14,32,128]{2,1,0:T(8,128)(2,1)S(1)} %collective-permute-done.refs_2_, ...), custom_call_target="tpu_custom_call" | custom-call | flops 1048576 | bytes 2097152 | tf_op jit(solution)/shard_map/pallas_call | solution.py:458
  11.2 2.2 %collective-permute-start.2 = (bf16[7,32,128]{2,1,0:T(8,128)(2,1)S(1)}, bf16[7,32,128]{2,1,0:T(8,128)(2,1)S(1)}, u32[]{:S(2)}, u32[]{:S(2)}) collective-permute-start(bf16[7,32,128]{2,1,0:T(8,128)(2,1)S(1)} %get-tuple-element.21), channel_id=1, source_target_pairs={{0,8},{1,2},{2,1},{3,4},{4,3},{5,6},{6,5},{7,15},{8,0},{9,10},{10,... | collective-permute-start | bytes 172040 | tf_op jit(solution)/shard_map/ppermute | solution.py:396
  13.4 1.3 %collective-permute-start.3 = (bf16[7,32,128]{2,1,0:T(8,128)(2,1)S(1)}, bf16[7,32,128]{2,1,0:T(8,128)(2,1)S(1)}, u32[]{:S(2)}, u32[]{:S(2)}) collective-permute-start(bf16[7,32,128]{2,1,0:T(8,128)(2,1)S(1)} %get-tuple-element.22), channel_id=1, source_target_pairs={{0,1},{1,0},{2,3},{3,2},{4,5},{5,4},{6,7},{7,6},{8,9},{9,8},{10,11... | collective-permute-start | bytes 172040 | tf_op jit(solution)/shard_map/ppermute | solution.py:396
  14.7 0.0 collective-permute-done.5.refs_5_
  14.7 0.0 collective-permute-done.6.refs_6_
  14.7 0.0 collective-permute-done.4.refs_3_
  14.7 1.8 %shard_map.67.refs_3_ = f32[8,128,256]{2,1,0:T(8,128)S(1)} custom-call(s32[2,3]{1,0:T(2,128)S(1)} %bitcast.11, bf16[3,16,32,128]{3,2,1,0:T(8,128)(2,1)S(1)} %get-tuple-element.17.refs_1_, bf16[14,32,128]{2,1,0:T(8,128)(2,1)S(1)} %collective-permute-done.refs_2_, bf16[13,32,128]{2,1,0:T(8,128)(2,1)S(1)} %collective-permute-done.4.refs_3_, ...), custom_call_target="tpu_custom_call" | custom-call | flops 1073741824 | bytes 4194304 | tf_op jit(solution)/shard_map/pallas_call | solution.py:467
  16.6 1.6 %collective-permute-done.2.refs_1_ = bf16[7,32,128]{2,1,0:T(8,128)(2,1)S(1)} collective-permute-done((bf16[7,32,128]{2,1,0:T(8,128)(2,1)S(1)}, bf16[7,32,128]{2,1,0:T(8,128)(2,1)S(1)}, u32[]{:S(2)}, u32[]{:S(2)}) %collective-permute-start.2) | collective-permute-done | bytes 57376 | tf_op jit(solution)/shard_map/ppermute | solution.py:396
  18.2 0.9 %collective-permute-done.3.refs_2_ = bf16[7,32,128]{2,1,0:T(8,128)(2,1)S(1)} collective-permute-done((bf16[7,32,128]{2,1,0:T(8,128)(2,1)S(1)}, bf16[7,32,128]{2,1,0:T(8,128)(2,1)S(1)}, u32[]{:S(2)}, u32[]{:S(2)}) %collective-permute-start.3) | collective-permute-done | bytes 57376 | tf_op jit(solution)/shard_map/ppermute | solution.py:396
  19.1 1.9 %shard_map.68 = bf16[2048,128]{1,0:T(8,128)(2,1)} custom-call(s32[2,3]{1,0:T(2,128)S(1)} %bitcast.12, bf16[7,32,128]{2,1,0:T(8,128)(2,1)S(1)} %collective-permute-done.2.refs_1_, bf16[7,32,128]{2,1,0:T(8,128)(2,1)S(1)} %collective-permute-done.3.refs_2_, f32[8,128,256]{2,1,0:T(8,128)S(1)} %shard_map.67.refs_3_, bf16[128,1664]{1,0:T(8,128)(2,1)S(1)} %get-tuple-element.28.refs_4_), custom_call_target="tpu_custom_call" | custom-call | flops 1048576 | bytes 2097152 | tf_op jit(solution)/shard_map/pallas_call | solution.py:474
Async XLA Ops:
  0.0 8.9 %copy-start = (bf16[128,16,128]{2,1,0:T(8,128)(2,1)S(1)}, bf16[128,16,128]{2,1,0:T(8,128)(2,1)}, u32[]{:S(2)}) copy-start(bf16[128,16,128]{2,1,0:T(8,128)(2,1)} %param.6) | copy-start | bytes 1572868
  0.0 8.7 %copy-start.3 = (f32[128]{0:T(128)S(1)}, f32[128]{0:T(128)}, u32[]{:S(2)}) copy-start(f32[128]{0:T(128)} %param.11) | copy-start | bytes 1540
  0.0 8.9 %copy-start.1 = (bf16[3,3,128,224]{2,3,1,0:T(8,128)(2,1)S(1)}, bf16[3,3,128,224]{2,3,1,0:T(8,128)(2,1)}, u32[]{:S(2)}) copy-start(bf16[3,3,128,224]{2,3,1,0:T(8,128)(2,1)} %param.10) | copy-start | bytes 1548292
  0.0 10.6 %copy-start.2 = (s32[3,2]{0,1:T(2,128)S(1)}, s32[3,2]{0,1:T(2,128)}, u32[]{:S(2)}) copy-start(s32[3,2]{0,1:T(2,128)} %param.8) | copy-start | bytes 76
  2.5 8.1 %collective-permute-start = (bf16[14,32,128]{2,1,0:T(8,128)(2,1)S(1)}, bf16[14,32,128]{2,1,0:T(8,128)(2,1)S(1)}, u32[]{:S(2)}, u32[]{:S(2)}) collective-permute-start(bf16[14,32,128]{2,1,0:T(8,128)(2,1)S(1)} %get-tuple-element.18), channel_id=1, source_target_pairs={{0,2},{1,3},{2,0},{3,1},{4,6},{5,7},{6,4},{7,5},{8,16},{9,17},{10,... | collective-permute-start | bytes 344072 | tf_op jit(solution)/shard_map/ppermute | solution.py:396
  8.1 6.6 %collective-permute-start.4 = (bf16[13,32,128]{2,1,0:T(8,128)(2,1)S(1)}, bf16[13,32,128]{2,1,0:T(8,128)(2,1)S(1)}, u32[]{:S(2)}, u32[]{:S(2)}) collective-permute-start(bf16[13,32,128]{2,1,0:T(8,128)(2,1)S(1)} %get-tuple-element.23), channel_id=1, source_target_pairs={{0,2},{1,3},{2,0},{3,1},{4,6},{5,7},{6,4},{7,5},{8,16},{9,17},{10,... | collective-permute-start | bytes 319496 | tf_op jit(solution)/shard_map/ppermute | solution.py:396
  8.2 1.5 %collective-permute-start.1 = (bf16[9,32,128]{2,1,0:T(8,128)(2,1)S(1)}, bf16[9,32,128]{2,1,0:T(8,128)(2,1)S(1)}, u32[]{:S(2)}, u32[]{:S(2)}) collective-permute-start(bf16[9,32,128]{2,1,0:T(8,128)(2,1)S(1)} %get-tuple-element.19), channel_id=1, source_target_pairs={{0,8},{1,9},{2,10},{3,11},{4,12},{5,13},{6,14},{7,15},{8,0},{9,1},... | collective-permute-start | bytes 221192 | tf_op jit(solution)/shard_map/ppermute | solution.py:396
  8.2 6.5 %collective-permute-start.5 = (bf16[9,32,128]{2,1,0:T(8,128)(2,1)S(1)}, bf16[9,32,128]{2,1,0:T(8,128)(2,1)S(1)}, u32[]{:S(2)}, u32[]{:S(2)}) collective-permute-start(bf16[9,32,128]{2,1,0:T(8,128)(2,1)S(1)} %get-tuple-element.24), channel_id=1, source_target_pairs={{0,8},{1,9},{2,10},{3,11},{4,12},{5,13},{6,14},{7,15},{8,0},{9,1},... | collective-permute-start | bytes 221192 | tf_op jit(solution)/shard_map/ppermute | solution.py:396
  8.7 6.0 %collective-permute-start.6 = (bf16[9,32,128]{2,1,0:T(8,128)(2,1)S(1)}, bf16[9,32,128]{2,1,0:T(8,128)(2,1)S(1)}, u32[]{:S(2)}, u32[]{:S(2)}) collective-permute-start(bf16[9,32,128]{2,1,0:T(8,128)(2,1)S(1)} %get-tuple-element.25), channel_id=1, source_target_pairs={{0,8},{1,9},{2,10},{3,11},{4,12},{5,13},{6,14},{7,15},{8,0},{9,1},... | collective-permute-start | bytes 221192 | tf_op jit(solution)/shard_map/ppermute | solution.py:396
  11.2 7.0 %collective-permute-start.2 = (bf16[7,32,128]{2,1,0:T(8,128)(2,1)S(1)}, bf16[7,32,128]{2,1,0:T(8,128)(2,1)S(1)}, u32[]{:S(2)}, u32[]{:S(2)}) collective-permute-start(bf16[7,32,128]{2,1,0:T(8,128)(2,1)S(1)} %get-tuple-element.21), channel_id=1, source_target_pairs={{0,8},{1,2},{2,1},{3,4},{4,3},{5,6},{6,5},{7,15},{8,0},{9,10},{10,... | collective-permute-start | bytes 172040 | tf_op jit(solution)/shard_map/ppermute | solution.py:396
  13.4 5.7 %collective-permute-start.3 = (bf16[7,32,128]{2,1,0:T(8,128)(2,1)S(1)}, bf16[7,32,128]{2,1,0:T(8,128)(2,1)S(1)}, u32[]{:S(2)}, u32[]{:S(2)}) collective-permute-start(bf16[7,32,128]{2,1,0:T(8,128)(2,1)S(1)} %get-tuple-element.22), channel_id=1, source_target_pairs={{0,1},{1,0},{2,3},{3,2},{4,5},{5,4},{6,7},{7,6},{8,9},{9,8},{10,11... | collective-permute-start | bytes 172040 | tf_op jit(solution)/shard_map/ppermute | solution.py:396
